TPU v7x, 32 devices: a whole 2x2x4 slice. The times are simulated.
32 devices in a mesh: tm: 8 (over y, x, core), space: 4 (over z).
Axes of the slice: x: 2, y: 2, z: 4, core: 2. Of those that a mesh axis runs over, the one named last changes fastest.
Arguments:
- evecs: bfloat16 [8, 2, 3, 1024, 128], P('tm', None, None, 'space'), may hold values from -2 to 2
- peramb: bfloat16 [8, 4, 8, 2, 128, 128], P('tm', 'space'), may hold values from -0.0234375 to 0.0234375
- momenta: int32 [4, 3], replicated, may hold values from -2 to 2, as said below
- unit_table: int32 [4, 2], replicated, may hold values from 0 to 3, as said below
- time_labels: int32 [8], replicated, may hold values from 0 to 7, each once
Outputs:
- blocks: bfloat16 [8, 4, 8, 2, 128, 128], P('tm', 'space')
Inputs may be any that keep to these rules, and one draw needn't show every extreme that they name: `momenta`: the first component of every momentum is one of 1, 2, -1, -2, and each of these four occurs; the other components take any value in range. `unit_table`: column 0 is a permutation of 0 to 3; column 1 lies in 0 to 3 and takes each of these values. `time_labels`: A permutation of 0 to 7.
All inputs are finite; a program needn't handle non-finite values.
Results may differ from a plain program's by a relative error of at most 0.0075.
Values may be sent and summed in bfloat16 or wider, within the bound.
No kernel may reach another device: no remote copies, remote signals or barrier semaphores. Data moves between devices by JAX's collectives and lax.ppermute only.
A program may use at most 64 MiB of HBM per device.

v0:
```python
import math

import jax
import jax.numpy as jnp
from jax import lax
from jax.sharding import PartitionSpec as P

LS = 40


def phase_tables(momenta, first_site, site_count):
    sites = first_site + jnp.arange(site_count, dtype=jnp.int32)
    coords = jnp.stack([sites % LS, sites // LS % LS, sites // (LS * LS)], axis=0)
    products = jnp.sum(momenta[:, :, None] * coords[None, :, :], axis=1)
    angles = (products % LS).astype(jnp.float32) * (2.0 * math.pi / LS)
    return (jnp.cos(angles), jnp.sin(angles))


def gram(vectors, cosine, sine):
    real_part = vectors[0]
    imag_part = vectors[1]
    cos_site = cosine[None, :, None]
    sin_site = sine[None, :, None]
    phased_real = (cos_site * real_part + sin_site * imag_part).astype(jnp.bfloat16)
    phased_imag = (cos_site * imag_part - sin_site * real_part).astype(jnp.bfloat16)
    columns = vectors.shape[-1]
    left = vectors.reshape(-1, columns)
    right_real = jnp.concatenate([phased_real, phased_imag], axis=0).reshape(-1, columns)
    right_imag = jnp.concatenate([phased_imag, -phased_real], axis=0).reshape(-1, columns)
    gram_real = jnp.dot(left.T, right_real, preferred_element_type=jnp.float32)
    gram_imag = jnp.dot(left.T, right_imag, preferred_element_type=jnp.float32)
    return jnp.stack([gram_real, gram_imag], axis=0)


def chain(sink_block, peramb_rows, sources, time_signs, phase_real, phase_imag):
    prop_real = peramb_rows[:, 0]
    prop_imag = peramb_rows[:, 1]
    mixed_real = jnp.einsum(
        "ij,njk->nik", sink_block[0], prop_real, preferred_element_type=jnp.float32
    ) - jnp.einsum("ij,njk->nik", sink_block[1], prop_imag, preferred_element_type=jnp.float32)
    mixed_imag = jnp.einsum(
        "ij,njk->nik", sink_block[0], prop_imag, preferred_element_type=jnp.float32
    ) + jnp.einsum("ij,njk->nik", sink_block[1], prop_real, preferred_element_type=jnp.float32)
    mixed_real = mixed_real.astype(jnp.bfloat16)
    mixed_imag = mixed_imag.astype(jnp.bfloat16)
    source_real = sources[:, 0]
    source_imag = sources[:, 1]
    block_real = jnp.einsum(
        "nij,nkj->nik", mixed_real, source_real, preferred_element_type=jnp.float32
    ) + jnp.einsum("nij,nkj->nik", mixed_imag, source_imag, preferred_element_type=jnp.float32)
    block_imag = jnp.einsum(
        "nij,nkj->nik", mixed_imag, source_real, preferred_element_type=jnp.float32
    ) - jnp.einsum("nij,nkj->nik", mixed_real, source_imag, preferred_element_type=jnp.float32)
    scaling = time_signs[:, None, None]
    out_real = scaling * (phase_real * block_real - phase_imag * block_imag)
    out_imag = scaling * (phase_real * block_imag + phase_imag * block_real)
    return jnp.stack([out_real, out_imag], axis=1).astype(jnp.bfloat16)


def body(evecs, peramb, momenta, unit_table, time_labels):
    site_count = evecs.shape[3]
    first_site = lax.axis_index("space") * site_count
    cosines, sines = phase_tables(momenta, first_site, site_count)
    vectors = evecs[0]
    unit_index = lax.axis_index("space")
    unit_row = lax.dynamic_index_in_dim(unit_table, unit_index, 0, keepdims=False)
    moment_index = unit_row[0]
    turns = unit_row[1]
    partial_all = lax.map(lambda angles: gram(vectors, angles[0], angles[1]), (cosines, sines))
    summed_all = lax.psum(partial_all, "space")
    own_block = lax.dynamic_index_in_dim(summed_all, moment_index, 0, keepdims=True).astype(
        jnp.bfloat16
    )
    phase_real = ((1 - turns % 2) * (1 - turns)).astype(jnp.float32)
    phase_imag = (turns % 2 * (2 - turns)).astype(jnp.float32)
    sink_slot = lax.axis_index("tm")
    sink_label = lax.dynamic_index_in_dim(time_labels, sink_slot, 0, keepdims=False)
    sink_block = own_block[0]
    peramb_local = peramb[0, 0]
    time_signs = jnp.where(time_labels > sink_label, -1.0, 1.0).astype(jnp.float32)
    result = chain(
        sink_block,
        peramb_local,
        lax.all_gather(own_block, "tm", axis=0, tiled=True),
        time_signs,
        phase_real,
        phase_imag,
    )
    return result[None, None]


def solution(mesh):
    return jax.shard_map(
        body,
        mesh=mesh,
        in_specs=(
            P("tm", None, None, "space", None),
            P("tm", "space", None, None, None, None),
            P(),
            P(),
            P(),
        ),
        out_specs=P("tm", "space", None, None, None, None),
        check_vma=False,
    )
```

profile of v0, /device:TPU:0, one launch (start us, length us, event | category | flops | bytes accessed | tf_op | source)
XLA Modules:
  0.0 63.4 jit_solution(16929732994443053661)
XLA Ops:
  0.0 0.0 copy-start
  0.0 0.7 %copy-done = s32[4,2]{0,1:T(2,128)S(1)} copy-done((s32[4,2]{0,1:T(2,128)S(1)}, s32[4,2]{0,1:T(2,128)}, u32[]{:S(2)}) %copy-start) | copy-done | bytes 56
  0.7 0.1 constant_dynamic-slice_fusion.2
  0.8 0.5 fusion.22
  3.3 0.0 copy-start.3
  3.3 0.7 %copy-done.3 = s32[4,3]{1,0:T(4,128)S(1)} copy-done((s32[4,3]{1,0:T(4,128)S(1)}, s32[4,3]{1,0:T(4,128)}, u32[]{:S(2)}) %copy-start.3) | copy-done | bytes 72
  4.0 0.1 copy.14
  4.0 0.1 multiply_reduce_fusion
  4.1 0.1 fusion.18
  4.2 9.2 %while.10 = (s32[]{:T(128)}, f32[4,2,128,128]{3,2,1,0:T(8,128)S(1)}, f32[4,256]{1,0:T(4,128)S(1)}, bf16[2,3,256,128]{3,2,1,0:T(8,128)(2,1)}, f32[4,256]{1,0:T(4,...) while((s32[]{:T(128)}, f32[4,2,128,128]{3,2,1,0:T(8,128)S(1)}, f32[4,256]{1,0:T(4,128)S(1)}, ...), condition=%wide.region_2.3_spmd, body=%wide.region_1.2_spmd.sunk | while | flops 102367232 | bytes 6824049 | solution.py:69
  4.2 0.0 copy-start.1
  4.2 1.2 %fusion.42 = (bf16[3,256,128]{2,1,0:T(8,128)(2,1)S(1)}, bf16[3,256,128]{2,1,0:T(8,128)(2,1)S(1)}) fusion(bf16[2,3,256,128]{3,2,1,0:T(8,128)(2,1)} %bitcast.111, f32[256]{0:T(256)S(1)} %bitcast.122, f32[256]{0:T(256)S(1)} %bitcast.124), kind=kLoop, calls=%fused_computation.57.clone.1 | loop fusion | flops 688128 | bytes 788480 | tf_op jit(solution)/shard_map/while/body/eval_jaxpr/neg | solution.py:29
  5.5 0.0 copy-done.1
  5.5 0.1 fusion.41
  5.7 0.1 pad_maximum_fusion.4
  5.7 0.3 convolution_bitcast_fusion.4
  6.0 0.3 convolution_bitcast_fusion.5
  6.4 0.1 copy.27
  6.5 0.0 copy-start.1
  6.5 1.2 %fusion.42 = (bf16[3,256,128]{2,1,0:T(8,128)(2,1)S(1)}, bf16[3,256,128]{2,1,0:T(8,128)(2,1)S(1)}) fusion(bf16[2,3,256,128]{3,2,1,0:T(8,128)(2,1)} %bitcast.111, f32[256]{0:T(256)S(1)} %bitcast.122, f32[256]{0:T(256)S(1)} %bitcast.124), kind=kLoop, calls=%fused_computation.57.clone.1 | loop fusion | flops 688128 | bytes 788480 | tf_op jit(solution)/shard_map/while/body/eval_jaxpr/neg | solution.py:29
  7.8 0.0 copy-done.1
  7.8 0.1 fusion.41
  8.0 0.1 pad_maximum_fusion.4
  8.0 0.3 convolution_bitcast_fusion.4
  8.3 0.3 convolution_bitcast_fusion.5
  8.7 0.1 copy.27
  8.8 0.0 copy-start.1
  8.8 1.2 %fusion.42 = (bf16[3,256,128]{2,1,0:T(8,128)(2,1)S(1)}, bf16[3,256,128]{2,1,0:T(8,128)(2,1)S(1)}) fusion(bf16[2,3,256,128]{3,2,1,0:T(8,128)(2,1)} %bitcast.111, f32[256]{0:T(256)S(1)} %bitcast.122, f32[256]{0:T(256)S(1)} %bitcast.124), kind=kLoop, calls=%fused_computation.57.clone.1 | loop fusion | flops 688128 | bytes 788480 | tf_op jit(solution)/shard_map/while/body/eval_jaxpr/neg | solution.py:29
  10.1 0.0 copy-done.1
  10.1 0.1 fusion.41
  10.3 0.1 pad_maximum_fusion.4
  10.3 0.3 convolution_bitcast_fusion.4
  10.6 0.3 convolution_bitcast_fusion.5
  11.0 0.1 copy.27
  11.1 0.0 copy-start.1
  11.1 1.2 %fusion.42 = (bf16[3,256,128]{2,1,0:T(8,128)(2,1)S(1)}, bf16[3,256,128]{2,1,0:T(8,128)(2,1)S(1)}) fusion(bf16[2,3,256,128]{3,2,1,0:T(8,128)(2,1)} %bitcast.111, f32[256]{0:T(256)S(1)} %bitcast.122, f32[256]{0:T(256)S(1)} %bitcast.124), kind=kLoop, calls=%fused_computation.57.clone.1 | loop fusion | flops 688128 | bytes 788480 | tf_op jit(solution)/shard_map/while/body/eval_jaxpr/neg | solution.py:29
  12.4 0.0 copy-done.1
  12.4 0.1 fusion.41
  12.6 0.1 pad_maximum_fusion.4
  12.6 0.3 convolution_bitcast_fusion.4
  12.9 0.3 convolution_bitcast_fusion.5
  13.3 0.1 copy.27
  13.4 0.0 copy-start.2
  13.4 32.2 %all-reduce.1 = bf16[4,2,128,128]{3,2,1,0:T(8,128)(2,1)S(1)} all-reduce(f32[4,2,128,128]{3,2,1,0:T(8,128)S(1)} %get-tuple-element.37), channel_id=1, replica_groups=mesh['tm'=8,'space'=4] {'space'}, use_global_device_ids=true, to_apply=%region_3.4 | all-reduce | flops 131072 | bytes 786432 | tf_op jit(solution)/shard_map/psum | solution.py:70
  45.7 0.0 copy-done.2
  45.8 0.2 fusion.10
  46.0 0.2 fusion.7
  46.2 9.9 %all_gather.3 = bf16[8,2,128,128]{3,2,1,0:T(8,128)(2,1)S(1)} all-gather(bf16[1,2,128,128]{3,2,1,0:T(8,128)(2,1)S(1)} %dynamic-slice_convert_fusion), channel_id=1, replica_groups=mesh['tm'=8,'space'=4] {'tm'}, dimensions={0}, use_global_device_ids=true | all-gather | bytes 589824 | tf_op jit(solution)/shard_map/all_gather | solution.py:84
  56.1 0.3 fusion.13
  56.4 0.2 fusion.11
  56.6 0.2 fusion.6
  56.8 0.3 fusion.12
  57.1 0.3 convolution_subtract_fusion.1
  60.2 0.0 copy-start.4
  60.2 0.6 %copy-done.4 = s32[8]{0:T(128)S(1)} copy-done((s32[8]{0:T(128)S(1)}, s32[8]{0:T(128)}, u32[]{:S(2)}) %copy-start.4) | copy-done | bytes 56
  60.9 0.6 dynamic_slice.19
  61.5 0.6 %compare_select_fusion = f32[8]{0:T(128)S(1)} fusion(s32[8]{0:T(128)S(1)} %copy-done.4, s32[]{:T(128)} %bitcast.14), kind=kLoop, calls=%fused_computation.50 | loop fusion | flops 16 | bytes 68 | tf_op jit(solution)/shard_map/jit(_where)/select_n | solution.py:80
  62.1 0.4 fusion.8
  62.5 0.1 pad_maximum_fusion.2
  62.6 0.8 %copy.19 = bf16[1,1,8,2,128,128]{5,4,3,2,1,0:T(8,128)(2,1)} copy(bf16[1,1,8,2,128,128]{5,4,2,3,1,0:T(8,128)(2,1)S(1)} %pad_maximum_fusion.2) | data formatting | bytes 1048576 | tf_op jit(solution)/shard_map/stack | solution.py:57
  (18 shorter events, 0.3 us)
Async XLA Ops:
  0.0 0.7 %copy-start = (s32[4,2]{0,1:T(2,128)S(1)}, s32[4,2]{0,1:T(2,128)}, u32[]{:S(2)}) copy-start(s32[4,2]{0,1:T(2,128)} %param.10) | copy-start | bytes 100
  3.3 0.7 %copy-start.3 = (s32[4,3]{1,0:T(4,128)S(1)}, s32[4,3]{1,0:T(4,128)}, u32[]{:S(2)}) copy-start(s32[4,3]{1,0:T(4,128)} %param.9) | copy-start | bytes 148
  4.2 1.3 %copy-start.1 = (bf16[1,2,3,256,128]{4,3,2,1,0:T(8,128)(2,1)S(1)}, bf16[1,2,3,256,128]{4,3,2,1,0:T(8,128)(2,1)}, u32[]{:S(2)}) copy-start(bf16[1,2,3,256,128]{4,3,2,1,0:T(8,128)(2,1)} %get-tuple-element.132) | copy-start | bytes 1179652 | tf_op jit(solution)/shard_map/while
  6.5 1.3 %copy-start.1 = (bf16[1,2,3,256,128]{4,3,2,1,0:T(8,128)(2,1)S(1)}, bf16[1,2,3,256,128]{4,3,2,1,0:T(8,128)(2,1)}, u32[]{:S(2)}) copy-start(bf16[1,2,3,256,128]{4,3,2,1,0:T(8,128)(2,1)} %get-tuple-element.132) | copy-start | bytes 1179652 | tf_op jit(solution)/shard_map/while
  8.8 1.3 %copy-start.1 = (bf16[1,2,3,256,128]{4,3,2,1,0:T(8,128)(2,1)S(1)}, bf16[1,2,3,256,128]{4,3,2,1,0:T(8,128)(2,1)}, u32[]{:S(2)}) copy-start(bf16[1,2,3,256,128]{4,3,2,1,0:T(8,128)(2,1)} %get-tuple-element.132) | copy-start | bytes 1179652 | tf_op jit(solution)/shard_map/while
  11.1 1.3 %copy-start.1 = (bf16[1,2,3,256,128]{4,3,2,1,0:T(8,128)(2,1)S(1)}, bf16[1,2,3,256,128]{4,3,2,1,0:T(8,128)(2,1)}, u32[]{:S(2)}) copy-start(bf16[1,2,3,256,128]{4,3,2,1,0:T(8,128)(2,1)} %get-tuple-element.132) | copy-start | bytes 1179652 | tf_op jit(solution)/shard_map/while
  13.4 32.3 %copy-start.2 = (bf16[1,1,8,2,128,128]{5,4,3,2,1,0:T(8,128)(2,1)S(1)}, bf16[1,1,8,2,128,128]{5,4,3,2,1,0:T(8,128)(2,1)}, u32[]{:S(2)}) copy-start(bf16[1,1,8,2,128,128]{5,4,3,2,1,0:T(8,128)(2,1)} %param.8) | copy-start | bytes 1572868
  60.2 0.7 %copy-start.4 = (s32[8]{0:T(128)S(1)}, s32[8]{0:T(128)}, u32[]{:S(2)}) copy-start(s32[8]{0:T(128)} %param.11) | copy-start | bytes 100
where the time goes:
time: 63.8 us; the launch traced here: 63.4 us
  blocking collectives  42.1 us (66%)
  other arithmetic  6.71 us (11%)
  between operations  4.93 us (8%)
  local copies, waits for them, and re-layouts  4.64 us (7%)
  matrix products  4.64 us (7%)
    psum x1, blocking collectives, body(): summed_all = lax.psum(partial_all, 'space')  32.2 us
    all_gather x1, blocking collectives, body(): lax.all_gather(own_block, 'tm', axis=0, tiled=True)  9.86 us
    neg x4, other arithmetic, gram(): -phased_real  4.95 us
    unnamed x10, local copies, waits for them, and re-layouts  2.13 us

commit v1 on v0

v1 whole, which is shorter than its diff:
```python
import functools
import math

import jax
import jax.numpy as jnp
import numpy as np
from jax import lax
from jax.experimental import pallas as pl
from jax.experimental.pallas import tpu as pltpu
from jax.sharding import PartitionSpec as P

LS = 40
LIMIT = 12 * 1024 * 1024
VMEM = pl.BlockSpec(memory_space=pltpu.VMEM)
HBM = pl.BlockSpec(memory_space=pltpu.HBM)


def floor_parts(values, base):
    quotient = jnp.floor((values + 0.5) * (1.0 / base))
    return quotient, values - base * quotient


def gram_kernel(count, evecs, momenta, table, trig, *rest):
    outs = rest[:count]
    vecs, left, moments, units, sems = rest[count:]
    load = pltpu.make_async_copy(evecs, vecs, sems.at[0])
    load_moments = pltpu.make_async_copy(momenta, moments, sems.at[1])
    load_units = pltpu.make_async_copy(table, units, sems.at[2])
    load.start()
    load_moments.start()
    load_units.start()
    me = lax.axis_index("space")
    colours, sites, columns = vecs.shape[1:]
    first = (me * sites).astype(jnp.float32)
    site = lax.broadcasted_iota(jnp.int32, (sites, columns), 0).astype(jnp.float32) + first
    row, x = floor_parts(site, float(LS))
    z, y = floor_parts(row, float(LS))
    load_moments.wait()
    load_units.wait()
    load.wait()
    for part in range(2):
        for colour in range(colours):
            left[pl.ds(part * columns, columns), pl.ds(colour * sites, sites)] = vecs[part, colour].T
    cos_table = jnp.broadcast_to(trig[0:1, :], (sites, columns))
    sin_table = jnp.broadcast_to(trig[1:2, :], (sites, columns))
    for k in range(count):
        moment = units[0, me ^ k]
        px = moments[moment, 0].astype(jnp.float32)
        py = moments[moment, 1].astype(jnp.float32)
        pz = moments[moment, 2].astype(jnp.float32)
        _, turns = floor_parts(px * x + py * y + pz * z, float(LS))
        index = turns.astype(jnp.int32)
        cosine = jnp.take_along_axis(cos_table, index, axis=1)
        sine = jnp.take_along_axis(sin_table, index, axis=1)
        total = None
        for colour in range(colours):
            real = vecs[0, colour].astype(jnp.float32)
            imag = vecs[1, colour].astype(jnp.float32)
            phased = jnp.concatenate(
                [
                    (cosine * real + sine * imag).astype(jnp.bfloat16),
                    (cosine * imag - sine * real).astype(jnp.bfloat16),
                ],
                axis=1,
            )
            term = jnp.dot(
                left[:, pl.ds(colour * sites, sites)], phased, preferred_element_type=jnp.float32
            )
            total = term if total is None else total + term
        outs[k][0] = (total[:columns, :columns] + total[columns:, columns:]).astype(outs[k].dtype)
        outs[k][1] = (total[:columns, columns:] - total[columns:, :columns]).astype(outs[k].dtype)


def partial_elementals(vectors, momenta, table, count):
    _, colours, sites, columns = vectors.shape
    angles = np.arange(128, dtype=np.float32) * np.float32(2.0 * math.pi / LS)
    trig = jnp.asarray(np.stack([np.cos(angles), np.sin(angles)] * 4).astype(np.float32))
    shape = (2, columns, columns)
    return pl.pallas_call(
        functools.partial(gram_kernel, count),
        out_shape=[
            jax.ShapeDtypeStruct(shape, jnp.float32 if k == 0 else jnp.bfloat16)
            for k in range(count)
        ],
        in_specs=[HBM, HBM, HBM, VMEM],
        out_specs=[VMEM] * count,
        scratch_shapes=[
            pltpu.VMEM(vectors.shape, vectors.dtype),
            pltpu.VMEM((2 * columns, colours * sites), vectors.dtype),
            pltpu.SMEM(momenta.shape, jnp.int32),
            pltpu.SMEM(table.shape, jnp.int32),
            pltpu.SemaphoreType.DMA((3,)),
        ],
        compiler_params=pltpu.CompilerParams(vmem_limit_bytes=LIMIT),
        cost_estimate=pl.CostEstimate(
            flops=count * 16 * colours * sites * columns * columns,
            bytes_accessed=4 * colours * sites * columns + count * 4 * columns * columns,
            transcendentals=0,
        ),
        name="gram",
    )(vectors, momenta, table, trig)


def mix_kernel(sink, peramb, table, labels, out, units, times, sems):
    load_units = pltpu.make_async_copy(table, units, sems.at[0])
    load_times = pltpu.make_async_copy(labels, times, sems.at[1])
    load_units.start()
    load_times.start()
    real = sink[0]
    imag = sink[1]
    columns = real.shape[0]
    left = jnp.concatenate(
        [jnp.concatenate([real, -imag], axis=1), jnp.concatenate([imag, real], axis=1)], axis=0
    )
    load_units.wait()
    load_times.wait()
    turns = units[1, lax.axis_index("space")]
    odd = lax.rem(turns, 2)
    phase_real = ((1 - odd) * (1 - turns)).astype(jnp.float32)
    phase_imag = (odd * (2 - turns)).astype(jnp.float32)
    own = times[lax.axis_index("tm")]
    for n in range(peramb.shape[0]):
        sign = jnp.where(times[n] > own, -1.0, 1.0).astype(jnp.float32)
        right = jnp.concatenate([peramb[n, 0], peramb[n, 1]], axis=0)
        mixed = jnp.dot(left, right, preferred_element_type=jnp.float32)
        mixed_real = mixed[:columns]
        mixed_imag = mixed[columns:]
        turn_real = sign * phase_real
        turn_imag = sign * phase_imag
        out[n, :, pl.ds(0, columns)] = (turn_real * mixed_real - turn_imag * mixed_imag).astype(
            out.dtype
        )
        out[n, :, pl.ds(columns, columns)] = (
            turn_real * mixed_imag + turn_imag * mixed_real
        ).astype(out.dtype)


def mix(sink, peramb, table, labels):
    slots, _, columns, _ = peramb.shape
    return pl.pallas_call(
        mix_kernel,
        out_shape=jax.ShapeDtypeStruct((slots, columns, 2 * columns), jnp.bfloat16),
        in_specs=[VMEM, VMEM, HBM, HBM],
        out_specs=VMEM,
        scratch_shapes=[
            pltpu.SMEM(table.shape, jnp.int32),
            pltpu.SMEM(labels.shape, jnp.int32),
            pltpu.SemaphoreType.DMA((2,)),
        ],
        compiler_params=pltpu.CompilerParams(vmem_limit_bytes=LIMIT),
        cost_estimate=pl.CostEstimate(
            flops=slots * 8 * columns**3, bytes_accessed=slots * 8 * columns**2, transcendentals=0
        ),
        name="mix",
    )(sink, peramb, table, labels)


def close_kernel(mixed, sources, out):
    columns = sources.shape[-1]
    for n in range(mixed.shape[0]):
        real = sources[n, 0]
        imag = sources[n, 1]
        right = jnp.concatenate(
            [jnp.concatenate([real, imag], axis=1), jnp.concatenate([-imag, real], axis=1)], axis=0
        )
        block = lax.dot_general(
            mixed[n], right, (((1,), (1,)), ((), ())), preferred_element_type=jnp.float32
        )
        out[n, 0] = block[:, :columns].astype(out.dtype)
        out[n, 1] = block[:, columns:].astype(out.dtype)


def close(mixed, sources):
    slots, columns, _ = mixed.shape
    return pl.pallas_call(
        close_kernel,
        out_shape=jax.ShapeDtypeStruct((slots, 2, columns, columns), jnp.bfloat16),
        in_specs=[VMEM, VMEM],
        out_specs=VMEM,
        compiler_params=pltpu.CompilerParams(vmem_limit_bytes=LIMIT),
        cost_estimate=pl.CostEstimate(
            flops=slots * 8 * columns**3, bytes_accessed=slots * 12 * columns**2, transcendentals=0
        ),
        name="close",
    )(mixed, sources)


def swap(value, axis, size, distance):
    return lax.ppermute(value, axis, [(a, a ^ distance) for a in range(size)])


def body(space, evecs, peramb, momenta, unit_table, time_labels):
    table = unit_table.T
    partials = partial_elementals(evecs[0], momenta, table, space)
    total = partials[0]
    arrived = [swap(partials[k], "space", space, k) for k in range(space - 1, 0, -1)]
    for value in arrived:
        total = total + value.astype(jnp.float32)
    sink = total.astype(jnp.bfloat16)
    sources = lax.all_gather(sink[None], "tm", axis=0, tiled=True)
    mixed = mix(sink, peramb[0, 0], table, time_labels)
    return close(mixed, sources)[None, None]


def solution(mesh):
    return jax.shard_map(
        functools.partial(body, mesh.shape["space"]),
        mesh=mesh,
        in_specs=(
            P("tm", None, None, "space", None),
            P("tm", "space", None, None, None, None),
            P(),
            P(),
            P(),
        ),
        out_specs=P("tm", "space", None, None, None, None),
        check_vma=False,
    )
```

time: 63.8 us -> 28.2 us (0.44)
  blocking collectives: 42.1 us -> 9.86 us
  other arithmetic: 6.71 us -> 0.04 us
  starting transfers between devices: 0 us -> 5.78 us
  waiting for transfers between devices: 0 us -> 4.96 us
  between operations: 4.93 us -> 0.04 us
  matrix products: 4.64 us -> 0 us
  Pallas kernels: 0 us -> 4.25 us
  local copies, waits for them, and re-layouts: 4.64 us -> 3.03 us
    psum x1 -> x0, blocking collectives: 32.2 us -> none  [body(): summed_all = lax.psum(partial_all, 'space')]
    ppermute x0 -> x3, starting transfers between devices: none -> 5.78 us  [swap(): return lax.ppermute(value, axis, [(a, a ^ distance) for a in range(size)])]
    ppermute x0 -> x3, waiting for transfers between devices: none -> 4.96 us  [swap(): return lax.ppermute(value, axis, [(a, a ^ distance) for a in range(size)])]
    neg x4 -> x0, other arithmetic: 4.95 us -> none  [gram(): -phased_real]
    dot_general x16 -> x0, matrix products: 4.64 us -> none  [the longest x4 1.26 us: gram(): gram_real = jnp.dot(left.T, right_real, preferred_element_type=jnp.float32)]
    pallas_call x0 -> x3, Pallas kernels: none -> 4.25 us  [the longest x1 1.96 us: partial_elementals(): pl.pallas_call(functools.partial(gram_kernel, count), out_shape=[jax.Shap...]
    unnamed x10 -> x12, local copies, waits for them, and re-layouts: 2.13 us -> 3.03 us
    another operation x1 -> x0, local copies, waits for them, and re-layouts: 0.83 us -> none  [chain(): return jnp.stack([out_real, out_imag], axis=1).astype(jnp.bfloat16)]
  transfers between devices with their start and end apart: 0 -> 3, of which waited for: 0 -> 2; matrix products, arithmetic and copies ran while one was open for 0% -> 0% of each run, Pallas kernels for 0% -> 0%
where the time goes in v1:
time: 28.2 us; the launch traced here: 28 us
  blocking collectives  9.86 us (35%)
  starting transfers between devices  5.78 us (20%)
  waiting for transfers between devices  4.96 us (18%)
  Pallas kernels  4.25 us (15%)
  local copies, waits for them, and re-layouts  3.03 us (11%)
    all_gather x1, blocking collectives, body(): sources = lax.all_gather(sink[None], 'tm', axis=0, tiled=True)  9.86 us
    ppermute x3, starting transfers between devices, swap(): return lax.ppermute(value, axis, [(a, a ^ distance) for a in range(size)])  5.78 us
    ppermute x3, waiting for transfers between devices, swap(): return lax.ppermute(value, axis, [(a, a ^ distance) for a in range(size)])  4.96 us
    unnamed x12, local copies, waits for them, and re-layouts  3.03 us
    pallas_call x1, Pallas kernels, partial_elementals(): pl.pallas_call(functools.partial(gram_kernel, count), out_shape=[jax.Shap...  1.96 us
    pallas_call x1, Pallas kernels, close(): pl.pallas_call(close_kernel, out_shape=jax.ShapeDtypeStruct((slots, 2, co...  1.28 us
    pallas_call x1, Pallas kernels, mix(): pl.pallas_call(mix_kernel, out_shape=jax.ShapeDtypeStruct((slots, columns...  1.01 us
  transfers between devices with their start and end apart: 3, of which 2 were waited for; matrix products, arithmetic and copies ran while one was open for 0% of the time, Pallas kernels for 0%

profile of v1, /device:TPU:0, one launch (start us, length us, event | category | flops | bytes accessed | tf_op | source)
XLA Modules:
  0.0 28.0 jit_solution(9074449686388828013)
XLA Ops:
  0.0 0.0 copy-start.4
  0.0 0.0 copy-start.1
  0.0 0.7 %copy-done.4 = s32[4,3]{1,0:T(4,128)S(1)} copy-done((s32[4,3]{1,0:T(4,128)S(1)}, s32[4,3]{1,0:T(4,128)}, u32[]{:S(2)}) %copy-start.4) | copy-done | bytes 72
  0.7 0.0 copy-done.1
  0.7 0.0 copy-start.3
  0.7 1.0 %copy-done.3 = bf16[1,2,3,256,128]{4,3,2,1,0:T(8,128)(2,1)S(1)} copy-done((bf16[1,2,3,256,128]{4,3,2,1,0:T(8,128)(2,1)S(1)}, bf16[1,2,3,256,128]{4,3,2,1,0:T(8,128)(2,1)}, u32[]{:S(2)}) %copy-start.3) | copy-done | bytes 393240
  1.7 0.0 copy-start.5
  1.7 0.7 %copy-done.5 = f32[8,128]{1,0:T(8,128)S(1)} copy-done((f32[8,128]{1,0:T(8,128)S(1)}, f32[8,128]{1,0:T(8,128)}, u32[]{:S(2)}) %copy-start.5) | copy-done | bytes 4120
  2.4 2.0 %gram.1 = (f32[2,128,128]{2,1,0:T(8,128)S(1)}, bf16[2,128,128]{2,1,0:T(8,128)(2,1)S(1)}, bf16[2,128,128]{2,1,0:T(8,128)(2,1)S(1)}, bf16[2,128,128]{2,1,0:T(8,128)(2,1)S(1)}) custom-call(bf16[2,3,256,128]{3,2,1,0:T(8,128)(2,1)S(1)} %bitcast.9, s32[4,3]{1,0:T(4,128)S(1)} %copy-done.4, s32[2,4]{1,0:T(2,128)S(1)} %bitcast.7, f32[8,128]{1,0:T(8,128)S(1)} %copy-done.5), custom_call_target="tpu_custom_call" | custom-call | flops 805306368 | bytes 655360 | tf_op jit(solution)/shard_map/gram/pallas_call | solution.py:79
  4.4 0.0 copy-start
  4.4 5.1 %collective-permute-start = (bf16[2,128,128]{2,1,0:T(8,128)(2,1)S(1)}, bf16[2,128,128]{2,1,0:T(8,128)(2,1)S(1)}, u32[]{:S(2)}, u32[]{:S(2)}) collective-permute-start(bf16[2,128,128]{2,1,0:T(8,128)(2,1)S(1)} %get-tuple-element.10), channel_id=1, source_target_pairs={{0,3},{1,2},{2,1},{3,0},{4,7},{5,6},{6,5},{7,4},{8,11},{9,10},{10,... | collective-permute-start | bytes 196616 | tf_op jit(solution)/shard_map/ppermute | solution.py:189
  9.5 0.0 collective-permute-start.1
  9.5 0.6 %collective-permute-start.2 = (bf16[2,128,128]{2,1,0:T(8,128)(2,1)S(1)}, bf16[2,128,128]{2,1,0:T(8,128)(2,1)S(1)}, u32[]{:S(2)}, u32[]{:S(2)}) collective-permute-start(bf16[2,128,128]{2,1,0:T(8,128)(2,1)S(1)} %get-tuple-element.12), channel_id=1, source_target_pairs={{0,1},{1,0},{2,3},{3,2},{4,5},{5,4},{6,7},{7,6},{8,9},{9,8},{10,11... | collective-permute-start | bytes 196616 | tf_op jit(solution)/shard_map/ppermute | solution.py:189
  10.1 1.8 %collective-permute-done = bf16[2,128,128]{2,1,0:T(8,128)(2,1)S(1)} collective-permute-done((bf16[2,128,128]{2,1,0:T(8,128)(2,1)S(1)}, bf16[2,128,128]{2,1,0:T(8,128)(2,1)S(1)}, u32[]{:S(2)}, u32[]{:S(2)}) %collective-permute-start) | collective-permute-done | bytes 65568 | tf_op jit(solution)/shard_map/ppermute | solution.py:189
  12.0 3.1 %collective-permute-done.1 = bf16[2,128,128]{2,1,0:T(8,128)(2,1)S(1)} collective-permute-done((bf16[2,128,128]{2,1,0:T(8,128)(2,1)S(1)}, bf16[2,128,128]{2,1,0:T(8,128)(2,1)S(1)}, u32[]{:S(2)}, u32[]{:S(2)}) %collective-permute-start.1) | collective-permute-done | bytes 65568 | tf_op jit(solution)/shard_map/ppermute | solution.py:189
  15.1 0.0 collective-permute-done.2
  15.2 9.9 %all-gather = bf16[16,128,128]{2,1,0:T(8,128)(2,1)S(1)} all-gather(bf16[2,128,128]{2,1,0:T(8,128)(2,1)S(1)} %add_convert_fusion.sink), channel_id=2, replica_groups=mesh['tm'=8,'space'=4] {'tm'}, dimensions={0}, use_global_device_ids=true | all-gather | bytes 589824 | tf_op jit(solution)/shard_map/all_gather | solution.py:200
  25.0 0.0 copy-start.2
  25.0 0.0 copy-done
  25.0 0.7 %copy-done.2 = s32[8]{0:T(128)S(1)} copy-done((s32[8]{0:T(128)S(1)}, s32[8]{0:T(128)}, u32[]{:S(2)}) %copy-start.2) | copy-done | bytes 56
  25.7 1.0 %mix.1.mixed = bf16[8,128,256]{2,1,0:T(8,128)(2,1)S(1)} custom-call(bf16[2,128,128]{2,1,0:T(8,128)(2,1)S(1)} %add_convert_fusion.sink, bf16[8,2,128,128]{3,2,1,0:T(8,128)(2,1)S(1)} %bitcast.6, s32[2,4]{1,0:T(2,128)S(1)} %bitcast.8, s32[8]{0:T(128)S(1)} %copy-done.2), custom_call_target="tpu_custom_call" | custom-call | flops 134217728 | bytes 1048576 | tf_op jit(solution)/shard_map/mix/pallas_call | solution.py:140
  26.7 1.3 %close.1 = bf16[8,2,128,128]{3,2,1,0:T(8,128)(2,1)} custom-call(bf16[8,128,256]{2,1,0:T(8,128)(2,1)S(1)} %mix.1.mixed, bf16[8,2,128,128]{3,2,1,0:T(8,128)(2,1)S(1)} %bitcast.5), custom_call_target="tpu_custom_call" | custom-call | flops 134217728 | bytes 1572864 | tf_op jit(solution)/shard_map/close/pallas_call | solution.py:175
  (1 shorter events, 0.0 us)
Async XLA Ops:
  0.0 0.7 %copy-start.4 = (s32[4,3]{1,0:T(4,128)S(1)}, s32[4,3]{1,0:T(4,128)}, u32[]{:S(2)}) copy-start(s32[4,3]{1,0:T(4,128)} %momenta.1) | copy-start | bytes 148
  0.0 0.7 %copy-start.1 = (s32[4,2]{0,1:T(2,128)S(1)}, s32[4,2]{0,1:T(2,128)}, u32[]{:S(2)}) copy-start(s32[4,2]{0,1:T(2,128)} %param.9) | copy-start | bytes 100
  0.7 1.0 %copy-start.3 = (bf16[1,2,3,256,128]{4,3,2,1,0:T(8,128)(2,1)S(1)}, bf16[1,2,3,256,128]{4,3,2,1,0:T(8,128)(2,1)}, u32[]{:S(2)}) copy-start(bf16[1,2,3,256,128]{4,3,2,1,0:T(8,128)(2,1)} %param.6) | copy-start | bytes 1179652
  1.7 0.7 %copy-start.5 = (f32[8,128]{1,0:T(8,128)S(1)}, f32[8,128]{1,0:T(8,128)}, u32[]{:S(2)}) copy-start(f32[8,128]{1,0:T(8,128)} %constant.2.clone.trig) | copy-start | bytes 12292
  4.4 20.7 %copy-start = (bf16[1,1,8,2,128,128]{5,4,3,2,1,0:T(8,128)(2,1)S(1)}, bf16[1,1,8,2,128,128]{5,4,3,2,1,0:T(8,128)(2,1)}, u32[]{:S(2)}) copy-start(bf16[1,1,8,2,128,128]{5,4,3,2,1,0:T(8,128)(2,1)} %param.7) | copy-start | bytes 1572868
  4.4 7.6 %collective-permute-start = (bf16[2,128,128]{2,1,0:T(8,128)(2,1)S(1)}, bf16[2,128,128]{2,1,0:T(8,128)(2,1)S(1)}, u32[]{:S(2)}, u32[]{:S(2)}) collective-permute-start(bf16[2,128,128]{2,1,0:T(8,128)(2,1)S(1)} %get-tuple-element.10), channel_id=1, source_target_pairs={{0,3},{1,2},{2,1},{3,0},{4,7},{5,6},{6,5},{7,4},{8,11},{9,10},{10,... | collective-permute-start | bytes 196616 | tf_op jit(solution)/shard_map/ppermute | solution.py:189
  9.5 5.6 %collective-permute-start.1 = (bf16[2,128,128]{2,1,0:T(8,128)(2,1)S(1)}, bf16[2,128,128]{2,1,0:T(8,128)(2,1)S(1)}, u32[]{:S(2)}, u32[]{:S(2)}) collective-permute-start(bf16[2,128,128]{2,1,0:T(8,128)(2,1)S(1)} %get-tuple-element.11), channel_id=1, source_target_pairs={{0,2},{1,3},{2,0},{3,1},{4,6},{5,7},{6,4},{7,5},{8,10},{9,11},{10,... | collective-permute-start | bytes 196616 | tf_op jit(solution)/shard_map/ppermute | solution.py:189
  9.5 5.6 %collective-permute-start.2 = (bf16[2,128,128]{2,1,0:T(8,128)(2,1)S(1)}, bf16[2,128,128]{2,1,0:T(8,128)(2,1)S(1)}, u32[]{:S(2)}, u32[]{:S(2)}) collective-permute-start(bf16[2,128,128]{2,1,0:T(8,128)(2,1)S(1)} %get-tuple-element.12), channel_id=1, source_target_pairs={{0,1},{1,0},{2,3},{3,2},{4,5},{5,4},{6,7},{7,6},{8,9},{9,8},{10,11... | collective-permute-start | bytes 196616 | tf_op jit(solution)/shard_map/ppermute | solution.py:189
  25.0 0.7 %copy-start.2 = (s32[8]{0:T(128)S(1)}, s32[8]{0:T(128)}, u32[]{:S(2)}) copy-start(s32[8]{0:T(128)} %labels.1) | copy-start | bytes 100

commit v2 on v1

v2 whole, which is shorter than its diff:
```python
import functools
import math

import jax
import jax.numpy as jnp
import numpy as np
from jax import lax
from jax.experimental import pallas as pl
from jax.experimental.pallas import tpu as pltpu
from jax.sharding import PartitionSpec as P


LS = 40
LIMIT = 12 * 1024 * 1024
VMEM = pl.BlockSpec(memory_space=pltpu.VMEM)
HBM = pl.BlockSpec(memory_space=pltpu.HBM)


def floor_parts(values, base):
    quotient = jnp.floor((values + 0.5) * (1.0 / base))
    return quotient, values - base * quotient


def in_hbm(value):
    return pltpu.with_memory_space_constraint(value, pltpu.HBM)


def site_parts(sites, columns):
    first = (lax.axis_index("space") * sites).astype(jnp.float32)
    site = lax.broadcasted_iota(jnp.int32, (sites, columns), 0).astype(jnp.float32) + first
    row, x = floor_parts(site, float(LS))
    z, y = floor_parts(row, float(LS))
    return x, y, z


def gram(vecs, left, moments, units, tables, parts, k):
    _, colours, sites, columns = vecs.shape
    x, y, z = parts
    moment = units[0, lax.axis_index("space") ^ k]
    px = moments[moment, 0].astype(jnp.float32)
    py = moments[moment, 1].astype(jnp.float32)
    pz = moments[moment, 2].astype(jnp.float32)
    _, turns = floor_parts(px * x + py * y + pz * z, float(LS))
    index = turns.astype(jnp.int32)
    cosine = jnp.take_along_axis(tables[0], index, axis=1)
    sine = jnp.take_along_axis(tables[1], index, axis=1)
    total = None
    for colour in range(colours):
        real = vecs[0, colour].astype(jnp.float32)
        imag = vecs[1, colour].astype(jnp.float32)
        phased = jnp.concatenate(
            [
                (cosine * real + sine * imag).astype(jnp.bfloat16),
                (cosine * imag - sine * real).astype(jnp.bfloat16),
            ],
            axis=1,
        )
        term = jnp.dot(
            left[:, pl.ds(colour * sites, sites)], phased, preferred_element_type=jnp.float32
        )
        total = term if total is None else total + term
    real = total[:columns, :columns] + total[columns:, columns:]
    imag = total[:columns, columns:] - total[columns:, :columns]
    return real, imag


def spread(trig, sites, columns):
    return [jnp.broadcast_to(trig[i : i + 1, :], (sites, columns)) for i in range(2)]


def gram_first(ks, evecs, momenta, table, trig_in, *rest):
    outs = rest[: len(ks)]
    vecs, left, trig, moments, units, sems = rest[len(ks) :]
    loads = [
        pltpu.make_async_copy(source, target, sems.at[i])
        for i, (source, target) in enumerate(
            ((evecs, vecs), (momenta, moments), (table, units), (trig_in, trig))
        )
    ]
    for load in loads:
        load.start()
    _, colours, sites, columns = vecs.shape
    parts = site_parts(sites, columns)
    for load in loads[::-1]:
        load.wait()
    for part in range(2):
        for colour in range(colours):
            left[pl.ds(part * columns, columns), pl.ds(colour * sites, sites)] = vecs[part, colour].T
    tables = spread(trig, sites, columns)
    for out, k in zip(outs, ks):
        real, imag = gram(vecs, left, moments, units, tables, parts, k)
        out[0] = real.astype(out.dtype)
        out[1] = imag.astype(out.dtype)


def gram_second(ks, vecs, left, trig, momenta, table, *rest):
    outs = rest[: len(ks)]
    moments, units, sems = rest[len(ks) :]
    loads = [
        pltpu.make_async_copy(source, target, sems.at[i])
        for i, (source, target) in enumerate(((momenta, moments), (table, units)))
    ]
    for load in loads:
        load.start()
    _, _, sites, columns = vecs.shape
    parts = site_parts(sites, columns)
    tables = spread(trig, sites, columns)
    for load in loads:
        load.wait()
    for out, k in zip(outs, ks):
        real, imag = gram(vecs, left, moments, units, tables, parts, k)
        out[0] = real.astype(out.dtype)
        out[1] = imag.astype(out.dtype)


def gram_cost(count, vectors):
    _, colours, sites, columns = vectors.shape
    return pl.CostEstimate(
        flops=count * 16 * colours * sites * columns * columns,
        bytes_accessed=4 * colours * sites * columns + count * 4 * columns * columns,
        transcendentals=0,
    )


def partial_elementals(vectors, momenta, table, count):
    _, colours, sites, columns = vectors.shape
    angles = np.arange(128, dtype=np.float32) * np.float32(2.0 * math.pi / LS)
    trig = jnp.asarray(np.stack([np.cos(angles), np.sin(angles)] * 4).astype(np.float32))
    shape = (2, columns, columns)
    far = list(range(count - 1, count // 2 - 1, -1))
    near = list(range(count // 2 - 1, -1, -1))
    momenta, table = in_hbm(momenta), in_hbm(table)
    small = [pltpu.SMEM(momenta.shape, jnp.int32), pltpu.SMEM(table.shape, jnp.int32)]
    params = pltpu.CompilerParams(vmem_limit_bytes=LIMIT)
    *first, vecs, left, trig = pl.pallas_call(
        functools.partial(gram_first, far),
        out_shape=[jax.ShapeDtypeStruct(shape, jnp.bfloat16) for _ in far]
        + [
            jax.ShapeDtypeStruct(vectors.shape, vectors.dtype),
            jax.ShapeDtypeStruct((2 * columns, colours * sites), vectors.dtype),
            jax.ShapeDtypeStruct(trig.shape, trig.dtype),
        ],
        in_specs=[HBM] * 4,
        out_specs=[VMEM] * (len(far) + 3),
        scratch_shapes=small + [pltpu.SemaphoreType.DMA((4,))],
        compiler_params=params,
        cost_estimate=gram_cost(len(far), vectors),
        name="gram_far",
    )(in_hbm(vectors), momenta, table, in_hbm(trig))
    second = pl.pallas_call(
        functools.partial(gram_second, near),
        out_shape=[
            jax.ShapeDtypeStruct(shape, jnp.float32 if k == 0 else jnp.bfloat16) for k in near
        ],
        in_specs=[VMEM] * 3 + [HBM] * 2,
        out_specs=[VMEM] * len(near),
        scratch_shapes=small + [pltpu.SemaphoreType.DMA((2,))],
        compiler_params=params,
        cost_estimate=gram_cost(len(near), vectors),
        name="gram_near",
    )(vecs, left, trig, momenta, table)
    return dict(zip(far + near, first + list(second)))


def mix_kernel(sink, peramb, table, labels, out, units, times, sems):
    load_units = pltpu.make_async_copy(table, units, sems.at[0])
    load_times = pltpu.make_async_copy(labels, times, sems.at[1])
    load_units.start()
    load_times.start()
    real = sink[0]
    imag = sink[1]
    columns = real.shape[0]
    left = jnp.concatenate(
        [jnp.concatenate([real, -imag], axis=1), jnp.concatenate([imag, real], axis=1)], axis=0
    )
    load_units.wait()
    load_times.wait()
    turns = units[1, lax.axis_index("space")]
    odd = lax.rem(turns, 2)
    phase_real = ((1 - odd) * (1 - turns)).astype(jnp.float32)
    phase_imag = (odd * (2 - turns)).astype(jnp.float32)
    me = lax.axis_index("tm")
    own = times[me]
    for k in range(peramb.shape[0]):
        n = me ^ k
        sign = jnp.where(times[n] > own, -1.0, 1.0).astype(jnp.float32)
        right = jnp.concatenate([peramb[n, 0], peramb[n, 1]], axis=0)
        mixed = jnp.dot(left, right, preferred_element_type=jnp.float32)
        mixed_real = mixed[:columns]
        mixed_imag = mixed[columns:]
        turn_real = sign * phase_real
        turn_imag = sign * phase_imag
        out[k, :, pl.ds(0, columns)] = (turn_real * mixed_real - turn_imag * mixed_imag).astype(
            out.dtype
        )
        out[k, :, pl.ds(columns, columns)] = (
            turn_real * mixed_imag + turn_imag * mixed_real
        ).astype(out.dtype)


def mix(sink, peramb, table, labels):
    slots, _, columns, _ = peramb.shape
    return pl.pallas_call(
        mix_kernel,
        out_shape=jax.ShapeDtypeStruct((slots, columns, 2 * columns), jnp.bfloat16),
        in_specs=[VMEM, VMEM, HBM, HBM],
        out_specs=VMEM,
        scratch_shapes=[
            pltpu.SMEM(table.shape, jnp.int32),
            pltpu.SMEM(labels.shape, jnp.int32),
            pltpu.SemaphoreType.DMA((2,)),
        ],
        compiler_params=pltpu.CompilerParams(vmem_limit_bytes=LIMIT),
        cost_estimate=pl.CostEstimate(
            flops=slots * 8 * columns**3, bytes_accessed=slots * 8 * columns**2, transcendentals=0
        ),
        name="mix",
    )(sink, peramb, in_hbm(table), in_hbm(labels))


def close_kernel(ks, before, mixed, *rest):
    sources = rest[: len(ks)]
    out, blocks, sems = rest[len(ks) + before :]
    columns = sources[0].shape[-1]
    me = lax.axis_index("tm")
    stores = []
    for i, (source, k) in enumerate(zip(sources, ks)):
        real = source[0]
        imag = source[1]
        right = jnp.concatenate(
            [jnp.concatenate([real, imag], axis=1), jnp.concatenate([-imag, real], axis=1)], axis=0
        )
        block = lax.dot_general(
            mixed[k], right, (((1,), (1,)), ((), ())), preferred_element_type=jnp.float32
        )
        blocks[i, 0] = block[:, :columns].astype(out.dtype)
        blocks[i, 1] = block[:, columns:].astype(out.dtype)
        store = pltpu.make_async_copy(blocks.at[i], out.at[me ^ k], sems.at[i])
        store.start()
        stores.append(store)
    for store in stores:
        store.wait()


def close(mixed, sources, ks, out=None):
    slots, columns, _ = mixed.shape
    before = [] if out is None else [out]
    shape = (slots, 2, columns, columns)
    return pl.pallas_call(
        functools.partial(close_kernel, ks, len(before)),
        out_shape=jax.ShapeDtypeStruct(shape, jnp.bfloat16),
        in_specs=[VMEM] * (1 + len(ks)) + [HBM] * len(before),
        out_specs=HBM,
        scratch_shapes=[
            pltpu.VMEM((len(ks),) + shape[1:], jnp.bfloat16),
            pltpu.SemaphoreType.DMA((len(ks),)),
        ],
        input_output_aliases={1 + len(ks): 0} if before else {},
        compiler_params=pltpu.CompilerParams(vmem_limit_bytes=LIMIT),
        cost_estimate=pl.CostEstimate(
            flops=len(ks) * 8 * columns**3,
            bytes_accessed=len(ks) * 12 * columns**2,
            transcendentals=0,
        ),
        name="close",
    )(mixed, *[sources[k] for k in ks], *before)


def swap(value, axis, size, distance):
    return lax.ppermute(value, axis, [(a, a ^ distance) for a in range(size)])


def body(space, times, evecs, peramb, momenta, unit_table, time_labels):
    table = unit_table.T
    partials = partial_elementals(evecs[0], momenta, table, space)
    total = partials[0]
    for k in range(1, space):
        total = total + swap(partials[k], "space", space, k).astype(jnp.float32)
    sink = total.astype(jnp.bfloat16)
    sources = {0: sink}
    for k in range(2, times, 2):
        sources[k] = swap(sink, "tm", times, k)
    mixed = mix(sink, peramb[0, 0], table, time_labels)
    for k in range(0, times, 2):
        sources[k + 1] = swap(sources[k], "tm", times, 1)
    last = [times - 2, times - 1]
    out = close(mixed, sources, [k for k in range(times) if k not in last])
    return close(mixed, sources, last, out)[None, None]


def solution(mesh):
    space, times = mesh.shape["space"], mesh.shape["tm"]
    return jax.shard_map(
        functools.partial(body, space, times),
        mesh=mesh,
        in_specs=(
            P("tm", None, None, "space", None),
            P("tm", "space", None, None, None, None),
            P(),
            P(),
            P(),
        ),
        out_specs=P("tm", "space", None, None, None, None),
        check_vma=False,
    )
```

time: 28.2 us -> 26.9 us (0.954)
  blocking collectives: 9.86 us -> 0 us
  waiting for transfers between devices: 4.96 us -> 10.8 us
  starting transfers between devices: 5.78 us -> 9.27 us
  local copies, waits for them, and re-layouts: 3.03 us -> 0.01 us
  Pallas kernels: 4.25 us -> 6.55 us
    all_gather x1 -> x0, blocking collectives: 9.86 us -> none  [body(): sources = lax.all_gather(sink[None], 'tm', axis=0, tiled=True)]
    ppermute x3 -> x10, waiting for transfers between devices: 4.96 us -> 10.8 us  [swap(): return lax.ppermute(value, axis, [(a, a ^ distance) for a in range(size)])]
    ppermute x3 -> x10, starting transfers between devices: 5.78 us -> 9.27 us  [swap(): return lax.ppermute(value, axis, [(a, a ^ distance) for a in range(size)])]
    unnamed x12 -> x2, local copies, waits for them, and re-layouts: 3.03 us -> 0.01 us
    pallas_call x2 -> x4, Pallas kernels: 3.24 us -> 5.4 us  [the longest x2 1.99 us: close(): pl.pallas_call(functools.partial(close_kernel, ks, len(before)), out_shap...]
  transfers between devices with their start and end apart: 3 -> 10, of which waited for: 2 -> 5; matrix products, arithmetic and copies ran while one was open for 0% -> 0% of each run, Pallas kernels for 0% -> 8%
where the time goes in v2:
time: 26.9 us; the launch traced here: 26.7 us
  waiting for transfers between devices  10.8 us (40%)
  starting transfers between devices  9.27 us (34%)
  Pallas kernels  6.55 us (24%)
    ppermute x10, waiting for transfers between devices, swap(): return lax.ppermute(value, axis, [(a, a ^ distance) for a in range(size)])  10.8 us
    ppermute x10, starting transfers between devices, swap(): return lax.ppermute(value, axis, [(a, a ^ distance) for a in range(size)])  9.27 us
    pallas_call x2, Pallas kernels, close(): pl.pallas_call(functools.partial(close_kernel, ks, len(before)), out_shap...  1.99 us
    pallas_call x1, Pallas kernels, partial_elementals(): pl.pallas_call(functools.partial(gram_first, far), out_shape=[jax.ShapeDt...  1.79 us
    pallas_call x1, Pallas kernels, partial_elementals(): pl.pallas_call(functools.partial(gram_second, near), out_shape=[jax.Shape...  1.62 us
    pallas_call x1, Pallas kernels, mix(): pl.pallas_call(mix_kernel, out_shape=jax.ShapeDtypeStruct((slots, columns...  1.15 us
  transfers between devices with their start and end apart: 10, of which 5 were waited for; matrix products, arithmetic and copies ran while one was open for 0% of the time, Pallas kernels for 8%

profile of v2, /device:TPU:0, one launch (start us, length us, event | category | flops | bytes accessed | tf_op | source)
XLA Modules:
  0.0 26.7 jit_solution(2470909353686556194)
XLA Ops:
  0.0 1.8 %gram_far.1 = (bf16[2,128,128]{2,1,0:T(8,128)(2,1)S(1)}, bf16[2,128,128]{2,1,0:T(8,128)(2,1)S(1)}, bf16[2,3,256,128]{3,2,1,0:T(8,128)(2,1)S(1)}, bf16[256,768]{1,0:T(8,128)(2,1)S(1)}, f32[8,128]{1,0:T(8,128)S(1)}) custom-call(bf16[2,3,256,128]{3,2,1,0:T(8,128)(2,1)} %bitcast.8, s32[4,3]{1,0:T(4,128)} %momenta.3, s32[2,4]{1,0:T(2,128)} %bitcast.5, ...), custom_call_target="tpu_custom_call" | custom-call | flops 402653184 | bytes 524288 | tf_op jit(solution)/shard_map/gram_far/pallas_call | solution.py:135
  1.8 0.0 copy-start
  1.8 1.6 %gram_near.1 = (bf16[2,128,128]{2,1,0:T(8,128)(2,1)S(1)}, f32[2,128,128]{2,1,0:T(8,128)S(1)}) custom-call(bf16[2,3,256,128]{3,2,1,0:T(8,128)(2,1)S(1)} %get-tuple-element.12.vecs, bf16[256,768]{1,0:T(8,128)(2,1)S(1)} %get-tuple-element.13.left, f32[8,128]{1,0:T(8,128)S(1)} %get-tuple-element.14.trig, s32[4,3]{1,0:T(4,128)} %momenta.3, s32[2,4]{1,0:T(2,128)} %bitcast.6), custom_call_target="tpu_custom_call" | custom-call | flops 402653184 | bytes 524288 | tf_op jit(solution)/shard_map/gram_near/pallas_call | solution.py:150
  3.4 3.1 %collective-permute-start = (bf16[2,128,128]{2,1,0:T(8,128)(2,1)S(1)}, bf16[2,128,128]{2,1,0:T(8,128)(2,1)S(1)}, u32[]{:S(2)}, u32[]{:S(2)}) collective-permute-start(bf16[2,128,128]{2,1,0:T(8,128)(2,1)S(1)} %get-tuple-element.16), channel_id=1, source_target_pairs={{0,1},{1,0},{2,3},{3,2},{4,5},{5,4},{6,7},{7,6},{8,9},{9,8},{10,11... | collective-permute-start | bytes 196616 | tf_op jit(solution)/shard_map/ppermute | solution.py:270
  6.5 2.6 %collective-permute-start.1 = (bf16[2,128,128]{2,1,0:T(8,128)(2,1)S(1)}, bf16[2,128,128]{2,1,0:T(8,128)(2,1)S(1)}, u32[]{:S(2)}, u32[]{:S(2)}) collective-permute-start(bf16[2,128,128]{2,1,0:T(8,128)(2,1)S(1)} %get-tuple-element.17), channel_id=1, source_target_pairs={{0,2},{1,3},{2,0},{3,1},{4,6},{5,7},{6,4},{7,5},{8,10},{9,11},{10,... | collective-permute-start | bytes 196616 | tf_op jit(solution)/shard_map/ppermute | solution.py:270
  9.1 0.0 collective-permute-start.2
  9.1 0.0 collective-permute-done
  9.1 4.7 %collective-permute-done.1 = bf16[2,128,128]{2,1,0:T(8,128)(2,1)S(1)} collective-permute-done((bf16[2,128,128]{2,1,0:T(8,128)(2,1)S(1)}, bf16[2,128,128]{2,1,0:T(8,128)(2,1)S(1)}, u32[]{:S(2)}, u32[]{:S(2)}) %collective-permute-start.1) | collective-permute-done | bytes 65568 | tf_op jit(solution)/shard_map/ppermute | solution.py:270
  13.8 1.4 %collective-permute-done.2 = bf16[2,128,128]{2,1,0:T(8,128)(2,1)S(1)} collective-permute-done((bf16[2,128,128]{2,1,0:T(8,128)(2,1)S(1)}, bf16[2,128,128]{2,1,0:T(8,128)(2,1)S(1)}, u32[]{:S(2)}, u32[]{:S(2)}) %collective-permute-start.2) | collective-permute-done | bytes 65568 | tf_op jit(solution)/shard_map/ppermute | solution.py:270
  15.3 1.6 %collective-permute-start.8 = (bf16[2,128,128]{2,1,0:T(8,128)(2,1)S(1)}, bf16[2,128,128]{2,1,0:T(8,128)(2,1)S(1)}, u32[]{:S(2)}, u32[]{:S(2)}) collective-permute-start(bf16[2,128,128]{2,1,0:T(8,128)(2,1)S(1)} %add_convert_fusion.sink.rest_0_), channel_id=1, source_target_pairs={{0,16},{4,20},{8,24},{12,28},{16,0},{20,4},{24,8},{28,12},{1,17},{... | collective-permute-start | bytes 196616 | tf_op jit(solution)/shard_map/ppermute | solution.py:270
  16.8 1.5 %collective-permute-start.6 = (bf16[2,128,128]{2,1,0:T(8,128)(2,1)S(1)}, bf16[2,128,128]{2,1,0:T(8,128)(2,1)S(1)}, u32[]{:S(2)}, u32[]{:S(2)}) collective-permute-start(bf16[2,128,128]{2,1,0:T(8,128)(2,1)S(1)} %add_convert_fusion.sink.rest_0_), channel_id=1, source_target_pairs={{0,8},{4,12},{8,0},{12,4},{16,24},{20,28},{24,16},{28,20},{1,9},{5... | collective-permute-start | bytes 196616 | tf_op jit(solution)/shard_map/ppermute | solution.py:270
  18.3 0.5 %collective-permute-start.3 = (bf16[2,128,128]{2,1,0:T(8,128)(2,1)S(1)}, bf16[2,128,128]{2,1,0:T(8,128)(2,1)S(1)}, u32[]{:S(2)}, u32[]{:S(2)}) collective-permute-start(bf16[2,128,128]{2,1,0:T(8,128)(2,1)S(1)} %add_convert_fusion.sink.rest_0_), channel_id=1, source_target_pairs={{0,24},{4,28},{8,16},{12,20},{16,8},{20,12},{24,0},{28,4},{1,25},{... | collective-permute-start | bytes 196616 | tf_op jit(solution)/shard_map/ppermute | solution.py:270
  18.8 0.0 collective-permute-start.5
  18.8 1.5 %collective-permute-done.8.rest_4_ = bf16[2,128,128]{2,1,0:T(8,128)(2,1)S(1)} collective-permute-done((bf16[2,128,128]{2,1,0:T(8,128)(2,1)S(1)}, bf16[2,128,128]{2,1,0:T(8,128)(2,1)S(1)}, u32[]{:S(2)}, u32[]{:S(2)}) %collective-permute-start.8) | collective-permute-done | bytes 65568 | tf_op jit(solution)/shard_map/ppermute | solution.py:270
  20.3 0.0 collective-permute-start.9
  20.3 0.8 %collective-permute-done.6.rest_2_ = bf16[2,128,128]{2,1,0:T(8,128)(2,1)S(1)} collective-permute-done((bf16[2,128,128]{2,1,0:T(8,128)(2,1)S(1)}, bf16[2,128,128]{2,1,0:T(8,128)(2,1)S(1)}, u32[]{:S(2)}, u32[]{:S(2)}) %collective-permute-start.6) | collective-permute-done | bytes 65568 | tf_op jit(solution)/shard_map/ppermute | solution.py:270
  21.1 0.0 collective-permute-start.7
  21.1 2.4 %collective-permute-done.3.rest_0_ = bf16[2,128,128]{2,1,0:T(8,128)(2,1)S(1)} collective-permute-done((bf16[2,128,128]{2,1,0:T(8,128)(2,1)S(1)}, bf16[2,128,128]{2,1,0:T(8,128)(2,1)S(1)}, u32[]{:S(2)}, u32[]{:S(2)}) %collective-permute-start.3) | collective-permute-done | bytes 65568 | tf_op jit(solution)/shard_map/ppermute | solution.py:270
  23.5 0.0 collective-permute-start.4
  23.5 0.0 copy-done
  23.5 1.2 %mix.1.mixed = bf16[8,128,256]{2,1,0:T(8,128)(2,1)S(1)} custom-call(bf16[2,128,128]{2,1,0:T(8,128)(2,1)S(1)} %add_convert_fusion.sink.rest_0_, bf16[8,2,128,128]{3,2,1,0:T(8,128)(2,1)S(1)} %bitcast.4, s32[2,4]{1,0:T(2,128)} %bitcast.7, s32[8]{0:T(128)} %labels.1), custom_call_target="tpu_custom_call" | custom-call | flops 134217728 | bytes 1048576 | tf_op jit(solution)/shard_map/mix/pallas_call | solution.py:203
  24.7 0.0 collective-permute-done.5.rest_1_
  24.7 0.0 collective-permute-done.9.rest_5_
  24.7 0.0 collective-permute-done.7.rest_3_
  24.7 1.1 %close.2.rest_2_ = bf16[8,2,128,128]{3,2,1,0:T(8,128)(2,1)} custom-call(bf16[8,128,256]{2,1,0:T(8,128)(2,1)S(1)} %mix.1.mixed, bf16[2,128,128]{2,1,0:T(8,128)(2,1)S(1)} %add_convert_fusion.sink.rest_0_, bf16[2,128,128]{2,1,0:T(8,128)(2,1)S(1)} %collective-permute-done.5.rest_1_, bf16[2,128,128]{2,1,0:T(8,128)(2,1)S(1)} %collective-permute-done.6.rest_2_, ...), custom_call_target="tpu_custom_call" | custom-call | flops 100663296 | bytes 1179648 | tf_op jit(solution)/shard_map/close/pallas_call | solution.py:249
  25.8 0.0 collective-permute-done.4.rest_1_
  25.8 0.9 %close.3 = bf16[8,2,128,128]{3,2,1,0:T(8,128)(2,1)} custom-call(bf16[8,128,256]{2,1,0:T(8,128)(2,1)S(1)} %mix.1.mixed, bf16[2,128,128]{2,1,0:T(8,128)(2,1)S(1)} %collective-permute-done.3.rest_0_, bf16[2,128,128]{2,1,0:T(8,128)(2,1)S(1)} %collective-permute-done.4.rest_1_, bf16[8,2,128,128]{3,2,1,0:T(8,128)(2,1)} %close.2.rest_2_), custom_call_target="tpu_custom_call", output_to_operand_aliasing={{}: (3, {})} | custom-call | flops 33554432 | bytes 393216 | tf_op jit(solution)/shard_map/close/pallas_call | solution.py:249
  (1 shorter events, 0.0 us)
Async XLA Ops:
  1.8 21.7 %copy-start = (bf16[1,1,8,2,128,128]{5,4,3,2,1,0:T(8,128)(2,1)S(1)}, bf16[1,1,8,2,128,128]{5,4,3,2,1,0:T(8,128)(2,1)}, u32[]{:S(2)}) copy-start(bf16[1,1,8,2,128,128]{5,4,3,2,1,0:T(8,128)(2,1)} %param.7) | copy-start | bytes 1572868
  3.4 5.7 %collective-permute-start = (bf16[2,128,128]{2,1,0:T(8,128)(2,1)S(1)}, bf16[2,128,128]{2,1,0:T(8,128)(2,1)S(1)}, u32[]{:S(2)}, u32[]{:S(2)}) collective-permute-start(bf16[2,128,128]{2,1,0:T(8,128)(2,1)S(1)} %get-tuple-element.16), channel_id=1, source_target_pairs={{0,1},{1,0},{2,3},{3,2},{4,5},{5,4},{6,7},{7,6},{8,9},{9,8},{10,11... | collective-permute-start | bytes 196616 | tf_op jit(solution)/shard_map/ppermute | solution.py:270
  6.5 7.3 %collective-permute-start.1 = (bf16[2,128,128]{2,1,0:T(8,128)(2,1)S(1)}, bf16[2,128,128]{2,1,0:T(8,128)(2,1)S(1)}, u32[]{:S(2)}, u32[]{:S(2)}) collective-permute-start(bf16[2,128,128]{2,1,0:T(8,128)(2,1)S(1)} %get-tuple-element.17), channel_id=1, source_target_pairs={{0,2},{1,3},{2,0},{3,1},{4,6},{5,7},{6,4},{7,5},{8,10},{9,11},{10,... | collective-permute-start | bytes 196616 | tf_op jit(solution)/shard_map/ppermute | solution.py:270
  9.1 6.1 %collective-permute-start.2 = (bf16[2,128,128]{2,1,0:T(8,128)(2,1)S(1)}, bf16[2,128,128]{2,1,0:T(8,128)(2,1)S(1)}, u32[]{:S(2)}, u32[]{:S(2)}) collective-permute-start(bf16[2,128,128]{2,1,0:T(8,128)(2,1)S(1)} %get-tuple-element.18), channel_id=1, source_target_pairs={{0,3},{1,2},{2,1},{3,0},{4,7},{5,6},{6,5},{7,4},{8,11},{9,10},{10,... | collective-permute-start | bytes 196616 | tf_op jit(solution)/shard_map/ppermute | solution.py:270
  15.3 5.0 %collective-permute-start.8 = (bf16[2,128,128]{2,1,0:T(8,128)(2,1)S(1)}, bf16[2,128,128]{2,1,0:T(8,128)(2,1)S(1)}, u32[]{:S(2)}, u32[]{:S(2)}) collective-permute-start(bf16[2,128,128]{2,1,0:T(8,128)(2,1)S(1)} %add_convert_fusion.sink.rest_0_), channel_id=1, source_target_pairs={{0,16},{4,20},{8,24},{12,28},{16,0},{20,4},{24,8},{28,12},{1,17},{... | collective-permute-start | bytes 196616 | tf_op jit(solution)/shard_map/ppermute | solution.py:270
  16.8 4.3 %collective-permute-start.6 = (bf16[2,128,128]{2,1,0:T(8,128)(2,1)S(1)}, bf16[2,128,128]{2,1,0:T(8,128)(2,1)S(1)}, u32[]{:S(2)}, u32[]{:S(2)}) collective-permute-start(bf16[2,128,128]{2,1,0:T(8,128)(2,1)S(1)} %add_convert_fusion.sink.rest_0_), channel_id=1, source_target_pairs={{0,8},{4,12},{8,0},{12,4},{16,24},{20,28},{24,16},{28,20},{1,9},{5... | collective-permute-start | bytes 196616 | tf_op jit(solution)/shard_map/ppermute | solution.py:270
  18.3 5.2 %collective-permute-start.3 = (bf16[2,128,128]{2,1,0:T(8,128)(2,1)S(1)}, bf16[2,128,128]{2,1,0:T(8,128)(2,1)S(1)}, u32[]{:S(2)}, u32[]{:S(2)}) collective-permute-start(bf16[2,128,128]{2,1,0:T(8,128)(2,1)S(1)} %add_convert_fusion.sink.rest_0_), channel_id=1, source_target_pairs={{0,24},{4,28},{8,16},{12,20},{16,8},{20,12},{24,0},{28,4},{1,25},{... | collective-permute-start | bytes 196616 | tf_op jit(solution)/shard_map/ppermute | solution.py:270
  18.8 5.9 %collective-permute-start.5 = (bf16[2,128,128]{2,1,0:T(8,128)(2,1)S(1)}, bf16[2,128,128]{2,1,0:T(8,128)(2,1)S(1)}, u32[]{:S(2)}, u32[]{:S(2)}) collective-permute-start(bf16[2,128,128]{2,1,0:T(8,128)(2,1)S(1)} %add_convert_fusion.sink.rest_0_), channel_id=1, source_target_pairs={{0,4},{4,0},{8,12},{12,8},{16,20},{20,16},{24,28},{28,24},{1,5},{5... | collective-permute-start | bytes 196616 | tf_op jit(solution)/shard_map/ppermute | solution.py:270
  20.3 4.4 %collective-permute-start.9 = (bf16[2,128,128]{2,1,0:T(8,128)(2,1)S(1)}, bf16[2,128,128]{2,1,0:T(8,128)(2,1)S(1)}, u32[]{:S(2)}, u32[]{:S(2)}) collective-permute-start(bf16[2,128,128]{2,1,0:T(8,128)(2,1)S(1)} %collective-permute-done.8.rest_4_), channel_id=1, source_target_pairs={{0,4},{4,0},{8,12},{12,8},{16,20},{20,16},{24,28},{28,24},{1,5},{5... | collective-permute-start | bytes 196616 | tf_op jit(solution)/shard_map/ppermute | solution.py:270
  21.1 3.6 %collective-permute-start.7 = (bf16[2,128,128]{2,1,0:T(8,128)(2,1)S(1)}, bf16[2,128,128]{2,1,0:T(8,128)(2,1)S(1)}, u32[]{:S(2)}, u32[]{:S(2)}) collective-permute-start(bf16[2,128,128]{2,1,0:T(8,128)(2,1)S(1)} %collective-permute-done.6.rest_2_), channel_id=1, source_target_pairs={{0,4},{4,0},{8,12},{12,8},{16,20},{20,16},{24,28},{28,24},{1,5},{5... | collective-permute-start | bytes 196616 | tf_op jit(solution)/shard_map/ppermute | solution.py:270
  23.5 2.3 %collective-permute-start.4 = (bf16[2,128,128]{2,1,0:T(8,128)(2,1)S(1)}, bf16[2,128,128]{2,1,0:T(8,128)(2,1)S(1)}, u32[]{:S(2)}, u32[]{:S(2)}) collective-permute-start(bf16[2,128,128]{2,1,0:T(8,128)(2,1)S(1)} %collective-permute-done.3.rest_0_), channel_id=1, source_target_pairs={{0,4},{4,0},{8,12},{12,8},{16,20},{20,16},{24,28},{28,24},{1,5},{5... | collective-permute-start | bytes 196616 | tf_op jit(solution)/shard_map/ppermute | solution.py:270

commit v3 on v2

--- a/solution.py
+++ b/solution.py
@@ -33,13 +33,16 @@
     return x, y, z
 
 
-def gram(vecs, left, moments, units, tables, parts, k):
+def momentum(moments, units, shift):
+    unit = lax.rem(lax.axis_index("space") + shift, lax.axis_size("space"))
+    moment = units[0, unit]
+    return [moments[moment, i].astype(jnp.float32) for i in range(3)]
+
+
+def gram(vecs, left, tables, parts, factors):
     _, colours, sites, columns = vecs.shape
     x, y, z = parts
-    moment = units[0, lax.axis_index("space") ^ k]
-    px = moments[moment, 0].astype(jnp.float32)
-    py = moments[moment, 1].astype(jnp.float32)
-    pz = moments[moment, 2].astype(jnp.float32)
+    px, py, pz = factors
     _, turns = floor_parts(px * x + py * y + pz * z, float(LS))
     index = turns.astype(jnp.int32)
     cosine = jnp.take_along_axis(tables[0], index, axis=1)
@@ -68,9 +71,9 @@
     return [jnp.broadcast_to(trig[i : i + 1, :], (sites, columns)) for i in range(2)]
 
 
-def gram_first(ks, evecs, momenta, table, trig_in, *rest):
-    outs = rest[: len(ks)]
-    vecs, left, trig, moments, units, sems = rest[len(ks) :]
+def gram_first(far, near, evecs, momenta, table, trig_in, *rest):
+    outs = rest[: len(far)]
+    vecs, left, trig, factors, moments, units, sems = rest[len(far) :]
     loads = [
         pltpu.make_async_copy(source, target, sems.at[i])
         for i, (source, target) in enumerate(
@@ -87,28 +90,22 @@
         for colour in range(colours):
             left[pl.ds(part * columns, columns), pl.ds(colour * sites, sites)] = vecs[part, colour].T
     tables = spread(trig, sites, columns)
-    for out, k in zip(outs, ks):
-        real, imag = gram(vecs, left, moments, units, tables, parts, k)
+    for i, k in enumerate(near):
+        for j, factor in enumerate(momentum(moments, units, k)):
+            factors[i, j] = jnp.full(factors.shape[2:], factor, jnp.float32)
+    for out, k in zip(outs, far):
+        real, imag = gram(vecs, left, tables, parts, momentum(moments, units, k))
         out[0] = real.astype(out.dtype)
         out[1] = imag.astype(out.dtype)
 
 
-def gram_second(ks, vecs, left, trig, momenta, table, *rest):
-    outs = rest[: len(ks)]
-    moments, units, sems = rest[len(ks) :]
-    loads = [
-        pltpu.make_async_copy(source, target, sems.at[i])
-        for i, (source, target) in enumerate(((momenta, moments), (table, units)))
-    ]
-    for load in loads:
-        load.start()
+def gram_second(vecs, left, trig, factors, *outs):
     _, _, sites, columns = vecs.shape
     parts = site_parts(sites, columns)
     tables = spread(trig, sites, columns)
-    for load in loads:
-        load.wait()
-    for out, k in zip(outs, ks):
-        real, imag = gram(vecs, left, moments, units, tables, parts, k)
+    for i, out in enumerate(outs):
+        own = [jnp.broadcast_to(factors[i, j, 0:1], (sites, columns)) for j in range(3)]
+        real, imag = gram(vecs, left, tables, parts, own)
         out[0] = real.astype(out.dtype)
         out[1] = imag.astype(out.dtype)
 
@@ -122,43 +119,41 @@
     )
 
 
-def partial_elementals(vectors, momenta, table, count):
+def partial_elementals(vectors, momenta, table, far, near):
     _, colours, sites, columns = vectors.shape
     angles = np.arange(128, dtype=np.float32) * np.float32(2.0 * math.pi / LS)
     trig = jnp.asarray(np.stack([np.cos(angles), np.sin(angles)] * 4).astype(np.float32))
     shape = (2, columns, columns)
-    far = list(range(count - 1, count // 2 - 1, -1))
-    near = list(range(count // 2 - 1, -1, -1))
     momenta, table = in_hbm(momenta), in_hbm(table)
     small = [pltpu.SMEM(momenta.shape, jnp.int32), pltpu.SMEM(table.shape, jnp.int32)]
     params = pltpu.CompilerParams(vmem_limit_bytes=LIMIT)
-    *first, vecs, left, trig = pl.pallas_call(
-        functools.partial(gram_first, far),
+    *first, vecs, left, trig, factors = pl.pallas_call(
+        functools.partial(gram_first, far, near),
         out_shape=[jax.ShapeDtypeStruct(shape, jnp.bfloat16) for _ in far]
         + [
             jax.ShapeDtypeStruct(vectors.shape, vectors.dtype),
             jax.ShapeDtypeStruct((2 * columns, colours * sites), vectors.dtype),
             jax.ShapeDtypeStruct(trig.shape, trig.dtype),
+            jax.ShapeDtypeStruct((len(near), 3, 8, columns), jnp.float32),
         ],
         in_specs=[HBM] * 4,
-        out_specs=[VMEM] * (len(far) + 3),
+        out_specs=[VMEM] * (len(far) + 4),
         scratch_shapes=small + [pltpu.SemaphoreType.DMA((4,))],
         compiler_params=params,
         cost_estimate=gram_cost(len(far), vectors),
         name="gram_far",
     )(in_hbm(vectors), momenta, table, in_hbm(trig))
     second = pl.pallas_call(
-        functools.partial(gram_second, near),
+        gram_second,
         out_shape=[
             jax.ShapeDtypeStruct(shape, jnp.float32 if k == 0 else jnp.bfloat16) for k in near
         ],
-        in_specs=[VMEM] * 3 + [HBM] * 2,
+        in_specs=[VMEM] * 4,
         out_specs=[VMEM] * len(near),
-        scratch_shapes=small + [pltpu.SemaphoreType.DMA((2,))],
         compiler_params=params,
         cost_estimate=gram_cost(len(near), vectors),
         name="gram_near",
-    )(vecs, left, trig, momenta, table)
+    )(vecs, left, trig, factors)
     return dict(zip(far + near, first + list(second)))
 
 
@@ -182,7 +177,7 @@
     me = lax.axis_index("tm")
     own = times[me]
     for k in range(peramb.shape[0]):
-        n = me ^ k
+        n = lax.axis_index("tm") ^ k
         sign = jnp.where(times[n] > own, -1.0, 1.0).astype(jnp.float32)
         right = jnp.concatenate([peramb[n, 0], peramb[n, 1]], axis=0)
         mixed = jnp.dot(left, right, preferred_element_type=jnp.float32)
@@ -222,7 +217,6 @@
     sources = rest[: len(ks)]
     out, blocks, sems = rest[len(ks) + before :]
     columns = sources[0].shape[-1]
-    me = lax.axis_index("tm")
     stores = []
     for i, (source, k) in enumerate(zip(sources, ks)):
         real = source[0]
@@ -235,7 +229,7 @@
         )
         blocks[i, 0] = block[:, :columns].astype(out.dtype)
         blocks[i, 1] = block[:, columns:].astype(out.dtype)
-        store = pltpu.make_async_copy(blocks.at[i], out.at[me ^ k], sems.at[i])
+        store = pltpu.make_async_copy(blocks.at[i], out.at[lax.axis_index("tm") ^ k], sems.at[i])
         store.start()
         stores.append(store)
     for store in stores:
@@ -266,24 +260,33 @@
     )(mixed, *[sources[k] for k in ks], *before)
 
 
-def swap(value, axis, size, distance):
-    return lax.ppermute(value, axis, [(a, a ^ distance) for a in range(size)])
+def sum_order(space):
+    shifts = list(range(1, space))
+    far = space // 2
+    return shifts, far
+
+
+def hop_order(times):
+    return [times - 2] + list(range(2, times - 2, 2))
 
 
 def body(space, times, evecs, peramb, momenta, unit_table, time_labels):
     table = unit_table.T
-    partials = partial_elementals(evecs[0], momenta, table, space)
+    shifts, far = sum_order(space)
+    partials = partial_elementals(evecs[0], momenta, table, shifts[:far], shifts[far:] + [0])
     total = partials[0]
-    for k in range(1, space):
-        total = total + swap(partials[k], "space", space, k).astype(jnp.float32)
+    for shift in shifts:
+        pairs = [(a, (a + shift) % space) for a in range(space)]
+        total = total + lax.ppermute(partials[shift], "space", pairs).astype(jnp.float32)
     sink = total.astype(jnp.bfloat16)
     sources = {0: sink}
-    for k in range(2, times, 2):
-        sources[k] = swap(sink, "tm", times, k)
+    hops = hop_order(times)
+    for k in hops:
+        sources[k] = lax.ppermute(sink, "tm", [(a, a ^ k) for a in range(times)])
     mixed = mix(sink, peramb[0, 0], table, time_labels)
-    for k in range(0, times, 2):
-        sources[k + 1] = swap(sources[k], "tm", times, 1)
-    last = [times - 2, times - 1]
+    for k in [0] + hops:
+        sources[k + 1] = lax.ppermute(sources[k], "tm", [(a, a ^ 1) for a in range(times)])
+    last = [k + i for k in hops[-2:] for i in range(2)]
     out = close(mixed, sources, [k for k in range(times) if k not in last])
     return close(mixed, sources, last, out)[None, None]
 

time: 26.9 us -> 25.9 us (0.963)
  Pallas kernels: 6.55 us -> 5.68 us
  waiting for transfers between devices: 10.8 us -> 10.2 us
  starting transfers between devices: 9.27 us -> 9.72 us
    pallas_call x2, Pallas kernels: 3.4 us -> 2.54 us  [the longest x1 1.79 us: partial_elementals(): pl.pallas_call(functools.partial(gram_first, far, near), out_shape=[jax.S...]
    ppermute x10, waiting for transfers between devices: 10.8 us -> 10.2 us  [the longest x3 6.44 us: body(): lax.ppermute(partials[shift], 'space', pairs).astype(jnp.float32)]
    ppermute x10, starting transfers between devices: 9.27 us -> 9.72 us  [the longest x3 6.14 us: body(): lax.ppermute(partials[shift], 'space', pairs).astype(jnp.float32)]
  transfers between devices with their start and end apart: 10 -> 10, of which waited for: 5 -> 6; matrix products, arithmetic and copies ran while one was open for 0% -> 0% of each run, Pallas kernels for 8% -> 8%
where the time goes in v3:
time: 25.9 us; the launch traced here: 25.7 us
  waiting for transfers between devices  10.2 us (39%)
  starting transfers between devices  9.72 us (38%)
  Pallas kernels  5.68 us (22%)
    ppermute x3, waiting for transfers between devices, body(): lax.ppermute(partials[shift], 'space', pairs).astype(jnp.float32)  6.44 us
    ppermute x3, starting transfers between devices, body(): lax.ppermute(partials[shift], 'space', pairs).astype(jnp.float32)  6.14 us
    ppermute x3, waiting for transfers between devices, body(): sources[k] = lax.ppermute(sink, 'tm', [(a, a ^ k) for a in range(times)])  3.72 us
    ppermute x3, starting transfers between devices, body(): sources[k] = lax.ppermute(sink, 'tm', [(a, a ^ k) for a in range(times)])  3.55 us
    pallas_call x2, Pallas kernels, close(): pl.pallas_call(functools.partial(close_kernel, ks, len(before)), out_shap...  1.99 us
    pallas_call x1, Pallas kernels, partial_elementals(): pl.pallas_call(functools.partial(gram_first, far, near), out_shape=[jax.S...  1.79 us
    pallas_call x1, Pallas kernels, mix(): pl.pallas_call(mix_kernel, out_shape=jax.ShapeDtypeStruct((slots, columns...  1.15 us
    pallas_call x1, Pallas kernels, partial_elementals(): pl.pallas_call(gram_second, out_shape=[jax.ShapeDtypeStruct(shape, jnp.fl...  0.75 us
  transfers between devices with their start and end apart: 10, of which 6 were waited for; matrix products, arithmetic and copies ran while one was open for 0% of the time, Pallas kernels for 8%

profile of v3, /device:TPU:0, one launch (start us, length us, event | category | flops | bytes accessed | tf_op | source)
XLA Modules:
  0.0 25.7 jit_solution(8081683388418556056)
XLA Ops:
  0.0 1.8 %gram_far.1 = (bf16[2,128,128]{2,1,0:T(8,128)(2,1)S(1)}, bf16[2,128,128]{2,1,0:T(8,128)(2,1)S(1)}, bf16[2,3,256,128]{3,2,1,0:T(8,128)(2,1)S(1)}, bf16[256,768]{1...) custom-call(bf16[2,3,256,128]{3,2,1,0:T(8,128)(2,1)} %bitcast.7, s32[4,3]{1,0:T(4,128)} %momenta.1, ...), custom_call_target="tpu_custom_call" | custom-call | flops 402653184 | bytes 524288 | tf_op jit(solution)/shard_map/gram_far/pallas_call | solution.py:130
  1.8 0.0 copy-start
  1.8 0.8 %gram_near.1 = (bf16[2,128,128]{2,1,0:T(8,128)(2,1)S(1)}, f32[2,128,128]{2,1,0:T(8,128)S(1)}) custom-call(bf16[2,3,256,128]{3,2,1,0:T(8,128)(2,1)S(1)} %get-tuple-element.13.vecs, bf16[256,768]{1,0:T(8,128)(2,1)S(1)} %get-tuple-element.14.left, f32[8,128]{1,0:T(8,128)S(1)} %get-tuple-element.15.trig, f32[2,3,8,128]{3,2,1,0:T(8,128)S(1)} %get-tuple-element.16.factors), custom_call_target="tpu_custom_call" | custom-call | flops 402653184 | bytes 524288 | tf_op jit(solution)/shard_map/gram_near/pallas_call | solution.py:146
  2.6 5.1 %collective-permute-start.2 = (bf16[2,128,128]{2,1,0:T(8,128)(2,1)S(1)}, bf16[2,128,128]{2,1,0:T(8,128)(2,1)S(1)}, u32[]{:S(2)}, u32[]{:S(2)}) collective-permute-start(bf16[2,128,128]{2,1,0:T(8,128)(2,1)S(1)} %get-tuple-element.20), channel_id=1, source_target_pairs={{0,3},{1,0},{2,1},{3,2},{4,7},{5,4},{6,5},{7,6},{8,11},{9,8},{10,9... | collective-permute-start | bytes 196616 | tf_op jit(solution)/shard_map/ppermute | solution.py:280
  7.7 0.0 collective-permute-start
  7.7 1.0 %collective-permute-start.1 = (bf16[2,128,128]{2,1,0:T(8,128)(2,1)S(1)}, bf16[2,128,128]{2,1,0:T(8,128)(2,1)S(1)}, u32[]{:S(2)}, u32[]{:S(2)}) collective-permute-start(bf16[2,128,128]{2,1,0:T(8,128)(2,1)S(1)} %get-tuple-element.19), channel_id=1, source_target_pairs={{0,2},{1,3},{2,0},{3,1},{4,6},{5,7},{6,4},{7,5},{8,10},{9,11},{10,... | collective-permute-start | bytes 196616 | tf_op jit(solution)/shard_map/ppermute | solution.py:280
  8.7 1.5 %collective-permute-done.2 = bf16[2,128,128]{2,1,0:T(8,128)(2,1)S(1)} collective-permute-done((bf16[2,128,128]{2,1,0:T(8,128)(2,1)S(1)}, bf16[2,128,128]{2,1,0:T(8,128)(2,1)S(1)}, u32[]{:S(2)}, u32[]{:S(2)}) %collective-permute-start.2) | collective-permute-done | bytes 65568 | tf_op jit(solution)/shard_map/ppermute | solution.py:280
  10.2 3.7 %collective-permute-done = bf16[2,128,128]{2,1,0:T(8,128)(2,1)S(1)} collective-permute-done((bf16[2,128,128]{2,1,0:T(8,128)(2,1)S(1)}, bf16[2,128,128]{2,1,0:T(8,128)(2,1)S(1)}, u32[]{:S(2)}, u32[]{:S(2)}) %collective-permute-start) | collective-permute-done | bytes 65568 | tf_op jit(solution)/shard_map/ppermute | solution.py:280
  13.8 1.3 %collective-permute-done.1 = bf16[2,128,128]{2,1,0:T(8,128)(2,1)S(1)} collective-permute-done((bf16[2,128,128]{2,1,0:T(8,128)(2,1)S(1)}, bf16[2,128,128]{2,1,0:T(8,128)(2,1)S(1)}, u32[]{:S(2)}, u32[]{:S(2)}) %collective-permute-start.1) | collective-permute-done | bytes 65568 | tf_op jit(solution)/shard_map/ppermute | solution.py:280
  15.2 2.5 %collective-permute-start.8 = (bf16[2,128,128]{2,1,0:T(8,128)(2,1)S(1)}, bf16[2,128,128]{2,1,0:T(8,128)(2,1)S(1)}, u32[]{:S(2)}, u32[]{:S(2)}) collective-permute-start(bf16[2,128,128]{2,1,0:T(8,128)(2,1)S(1)} %add_convert_fusion.sink.rest_0_), channel_id=1, source_target_pairs={{0,24},{4,28},{8,16},{12,20},{16,8},{20,12},{24,0},{28,4},{1,25},{... | collective-permute-start | bytes 196616 | tf_op jit(solution)/shard_map/ppermute | solution.py:285
  17.7 0.5 %collective-permute-start.5 = (bf16[2,128,128]{2,1,0:T(8,128)(2,1)S(1)}, bf16[2,128,128]{2,1,0:T(8,128)(2,1)S(1)}, u32[]{:S(2)}, u32[]{:S(2)}) collective-permute-start(bf16[2,128,128]{2,1,0:T(8,128)(2,1)S(1)} %add_convert_fusion.sink.rest_0_), channel_id=1, source_target_pairs={{0,16},{4,20},{8,24},{12,28},{16,0},{20,4},{24,8},{28,12},{1,17},{... | collective-permute-start | bytes 196616 | tf_op jit(solution)/shard_map/ppermute | solution.py:285
  18.2 0.5 %collective-permute-start.3 = (bf16[2,128,128]{2,1,0:T(8,128)(2,1)S(1)}, bf16[2,128,128]{2,1,0:T(8,128)(2,1)S(1)}, u32[]{:S(2)}, u32[]{:S(2)}) collective-permute-start(bf16[2,128,128]{2,1,0:T(8,128)(2,1)S(1)} %add_convert_fusion.sink.rest_0_), channel_id=1, source_target_pairs={{0,8},{4,12},{8,0},{12,4},{16,24},{20,28},{24,16},{28,20},{1,9},{5... | collective-permute-start | bytes 196616 | tf_op jit(solution)/shard_map/ppermute | solution.py:285
  18.7 0.0 collective-permute-start.7
  18.8 1.7 %collective-permute-done.8.rest_2_ = bf16[2,128,128]{2,1,0:T(8,128)(2,1)S(1)} collective-permute-done((bf16[2,128,128]{2,1,0:T(8,128)(2,1)S(1)}, bf16[2,128,128]{2,1,0:T(8,128)(2,1)S(1)}, u32[]{:S(2)}, u32[]{:S(2)}) %collective-permute-start.8) | collective-permute-done | bytes 65568 | tf_op jit(solution)/shard_map/ppermute | solution.py:285
  20.4 0.0 collective-permute-start.9
  20.4 1.5 %collective-permute-done.5.rest_2_ = bf16[2,128,128]{2,1,0:T(8,128)(2,1)S(1)} collective-permute-done((bf16[2,128,128]{2,1,0:T(8,128)(2,1)S(1)}, bf16[2,128,128]{2,1,0:T(8,128)(2,1)S(1)}, u32[]{:S(2)}, u32[]{:S(2)}) %collective-permute-start.5) | collective-permute-done | bytes 65568 | tf_op jit(solution)/shard_map/ppermute | solution.py:285
  22.0 0.0 collective-permute-start.6
  22.0 0.5 %collective-permute-done.3.rest_0_ = bf16[2,128,128]{2,1,0:T(8,128)(2,1)S(1)} collective-permute-done((bf16[2,128,128]{2,1,0:T(8,128)(2,1)S(1)}, bf16[2,128,128]{2,1,0:T(8,128)(2,1)S(1)}, u32[]{:S(2)}, u32[]{:S(2)}) %collective-permute-start.3) | collective-permute-done | bytes 65568 | tf_op jit(solution)/shard_map/ppermute | solution.py:285
  22.5 0.0 collective-permute-start.4
  22.5 0.0 copy-done
  22.5 1.1 %mix.1.mixed = bf16[8,128,256]{2,1,0:T(8,128)(2,1)S(1)} custom-call(bf16[2,128,128]{2,1,0:T(8,128)(2,1)S(1)} %add_convert_fusion.sink.rest_0_, bf16[8,2,128,128]{3,2,1,0:T(8,128)(2,1)S(1)} %bitcast.4, s32[2,4]{1,0:T(2,128)} %bitcast.6, s32[8]{0:T(128)} %labels.1), custom_call_target="tpu_custom_call" | custom-call | flops 134217728 | bytes 1048576 | tf_op jit(solution)/shard_map/mix/pallas_call | solution.py:198
  23.6 0.0 collective-permute-done.7.rest_1_
  23.7 0.0 collective-permute-done.9.rest_3_
  23.7 1.0 %close.2.rest_4_ = bf16[8,2,128,128]{3,2,1,0:T(8,128)(2,1)} custom-call(bf16[8,128,256]{2,1,0:T(8,128)(2,1)S(1)} %mix.1.mixed, bf16[2,128,128]{2,1,0:T(8,128)(2,1)S(1)} %add_convert_fusion.sink.rest_0_, bf16[2,128,128]{2,1,0:T(8,128)(2,1)S(1)} %collective-permute-done.7.rest_1_, bf16[2,128,128]{2,1,0:T(8,128)(2,1)S(1)} %collective-permute-done.8.rest_2_, ...), custom_call_target="tpu_custom_call" | custom-call | flops 67108864 | bytes 786432 | tf_op jit(solution)/shard_map/close/pallas_call | solution.py:243
  24.7 0.0 collective-permute-done.6.rest_3_
  24.7 0.0 collective-permute-done.4.rest_1_
  24.7 1.0 %close.3 = bf16[8,2,128,128]{3,2,1,0:T(8,128)(2,1)} custom-call(bf16[8,128,256]{2,1,0:T(8,128)(2,1)S(1)} %mix.1.mixed, bf16[2,128,128]{2,1,0:T(8,128)(2,1)S(1)} %collective-permute-done.3.rest_0_, bf16[2,128,128]{2,1,0:T(8,128)(2,1)S(1)} %collective-permute-done.4.rest_1_, ...), custom_call_target="tpu_custom_call", output_to_operand_aliasing={{}: (5, {})} | custom-call | flops 67108864 | bytes 786432 | tf_op jit(solution)/shard_map/close/pallas_call | solution.py:243
  (1 shorter events, 0.0 us)
Async XLA Ops:
  1.8 20.7 %copy-start = (bf16[1,1,8,2,128,128]{5,4,3,2,1,0:T(8,128)(2,1)S(1)}, bf16[1,1,8,2,128,128]{5,4,3,2,1,0:T(8,128)(2,1)}, u32[]{:S(2)}) copy-start(bf16[1,1,8,2,128,128]{5,4,3,2,1,0:T(8,128)(2,1)} %param.7) | copy-start | bytes 1572868
  2.6 7.6 %collective-permute-start.2 = (bf16[2,128,128]{2,1,0:T(8,128)(2,1)S(1)}, bf16[2,128,128]{2,1,0:T(8,128)(2,1)S(1)}, u32[]{:S(2)}, u32[]{:S(2)}) collective-permute-start(bf16[2,128,128]{2,1,0:T(8,128)(2,1)S(1)} %get-tuple-element.20), channel_id=1, source_target_pairs={{0,3},{1,0},{2,1},{3,2},{4,7},{5,4},{6,5},{7,6},{8,11},{9,8},{10,9... | collective-permute-start | bytes 196616 | tf_op jit(solution)/shard_map/ppermute | solution.py:280
  7.7 6.2 %collective-permute-start = (bf16[2,128,128]{2,1,0:T(8,128)(2,1)S(1)}, bf16[2,128,128]{2,1,0:T(8,128)(2,1)S(1)}, u32[]{:S(2)}, u32[]{:S(2)}) collective-permute-start(bf16[2,128,128]{2,1,0:T(8,128)(2,1)S(1)} %get-tuple-element.18), channel_id=1, source_target_pairs={{0,1},{1,2},{2,3},{3,0},{4,5},{5,6},{6,7},{7,4},{8,9},{9,10},{10,1... | collective-permute-start | bytes 196616 | tf_op jit(solution)/shard_map/ppermute | solution.py:280
  7.7 7.5 %collective-permute-start.1 = (bf16[2,128,128]{2,1,0:T(8,128)(2,1)S(1)}, bf16[2,128,128]{2,1,0:T(8,128)(2,1)S(1)}, u32[]{:S(2)}, u32[]{:S(2)}) collective-permute-start(bf16[2,128,128]{2,1,0:T(8,128)(2,1)S(1)} %get-tuple-element.19), channel_id=1, source_target_pairs={{0,2},{1,3},{2,0},{3,1},{4,6},{5,7},{6,4},{7,5},{8,10},{9,11},{10,... | collective-permute-start | bytes 196616 | tf_op jit(solution)/shard_map/ppermute | solution.py:280
  15.2 5.2 %collective-permute-start.8 = (bf16[2,128,128]{2,1,0:T(8,128)(2,1)S(1)}, bf16[2,128,128]{2,1,0:T(8,128)(2,1)S(1)}, u32[]{:S(2)}, u32[]{:S(2)}) collective-permute-start(bf16[2,128,128]{2,1,0:T(8,128)(2,1)S(1)} %add_convert_fusion.sink.rest_0_), channel_id=1, source_target_pairs={{0,24},{4,28},{8,16},{12,20},{16,8},{20,12},{24,0},{28,4},{1,25},{... | collective-permute-start | bytes 196616 | tf_op jit(solution)/shard_map/ppermute | solution.py:285
  17.7 4.3 %collective-permute-start.5 = (bf16[2,128,128]{2,1,0:T(8,128)(2,1)S(1)}, bf16[2,128,128]{2,1,0:T(8,128)(2,1)S(1)}, u32[]{:S(2)}, u32[]{:S(2)}) collective-permute-start(bf16[2,128,128]{2,1,0:T(8,128)(2,1)S(1)} %add_convert_fusion.sink.rest_0_), channel_id=1, source_target_pairs={{0,16},{4,20},{8,24},{12,28},{16,0},{20,4},{24,8},{28,12},{1,17},{... | collective-permute-start | bytes 196616 | tf_op jit(solution)/shard_map/ppermute | solution.py:285
  18.2 4.3 %collective-permute-start.3 = (bf16[2,128,128]{2,1,0:T(8,128)(2,1)S(1)}, bf16[2,128,128]{2,1,0:T(8,128)(2,1)S(1)}, u32[]{:S(2)}, u32[]{:S(2)}) collective-permute-start(bf16[2,128,128]{2,1,0:T(8,128)(2,1)S(1)} %add_convert_fusion.sink.rest_0_), channel_id=1, source_target_pairs={{0,8},{4,12},{8,0},{12,4},{16,24},{20,28},{24,16},{28,20},{1,9},{5... | collective-permute-start | bytes 196616 | tf_op jit(solution)/shard_map/ppermute | solution.py:285
  18.7 4.9 %collective-permute-start.7 = (bf16[2,128,128]{2,1,0:T(8,128)(2,1)S(1)}, bf16[2,128,128]{2,1,0:T(8,128)(2,1)S(1)}, u32[]{:S(2)}, u32[]{:S(2)}) collective-permute-start(bf16[2,128,128]{2,1,0:T(8,128)(2,1)S(1)} %add_convert_fusion.sink.rest_0_), channel_id=1, source_target_pairs={{0,4},{4,0},{8,12},{12,8},{16,20},{20,16},{24,28},{28,24},{1,5},{5... | collective-permute-start | bytes 196616 | tf_op jit(solution)/shard_map/ppermute | solution.py:288
  20.4 3.2 %collective-permute-start.9 = (bf16[2,128,128]{2,1,0:T(8,128)(2,1)S(1)}, bf16[2,128,128]{2,1,0:T(8,128)(2,1)S(1)}, u32[]{:S(2)}, u32[]{:S(2)}) collective-permute-start(bf16[2,128,128]{2,1,0:T(8,128)(2,1)S(1)} %collective-permute-done.8.rest_2_), channel_id=1, source_target_pairs={{0,4},{4,0},{8,12},{12,8},{16,20},{20,16},{24,28},{28,24},{1,5},{5... | collective-permute-start | bytes 196616 | tf_op jit(solution)/shard_map/ppermute | solution.py:288
  22.0 2.7 %collective-permute-start.6 = (bf16[2,128,128]{2,1,0:T(8,128)(2,1)S(1)}, bf16[2,128,128]{2,1,0:T(8,128)(2,1)S(1)}, u32[]{:S(2)}, u32[]{:S(2)}) collective-permute-start(bf16[2,128,128]{2,1,0:T(8,128)(2,1)S(1)} %collective-permute-done.5.rest_2_), channel_id=1, source_target_pairs={{0,4},{4,0},{8,12},{12,8},{16,20},{20,16},{24,28},{28,24},{1,5},{5... | collective-permute-start | bytes 196616 | tf_op jit(solution)/shard_map/ppermute | solution.py:288
  22.5 2.2 %collective-permute-start.4 = (bf16[2,128,128]{2,1,0:T(8,128)(2,1)S(1)}, bf16[2,128,128]{2,1,0:T(8,128)(2,1)S(1)}, u32[]{:S(2)}, u32[]{:S(2)}) collective-permute-start(bf16[2,128,128]{2,1,0:T(8,128)(2,1)S(1)} %collective-permute-done.3.rest_0_), channel_id=1, source_target_pairs={{0,4},{4,0},{8,12},{12,8},{16,20},{20,16},{24,28},{28,24},{1,5},{5... | collective-permute-start | bytes 196616 | tf_op jit(solution)/shard_map/ppermute | solution.py:288

commit v4 on v3

v4 whole, which is shorter than its diff:
```python
import functools
import math

import jax
import jax.numpy as jnp
import numpy as np
from jax import lax
from jax.experimental import pallas as pl
from jax.experimental.pallas import tpu as pltpu
from jax.sharding import PartitionSpec as P


LS = 40
LATE = 4
LIMIT = 12 * 1024 * 1024
VMEM = pl.BlockSpec(memory_space=pltpu.VMEM)
HBM = pl.BlockSpec(memory_space=pltpu.HBM)


def floor_parts(values, base):
    quotient = jnp.floor((values + 0.5) * (1.0 / base))
    return quotient, values - base * quotient


def in_hbm(value):
    return pltpu.with_memory_space_constraint(value, pltpu.HBM)


def site_parts(count, sites):
    first = (lax.axis_index("space") * sites).astype(jnp.float32)
    site = lax.broadcasted_iota(jnp.int32, (count, sites), 1).astype(jnp.float32) + first
    row, x = floor_parts(site, float(LS))
    if sites * lax.axis_size("space") <= LS * LS:
        return [x, row]
    z, y = floor_parts(row, float(LS))
    return [x, y, z]


def ring(size):
    return [at ^ (at >> 1) for at in range(size)]


def partner(size, shift):
    places = ring(size)
    me = lax.axis_index("space")
    target = jnp.int32(0)
    for at, place in enumerate(places):
        target = jnp.where(me == place, places[(at + shift) % size], target)
    return target


def along(size, shift):
    places = ring(size)
    return [(place, places[(at + shift) % size]) for at, place in enumerate(places)]


def phases(moments, units, trig, shifts, sites, targets):
    count = len(shifts)
    which = lax.broadcasted_iota(jnp.int32, (count, sites), 0)
    rows = [
        units[0, partner(lax.axis_size("space"), shift)]
        for shift in shifts
    ]
    product = jnp.zeros((count, sites), jnp.float32)
    for i, part in enumerate(site_parts(count, sites)):
        factor = jnp.zeros((count, sites), jnp.float32)
        for k, row in enumerate(rows):
            factor = jnp.where(which == k, moments[row, i].astype(jnp.float32), factor)
        product = product + factor * part
    _, turns = floor_parts(product, float(LS))
    index = turns.astype(jnp.int32)
    lanes = trig.shape[1]
    values = []
    for i in range(2):
        table = jnp.broadcast_to(trig[i : i + 1, :], (count, lanes))
        pieces = [
            jnp.take_along_axis(
                table, index[:, at : at + lanes], axis=1, mode="promise_in_bounds"
            )
            for at in range(0, sites, lanes)
        ]
        values.append(jnp.concatenate(pieces, axis=1))
    rest = jnp.concatenate(values, axis=0)
    pieces = []
    for _ in range(3):
        piece = rest.astype(jnp.bfloat16).astype(jnp.float32)
        pieces.append(piece)
        rest = rest - piece
    left = jnp.concatenate(pieces, axis=0).astype(jnp.bfloat16)
    shape = (left.shape[0], 2 * count * lanes)
    row = lax.rem(lax.broadcasted_iota(jnp.int32, shape, 0), 2 * count)
    column = lax.div(lax.broadcasted_iota(jnp.int32, shape, 1), lanes)
    right = (row == column).astype(jnp.float32).astype(jnp.bfloat16)
    spread = lax.dot_general(
        left, right, (((0,), (0,)), ((), ())), preferred_element_type=jnp.float32
    )
    for k, target in enumerate(targets):
        for i in range(2):
            at = (i * count + k) * lanes
            target[i] = spread[:, at : at + lanes]


def gram(vecs, left, wave, colour):
    sites = vecs.shape[2]
    real = vecs[0, colour].astype(jnp.float32)
    imag = vecs[1, colour].astype(jnp.float32)
    cosine = wave[0]
    sine = wave[1]
    phased = jnp.concatenate(
        [
            (cosine * real + sine * imag).astype(jnp.bfloat16),
            (cosine * imag - sine * real).astype(jnp.bfloat16),
        ],
        axis=1,
    )
    return jnp.dot(
        left[:, pl.ds(colour * sites, sites)], phased, preferred_element_type=jnp.float32
    )


def keep(out, total):
    columns = out.shape[-1]
    out[0] = (total[:columns, :columns] + total[columns:, columns:]).astype(out.dtype)
    out[1] = (total[:columns, columns:] - total[columns:, :columns]).astype(out.dtype)


def gram_first(far, near, evecs, momenta, table, trig_in, *rest):
    outs = rest[: len(far)]
    vecs, left, waves, own, trig, moments, units, sems = rest[len(far) :]
    _, colours, sites, columns = vecs.shape
    small = [
        pltpu.make_async_copy(source, target, sems.at[i])
        for i, (source, target) in enumerate(((momenta, moments), (table, units), (trig_in, trig)))
    ]
    large = [pltpu.make_async_copy(evecs, vecs, sems.at[3])]
    for load in small + large:
        load.start()
    for load in small:
        load.wait()
    shifts = far + near
    targets = [own.at[i] for i in range(len(far))] + [waves.at[i] for i in range(len(near))]
    for at in range(0, len(shifts), 4):
        phases(moments, units, trig, shifts[at : at + 4], sites, targets[at : at + 4])
    totals = [None] * len(far)
    for colour in range(colours):
        if colour == 0:
            large[0].wait()
        for part in range(2):
            left[pl.ds(part * columns, columns), pl.ds(colour * sites, sites)] = vecs[part, colour].T
        if len(far) > 4:
            continue
        for i in range(len(far)):
            term = gram(vecs, left, own.at[i], colour)
            totals[i] = term if totals[i] is None else totals[i] + term
    for i, out in enumerate(outs):
        if totals[i] is None:
            totals[i] = sum(gram(vecs, left, own.at[i], colour) for colour in range(colours))
        keep(out, totals[i])


def gram_second(vecs, left, waves, *outs):
    for i, out in enumerate(outs):
        keep(out, sum(gram(vecs, left, waves.at[i], colour) for colour in range(vecs.shape[1])))


def gram_cost(count, vectors):
    _, colours, sites, columns = vectors.shape
    return pl.CostEstimate(
        flops=count * 16 * colours * sites * columns * columns,
        bytes_accessed=4 * colours * sites * columns + count * 4 * columns * columns,
        transcendentals=0,
    )


def partial_elementals(vectors, momenta, table, far, near):
    _, colours, sites, columns = vectors.shape
    angles = np.arange(128, dtype=np.float32) * np.float32(2.0 * math.pi / LS)
    trig = jnp.asarray(np.stack([np.cos(angles), np.sin(angles)] * 4).astype(np.float32))
    shape = (2, columns, columns)
    momenta, table = in_hbm(momenta), in_hbm(table)
    small = [pltpu.SMEM(momenta.shape, jnp.int32), pltpu.SMEM(table.shape, jnp.int32)]
    params = pltpu.CompilerParams(vmem_limit_bytes=LIMIT)
    wave = (2, sites, columns)
    *first, vecs, left, waves = pl.pallas_call(
        functools.partial(gram_first, far, near),
        out_shape=[jax.ShapeDtypeStruct(shape, jnp.bfloat16) for _ in far]
        + [
            jax.ShapeDtypeStruct(vectors.shape, vectors.dtype),
            jax.ShapeDtypeStruct((2 * columns, colours * sites), vectors.dtype),
            jax.ShapeDtypeStruct((len(near),) + wave, jnp.float32),
        ],
        in_specs=[HBM] * 4,
        out_specs=[VMEM] * (len(far) + 3),
        scratch_shapes=[
            pltpu.VMEM((len(far),) + wave, jnp.float32),
            pltpu.VMEM(trig.shape, trig.dtype),
            *small,
            pltpu.SemaphoreType.DMA((4,)),
        ],
        compiler_params=params,
        cost_estimate=gram_cost(len(far), vectors),
        name="gram_far",
    )(in_hbm(vectors), momenta, table, in_hbm(trig))
    second = pl.pallas_call(
        gram_second,
        out_shape=[
            jax.ShapeDtypeStruct(shape, jnp.float32 if k == 0 else jnp.bfloat16) for k in near
        ],
        in_specs=[VMEM] * 3,
        out_specs=[VMEM] * len(near),
        compiler_params=params,
        cost_estimate=gram_cost(len(near), vectors),
        name="gram_near",
    )(vecs, left, waves)
    return dict(zip(far + near, first + list(second)))


def slot_of(masks):
    me = lax.axis_index("tm")
    return me ^ jnp.where(me & 1 == 1, masks[1], masks[0])


def mix_kernel(masks, sink, peramb, table, labels, out, units, times, sems):
    load_units = pltpu.make_async_copy(table, units, sems.at[0])
    load_times = pltpu.make_async_copy(labels, times, sems.at[1])
    load_units.start()
    load_times.start()
    real = sink[0]
    imag = sink[1]
    columns = real.shape[0]
    left = jnp.concatenate(
        [jnp.concatenate([real, -imag], axis=1), jnp.concatenate([imag, real], axis=1)], axis=0
    )
    load_units.wait()
    load_times.wait()
    turns = units[1, lax.axis_index("space")]
    odd = lax.rem(turns, 2)
    phase_real = ((1 - odd) * (1 - turns)).astype(jnp.float32)
    phase_imag = (odd * (2 - turns)).astype(jnp.float32)
    me = lax.axis_index("tm")
    own = times[me]
    for k in range(peramb.shape[0]):
        n = slot_of(masks[k])
        sign = jnp.where(times[n] > own, -1.0, 1.0).astype(jnp.float32)
        right = jnp.concatenate([peramb[n, 0], peramb[n, 1]], axis=0)
        mixed = jnp.dot(left, right, preferred_element_type=jnp.float32)
        mixed_real = mixed[:columns]
        mixed_imag = mixed[columns:]
        turn_real = sign * phase_real
        turn_imag = sign * phase_imag
        out[k, :, pl.ds(0, columns)] = (turn_real * mixed_real - turn_imag * mixed_imag).astype(
            out.dtype
        )
        out[k, :, pl.ds(columns, columns)] = (
            turn_real * mixed_imag + turn_imag * mixed_real
        ).astype(out.dtype)


def mix(sink, peramb, table, labels, masks):
    slots, _, columns, _ = peramb.shape
    return pl.pallas_call(
        functools.partial(mix_kernel, masks),
        out_shape=jax.ShapeDtypeStruct((slots, columns, 2 * columns), jnp.bfloat16),
        in_specs=[VMEM, VMEM, HBM, HBM],
        out_specs=VMEM,
        scratch_shapes=[
            pltpu.SMEM(table.shape, jnp.int32),
            pltpu.SMEM(labels.shape, jnp.int32),
            pltpu.SemaphoreType.DMA((2,)),
        ],
        compiler_params=pltpu.CompilerParams(vmem_limit_bytes=LIMIT),
        cost_estimate=pl.CostEstimate(
            flops=slots * 8 * columns**3, bytes_accessed=slots * 8 * columns**2, transcendentals=0
        ),
        name="mix",
    )(sink, peramb, in_hbm(table), in_hbm(labels))


def close_kernel(ks, masks, before, mixed, *rest):
    sources = rest[: len(ks)]
    out, blocks, sems = rest[len(ks) + before :]
    columns = sources[0].shape[-1]
    stores = []
    for i, (source, k) in enumerate(zip(sources, ks)):
        real = source[0]
        imag = source[1]
        right = jnp.concatenate(
            [jnp.concatenate([real, imag], axis=1), jnp.concatenate([-imag, real], axis=1)], axis=0
        )
        block = lax.dot_general(
            mixed[k], right, (((1,), (1,)), ((), ())), preferred_element_type=jnp.float32
        )
        blocks[i, 0] = block[:, :columns].astype(out.dtype)
        blocks[i, 1] = block[:, columns:].astype(out.dtype)
        store = pltpu.make_async_copy(blocks.at[i], out.at[slot_of(masks[k])], sems.at[i])
        store.start()
        stores.append(store)
    for store in stores:
        store.wait()


def close(mixed, sources, ks, masks, out=None):
    slots, columns, _ = mixed.shape
    before = [] if out is None else [out]
    shape = (slots, 2, columns, columns)
    return pl.pallas_call(
        functools.partial(close_kernel, ks, masks, len(before)),
        out_shape=jax.ShapeDtypeStruct(shape, jnp.bfloat16),
        in_specs=[VMEM] * (1 + len(ks)) + [HBM] * len(before),
        out_specs=HBM,
        scratch_shapes=[
            pltpu.VMEM((len(ks),) + shape[1:], jnp.bfloat16),
            pltpu.SemaphoreType.DMA((len(ks),)),
        ],
        input_output_aliases={1 + len(ks): 0} if before else {},
        compiler_params=pltpu.CompilerParams(vmem_limit_bytes=LIMIT),
        cost_estimate=pl.CostEstimate(
            flops=len(ks) * 8 * columns**3,
            bytes_accessed=len(ks) * 12 * columns**2,
            transcendentals=0,
        ),
        name="close",
    )(mixed, *[sources[k] for k in ks], *before)


def sum_order(space):
    shifts = list(range(1, space))
    return shifts, space // 2


def hop_order(times):
    return [(k, k) for k in range(times - 2, 0, -2)]


def body(space, times, evecs, peramb, momenta, unit_table, time_labels):
    table = unit_table.T
    shifts, far = sum_order(space)
    partials = partial_elementals(evecs[0], momenta, table, shifts[:far], shifts[far:] + [0])
    total = partials[0]
    for shift in shifts:
        pairs = along(space, shift)
        total = total + lax.ppermute(partials[shift], "space", pairs).astype(jnp.float32)
    sink = total.astype(jnp.bfloat16)
    hops = hop_order(times)
    masks = [(0, 0), (1, 1)]
    for even, odd in hops:
        masks += [(even, odd), (odd ^ 1, even ^ 1)]
    sources = {0: sink}
    for i in range(1, len(hops) + 1):
        even, odd = masks[2 * i]
        pairs = [(a, a ^ (odd if a & 1 else even)) for a in range(times)]
        sources[2 * i] = lax.ppermute(sink, "tm", pairs)
    mixed = mix(sink, peramb[0, 0], table, time_labels, masks)
    for i in range(len(hops) + 1):
        pairs = [(a, a ^ 1) for a in range(times)]
        sources[2 * i + 1] = lax.ppermute(sources[2 * i], "tm", pairs)
    out = close(mixed, sources, list(range(times - LATE)), masks)
    return close(mixed, sources, list(range(times - LATE, times)), masks, out)[None, None]


def solution(mesh):
    space, times = mesh.shape["space"], mesh.shape["tm"]
    return jax.shard_map(
        functools.partial(body, space, times),
        mesh=mesh,
        in_specs=(
            P("tm", None, None, "space", None),
            P("tm", "space", None, None, None, None),
            P(),
            P(),
            P(),
        ),
        out_specs=P("tm", "space", None, None, None, None),
        check_vma=False,
    )
```

time: 25.9 us -> 24 us (0.927)
  waiting for transfers between devices: 10.2 us -> 7.83 us
  starting transfers between devices: 9.72 us -> 10.7 us
  Pallas kernels: 5.68 us -> 5.17 us
    ppermute x3, waiting for transfers between devices: 6.44 us -> 4.05 us  [body(): lax.ppermute(partials[shift], 'space', pairs).astype(jnp.float32)]
    ppermute x3, starting transfers between devices: 6.14 us -> 7.16 us  [body(): lax.ppermute(partials[shift], 'space', pairs).astype(jnp.float32)]
    pallas_call x1, Pallas kernels: 0.75 us -> 0.41 us  [partial_elementals(): pl.pallas_call(gram_second, out_shape=[jax.ShapeDtypeStruct(shape, jnp.fl...]
  transfers between devices with their start and end apart: 10 -> 10, of which waited for: 6 -> 4; matrix products, arithmetic and copies ran while one was open for 0% -> 0% of each run, Pallas kernels for 8% -> 9%
where the time goes in v4:
time: 24 us; the launch traced here: 23.8 us
  starting transfers between devices  10.7 us (45%)
  waiting for transfers between devices  7.83 us (33%)
  Pallas kernels  5.17 us (22%)
    ppermute x3, starting transfers between devices, body(): lax.ppermute(partials[shift], 'space', pairs).astype(jnp.float32)  7.16 us
    ppermute x3, waiting for transfers between devices, body(): lax.ppermute(partials[shift], 'space', pairs).astype(jnp.float32)  4.05 us
    ppermute x3, waiting for transfers between devices, body(): sources[2 * i] = lax.ppermute(sink, 'tm', pairs)  3.77 us
    ppermute x3, starting transfers between devices, body(): sources[2 * i] = lax.ppermute(sink, 'tm', pairs)  3.55 us
    pallas_call x2, Pallas kernels, close(): pl.pallas_call(functools.partial(close_kernel, ks, masks, len(before)), o...  1.99 us
    pallas_call x1, Pallas kernels, partial_elementals(): pl.pallas_call(functools.partial(gram_first, far, near), out_shape=[jax.S...  1.61 us
    pallas_call x1, Pallas kernels, mix(): pl.pallas_call(functools.partial(mix_kernel, masks), out_shape=jax.ShapeD...  1.15 us
  transfers between devices with their start and end apart: 10, of which 4 were waited for; matrix products, arithmetic and copies ran while one was open for 0% of the time, Pallas kernels for 9%

profile of v4, /device:TPU:0, one launch (start us, length us, event | category | flops | bytes accessed | tf_op | source)
XLA Modules:
  0.0 23.8 jit_solution(4803120048693935886)
XLA Ops:
  0.0 1.6 %gram_far.1 = (bf16[2,128,128]{2,1,0:T(8,128)(2,1)S(1)}, bf16[2,128,128]{2,1,0:T(8,128)(2,1)S(1)}, bf16[2,3,256,128]{3,2,1,0:T(8,128)(2,1)S(1)}, bf16[256,768]{1,0:T(8,128)(2,1)S(1)}, f32[2,2,256,128]{3,2,1,0:T(8,128)S(1)}) custom-call(bf16[2,3,256,128]{3,2,1,0:T(8,128)(2,1)} %bitcast.7, s32[4,3]{1,0:T(4,128)} %momenta.1, s32[2,4]{1,0:T(2,128)} %bitcast.5, ...), custom_call_target="tpu_custom_call" | custom-call | flops 402653184 | bytes 524288 | tf_op jit(solution)/shard_map/gram_far/pallas_call | solution.py:184
  1.6 0.0 copy-start
  1.6 0.4 %gram_near.1 = (bf16[2,128,128]{2,1,0:T(8,128)(2,1)S(1)}, f32[2,128,128]{2,1,0:T(8,128)S(1)}) custom-call(bf16[2,3,256,128]{3,2,1,0:T(8,128)(2,1)S(1)} %get-tuple-element.12.vecs, bf16[256,768]{1,0:T(8,128)(2,1)S(1)} %get-tuple-element.13.left, f32[2,2,256,128]{3,2,1,0:T(8,128)S(1)} %get-tuple-element.14.waves), custom_call_target="tpu_custom_call" | custom-call | flops 402653184 | bytes 524288 | tf_op jit(solution)/shard_map/gram_near/pallas_call | solution.py:204
  2.1 4.1 %collective-permute-start.2 = (bf16[2,128,128]{2,1,0:T(8,128)(2,1)S(1)}, bf16[2,128,128]{2,1,0:T(8,128)(2,1)S(1)}, u32[]{:S(2)}, u32[]{:S(2)}) collective-permute-start(bf16[2,128,128]{2,1,0:T(8,128)(2,1)S(1)} %get-tuple-element.18), channel_id=1, source_target_pairs={{0,2},{1,0},{3,1},{2,3},{4,6},{5,4},{7,5},{6,7},{8,10},{9,8},{11,9... | collective-permute-start | bytes 196616 | tf_op jit(solution)/shard_map/ppermute | solution.py:342
  6.2 0.0 collective-permute-start
  6.2 3.0 %collective-permute-start.1 = (bf16[2,128,128]{2,1,0:T(8,128)(2,1)S(1)}, bf16[2,128,128]{2,1,0:T(8,128)(2,1)S(1)}, u32[]{:S(2)}, u32[]{:S(2)}) collective-permute-start(bf16[2,128,128]{2,1,0:T(8,128)(2,1)S(1)} %get-tuple-element.17), channel_id=1, source_target_pairs={{0,3},{1,2},{3,0},{2,1},{4,7},{5,6},{7,4},{6,5},{8,11},{9,10},{11,... | collective-permute-start | bytes 196616 | tf_op jit(solution)/shard_map/ppermute | solution.py:342
  9.2 0.0 collective-permute-done.2
  9.2 4.0 %collective-permute-done = bf16[2,128,128]{2,1,0:T(8,128)(2,1)S(1)} collective-permute-done((bf16[2,128,128]{2,1,0:T(8,128)(2,1)S(1)}, bf16[2,128,128]{2,1,0:T(8,128)(2,1)S(1)}, u32[]{:S(2)}, u32[]{:S(2)}) %collective-permute-start) | collective-permute-done | bytes 65568 | tf_op jit(solution)/shard_map/ppermute | solution.py:342
  13.3 0.0 collective-permute-done.1
  13.3 2.5 %collective-permute-start.8 = (bf16[2,128,128]{2,1,0:T(8,128)(2,1)S(1)}, bf16[2,128,128]{2,1,0:T(8,128)(2,1)S(1)}, u32[]{:S(2)}, u32[]{:S(2)}) collective-permute-start(bf16[2,128,128]{2,1,0:T(8,128)(2,1)S(1)} %add_convert_fusion.sink.rest_0_), channel_id=1, source_target_pairs={{0,24},{4,28},{8,16},{12,20},{16,8},{20,12},{24,0},{28,4},{1,25},{... | collective-permute-start | bytes 196616 | tf_op jit(solution)/shard_map/ppermute | solution.py:352
  15.8 0.5 %collective-permute-start.5 = (bf16[2,128,128]{2,1,0:T(8,128)(2,1)S(1)}, bf16[2,128,128]{2,1,0:T(8,128)(2,1)S(1)}, u32[]{:S(2)}, u32[]{:S(2)}) collective-permute-start(bf16[2,128,128]{2,1,0:T(8,128)(2,1)S(1)} %add_convert_fusion.sink.rest_0_), channel_id=1, source_target_pairs={{0,8},{4,12},{8,0},{12,4},{16,24},{20,28},{24,16},{28,20},{1,9},{5... | collective-permute-start | bytes 196616 | tf_op jit(solution)/shard_map/ppermute | solution.py:352
  16.4 0.5 %collective-permute-start.3 = (bf16[2,128,128]{2,1,0:T(8,128)(2,1)S(1)}, bf16[2,128,128]{2,1,0:T(8,128)(2,1)S(1)}, u32[]{:S(2)}, u32[]{:S(2)}) collective-permute-start(bf16[2,128,128]{2,1,0:T(8,128)(2,1)S(1)} %add_convert_fusion.sink.rest_0_), channel_id=1, source_target_pairs={{0,16},{4,20},{8,24},{12,28},{16,0},{20,4},{24,8},{28,12},{1,17},{... | collective-permute-start | bytes 196616 | tf_op jit(solution)/shard_map/ppermute | solution.py:352
  16.9 0.0 collective-permute-start.7
  16.9 1.7 %collective-permute-done.8.rest_2_ = bf16[2,128,128]{2,1,0:T(8,128)(2,1)S(1)} collective-permute-done((bf16[2,128,128]{2,1,0:T(8,128)(2,1)S(1)}, bf16[2,128,128]{2,1,0:T(8,128)(2,1)S(1)}, u32[]{:S(2)}, u32[]{:S(2)}) %collective-permute-start.8) | collective-permute-done | bytes 65568 | tf_op jit(solution)/shard_map/ppermute | solution.py:352
  18.5 0.0 collective-permute-start.9
  18.5 1.6 %collective-permute-done.5.rest_2_ = bf16[2,128,128]{2,1,0:T(8,128)(2,1)S(1)} collective-permute-done((bf16[2,128,128]{2,1,0:T(8,128)(2,1)S(1)}, bf16[2,128,128]{2,1,0:T(8,128)(2,1)S(1)}, u32[]{:S(2)}, u32[]{:S(2)}) %collective-permute-start.5) | collective-permute-done | bytes 65568 | tf_op jit(solution)/shard_map/ppermute | solution.py:352
  20.1 0.0 collective-permute-start.6
  20.1 0.5 %collective-permute-done.3.rest_0_ = bf16[2,128,128]{2,1,0:T(8,128)(2,1)S(1)} collective-permute-done((bf16[2,128,128]{2,1,0:T(8,128)(2,1)S(1)}, bf16[2,128,128]{2,1,0:T(8,128)(2,1)S(1)}, u32[]{:S(2)}, u32[]{:S(2)}) %collective-permute-start.3) | collective-permute-done | bytes 65568 | tf_op jit(solution)/shard_map/ppermute | solution.py:352
  20.6 0.0 collective-permute-start.4
  20.6 0.0 copy-done
  20.6 1.2 %mix.1.mixed = bf16[8,128,256]{2,1,0:T(8,128)(2,1)S(1)} custom-call(bf16[2,128,128]{2,1,0:T(8,128)(2,1)S(1)} %add_convert_fusion.sink.rest_0_, bf16[8,2,128,128]{3,2,1,0:T(8,128)(2,1)S(1)} %bitcast.4, s32[2,4]{1,0:T(2,128)} %bitcast.6, s32[8]{0:T(128)} %labels.1), custom_call_target="tpu_custom_call" | custom-call | flops 134217728 | bytes 1048576 | tf_op jit(solution)/shard_map/mix/pallas_call | solution.py:261
  21.8 0.0 collective-permute-done.7.rest_1_
  21.8 0.0 collective-permute-done.9.rest_3_
  21.8 1.0 %close.2.rest_4_ = bf16[8,2,128,128]{3,2,1,0:T(8,128)(2,1)} custom-call(bf16[8,128,256]{2,1,0:T(8,128)(2,1)S(1)} %mix.1.mixed, bf16[2,128,128]{2,1,0:T(8,128)(2,1)S(1)} %add_convert_fusion.sink.rest_0_, bf16[2,128,128]{2,1,0:T(8,128)(2,1)S(1)} %collective-permute-done.7.rest_1_, bf16[2,128,128]{2,1,0:T(8,128)(2,1)S(1)} %collective-permute-done.8.rest_2_, ...), custom_call_target="tpu_custom_call" | custom-call | flops 67108864 | bytes 786432 | tf_op jit(solution)/shard_map/close/pallas_call | solution.py:306
  22.8 0.0 collective-permute-done.6.rest_3_
  22.8 0.0 collective-permute-done.4.rest_1_
  22.8 1.0 %close.3 = bf16[8,2,128,128]{3,2,1,0:T(8,128)(2,1)} custom-call(bf16[8,128,256]{2,1,0:T(8,128)(2,1)S(1)} %mix.1.mixed, bf16[2,128,128]{2,1,0:T(8,128)(2,1)S(1)} %collective-permute-done.3.rest_0_, bf16[2,128,128]{2,1,0:T(8,128)(2,1)S(1)} %collective-permute-done.4.rest_1_, ...), custom_call_target="tpu_custom_call", output_to_operand_aliasing={{}: (5, {})} | custom-call | flops 67108864 | bytes 786432 | tf_op jit(solution)/shard_map/close/pallas_call | solution.py:306
  (1 shorter events, 0.0 us)
Async XLA Ops:
  1.6 19.0 %copy-start = (bf16[1,1,8,2,128,128]{5,4,3,2,1,0:T(8,128)(2,1)S(1)}, bf16[1,1,8,2,128,128]{5,4,3,2,1,0:T(8,128)(2,1)}, u32[]{:S(2)}) copy-start(bf16[1,1,8,2,128,128]{5,4,3,2,1,0:T(8,128)(2,1)} %param.7) | copy-start | bytes 1572868
  2.1 7.2 %collective-permute-start.2 = (bf16[2,128,128]{2,1,0:T(8,128)(2,1)S(1)}, bf16[2,128,128]{2,1,0:T(8,128)(2,1)S(1)}, u32[]{:S(2)}, u32[]{:S(2)}) collective-permute-start(bf16[2,128,128]{2,1,0:T(8,128)(2,1)S(1)} %get-tuple-element.18), channel_id=1, source_target_pairs={{0,2},{1,0},{3,1},{2,3},{4,6},{5,4},{7,5},{6,7},{8,10},{9,8},{11,9... | collective-permute-start | bytes 196616 | tf_op jit(solution)/shard_map/ppermute | solution.py:342
  6.2 7.1 %collective-permute-start = (bf16[2,128,128]{2,1,0:T(8,128)(2,1)S(1)}, bf16[2,128,128]{2,1,0:T(8,128)(2,1)S(1)}, u32[]{:S(2)}, u32[]{:S(2)}) collective-permute-start(bf16[2,128,128]{2,1,0:T(8,128)(2,1)S(1)} %get-tuple-element.16), channel_id=1, source_target_pairs={{0,1},{1,3},{3,2},{2,0},{4,5},{5,7},{7,6},{6,4},{8,9},{9,11},{11,1... | collective-permute-start | bytes 196616 | tf_op jit(solution)/shard_map/ppermute | solution.py:342
  6.2 7.1 %collective-permute-start.1 = (bf16[2,128,128]{2,1,0:T(8,128)(2,1)S(1)}, bf16[2,128,128]{2,1,0:T(8,128)(2,1)S(1)}, u32[]{:S(2)}, u32[]{:S(2)}) collective-permute-start(bf16[2,128,128]{2,1,0:T(8,128)(2,1)S(1)} %get-tuple-element.17), channel_id=1, source_target_pairs={{0,3},{1,2},{3,0},{2,1},{4,7},{5,6},{7,4},{6,5},{8,11},{9,10},{11,... | collective-permute-start | bytes 196616 | tf_op jit(solution)/shard_map/ppermute | solution.py:342
  13.3 5.2 %collective-permute-start.8 = (bf16[2,128,128]{2,1,0:T(8,128)(2,1)S(1)}, bf16[2,128,128]{2,1,0:T(8,128)(2,1)S(1)}, u32[]{:S(2)}, u32[]{:S(2)}) collective-permute-start(bf16[2,128,128]{2,1,0:T(8,128)(2,1)S(1)} %add_convert_fusion.sink.rest_0_), channel_id=1, source_target_pairs={{0,24},{4,28},{8,16},{12,20},{16,8},{20,12},{24,0},{28,4},{1,25},{... | collective-permute-start | bytes 196616 | tf_op jit(solution)/shard_map/ppermute | solution.py:352
  15.8 4.3 %collective-permute-start.5 = (bf16[2,128,128]{2,1,0:T(8,128)(2,1)S(1)}, bf16[2,128,128]{2,1,0:T(8,128)(2,1)S(1)}, u32[]{:S(2)}, u32[]{:S(2)}) collective-permute-start(bf16[2,128,128]{2,1,0:T(8,128)(2,1)S(1)} %add_convert_fusion.sink.rest_0_), channel_id=1, source_target_pairs={{0,8},{4,12},{8,0},{12,4},{16,24},{20,28},{24,16},{28,20},{1,9},{5... | collective-permute-start | bytes 196616 | tf_op jit(solution)/shard_map/ppermute | solution.py:352
  16.4 4.3 %collective-permute-start.3 = (bf16[2,128,128]{2,1,0:T(8,128)(2,1)S(1)}, bf16[2,128,128]{2,1,0:T(8,128)(2,1)S(1)}, u32[]{:S(2)}, u32[]{:S(2)}) collective-permute-start(bf16[2,128,128]{2,1,0:T(8,128)(2,1)S(1)} %add_convert_fusion.sink.rest_0_), channel_id=1, source_target_pairs={{0,16},{4,20},{8,24},{12,28},{16,0},{20,4},{24,8},{28,12},{1,17},{... | collective-permute-start | bytes 196616 | tf_op jit(solution)/shard_map/ppermute | solution.py:352
  16.9 4.9 %collective-permute-start.7 = (bf16[2,128,128]{2,1,0:T(8,128)(2,1)S(1)}, bf16[2,128,128]{2,1,0:T(8,128)(2,1)S(1)}, u32[]{:S(2)}, u32[]{:S(2)}) collective-permute-start(bf16[2,128,128]{2,1,0:T(8,128)(2,1)S(1)} %add_convert_fusion.sink.rest_0_), channel_id=1, source_target_pairs={{0,4},{4,0},{8,12},{12,8},{16,20},{20,16},{24,28},{28,24},{1,5},{5... | collective-permute-start | bytes 196616 | tf_op jit(solution)/shard_map/ppermute | solution.py:356
  18.5 3.3 %collective-permute-start.9 = (bf16[2,128,128]{2,1,0:T(8,128)(2,1)S(1)}, bf16[2,128,128]{2,1,0:T(8,128)(2,1)S(1)}, u32[]{:S(2)}, u32[]{:S(2)}) collective-permute-start(bf16[2,128,128]{2,1,0:T(8,128)(2,1)S(1)} %collective-permute-done.8.rest_2_), channel_id=1, source_target_pairs={{0,4},{4,0},{8,12},{12,8},{16,20},{20,16},{24,28},{28,24},{1,5},{5... | collective-permute-start | bytes 196616 | tf_op jit(solution)/shard_map/ppermute | solution.py:356
  20.1 2.7 %collective-permute-start.6 = (bf16[2,128,128]{2,1,0:T(8,128)(2,1)S(1)}, bf16[2,128,128]{2,1,0:T(8,128)(2,1)S(1)}, u32[]{:S(2)}, u32[]{:S(2)}) collective-permute-start(bf16[2,128,128]{2,1,0:T(8,128)(2,1)S(1)} %collective-permute-done.5.rest_2_), channel_id=1, source_target_pairs={{0,4},{4,0},{8,12},{12,8},{16,20},{20,16},{24,28},{28,24},{1,5},{5... | collective-permute-start | bytes 196616 | tf_op jit(solution)/shard_map/ppermute | solution.py:356
  20.6 2.2 %collective-permute-start.4 = (bf16[2,128,128]{2,1,0:T(8,128)(2,1)S(1)}, bf16[2,128,128]{2,1,0:T(8,128)(2,1)S(1)}, u32[]{:S(2)}, u32[]{:S(2)}) collective-permute-start(bf16[2,128,128]{2,1,0:T(8,128)(2,1)S(1)} %collective-permute-done.3.rest_0_), channel_id=1, source_target_pairs={{0,4},{4,0},{8,12},{12,8},{16,20},{20,16},{24,28},{28,24},{1,5},{5... | collective-permute-start | bytes 196616 | tf_op jit(solution)/shard_map/ppermute | solution.py:356

commit v5 on v4

--- a/solution.py
+++ b/solution.py
@@ -11,7 +11,6 @@
 
 
 LS = 40
-LATE = 4
 LIMIT = 12 * 1024 * 1024
 VMEM = pl.BlockSpec(memory_space=pltpu.VMEM)
 HBM = pl.BlockSpec(memory_space=pltpu.HBM)
@@ -126,7 +125,8 @@
 
 def gram_first(far, near, evecs, momenta, table, trig_in, *rest):
     outs = rest[: len(far)]
-    vecs, left, waves, own, trig, moments, units, sems = rest[len(far) :]
+    early = rest[len(far) : len(far) + len(near)]
+    vecs, left, waves, own, trig, moments, units, sems = rest[len(far) + len(near) :]
     _, colours, sites, columns = vecs.shape
     small = [
         pltpu.make_async_copy(source, target, sems.at[i])
@@ -157,10 +157,28 @@
             totals[i] = sum(gram(vecs, left, own.at[i], colour) for colour in range(colours))
         keep(out, totals[i])
 
-
-def gram_second(vecs, left, waves, *outs):
+    @pl.when(lax.axis_index("space") == 0)
+    def _():
+        gram_near(vecs, left, waves, early)
+
+
+def gram_near(vecs, left, waves, outs):
     for i, out in enumerate(outs):
         keep(out, sum(gram(vecs, left, waves.at[i], colour) for colour in range(vecs.shape[1])))
+
+
+def gram_second(vecs, left, waves, *rest):
+    early = rest[: len(rest) // 2]
+    outs = rest[len(rest) // 2 :]
+
+    @pl.when(lax.axis_index("space") == 0)
+    def _():
+        for out, value in zip(outs, early):
+            out[...] = value[...]
+
+    @pl.when(lax.axis_index("space") != 0)
+    def _():
+        gram_near(vecs, left, waves, outs)
 
 
 def gram_cost(count, vectors):
@@ -181,16 +199,20 @@
     small = [pltpu.SMEM(momenta.shape, jnp.int32), pltpu.SMEM(table.shape, jnp.int32)]
     params = pltpu.CompilerParams(vmem_limit_bytes=LIMIT)
     wave = (2, sites, columns)
+    near_shape = [
+        jax.ShapeDtypeStruct(shape, jnp.float32 if k == 0 else jnp.bfloat16) for k in near
+    ]
     *first, vecs, left, waves = pl.pallas_call(
         functools.partial(gram_first, far, near),
         out_shape=[jax.ShapeDtypeStruct(shape, jnp.bfloat16) for _ in far]
+        + near_shape
         + [
             jax.ShapeDtypeStruct(vectors.shape, vectors.dtype),
             jax.ShapeDtypeStruct((2 * columns, colours * sites), vectors.dtype),
             jax.ShapeDtypeStruct((len(near),) + wave, jnp.float32),
         ],
         in_specs=[HBM] * 4,
-        out_specs=[VMEM] * (len(far) + 3),
+        out_specs=[VMEM] * (len(far) + len(near) + 3),
         scratch_shapes=[
             pltpu.VMEM((len(far),) + wave, jnp.float32),
             pltpu.VMEM(trig.shape, trig.dtype),
@@ -203,16 +225,14 @@
     )(in_hbm(vectors), momenta, table, in_hbm(trig))
     second = pl.pallas_call(
         gram_second,
-        out_shape=[
-            jax.ShapeDtypeStruct(shape, jnp.float32 if k == 0 else jnp.bfloat16) for k in near
-        ],
-        in_specs=[VMEM] * 3,
+        out_shape=near_shape,
+        in_specs=[VMEM] * (3 + len(near)),
         out_specs=[VMEM] * len(near),
         compiler_params=params,
         cost_estimate=gram_cost(len(near), vectors),
         name="gram_near",
-    )(vecs, left, waves)
-    return dict(zip(far + near, first + list(second)))
+    )(vecs, left, waves, *first[len(far) :])
+    return dict(zip(far + near, first[: len(far)] + list(second)))
 
 
 def slot_of(masks):
@@ -354,8 +374,10 @@
     for i in range(len(hops) + 1):
         pairs = [(a, a ^ 1) for a in range(times)]
         sources[2 * i + 1] = lax.ppermute(sources[2 * i], "tm", pairs)
-    out = close(mixed, sources, list(range(times - LATE)), masks)
-    return close(mixed, sources, list(range(times - LATE, times)), masks, out)[None, None]
+    late = [times - 3, times - 1]
+    early = [k for k in range(times) if k not in late]
+    out = close(mixed, sources, early, masks)
+    return close(mixed, sources, late, masks, out)[None, None]
 
 
 def solution(mesh):

time: 24 us -> 24 us (level)
    pallas_call x1, Pallas kernels: 1.61 us -> 2.03 us  [partial_elementals(): pl.pallas_call(functools.partial(gram_first, far, near), out_shape=[jax.S...]
    pallas_call x1, Pallas kernels: 0.41 us -> 0.03 us  [partial_elementals(): pl.pallas_call(gram_second, out_shape=near_shape, in_specs=[VMEM] * (3 +...]
where the time goes in v5:
time: 24 us; the launch traced here: 23.9 us
  starting transfers between devices  10.7 us (45%)
  waiting for transfers between devices  7.82 us (33%)
  Pallas kernels  5.21 us (22%)
    ppermute x3, starting transfers between devices, body(): lax.ppermute(partials[shift], 'space', pairs).astype(jnp.float32)  7.14 us
    ppermute x3, waiting for transfers between devices, body(): lax.ppermute(partials[shift], 'space', pairs).astype(jnp.float32)  4.05 us
    ppermute x3, waiting for transfers between devices, body(): sources[2 * i] = lax.ppermute(sink, 'tm', pairs)  3.76 us
    ppermute x3, starting transfers between devices, body(): sources[2 * i] = lax.ppermute(sink, 'tm', pairs)  3.55 us
    pallas_call x1, Pallas kernels, partial_elementals(): pl.pallas_call(functools.partial(gram_first, far, near), out_shape=[jax.S...  2.03 us
    pallas_call x2, Pallas kernels, close(): pl.pallas_call(functools.partial(close_kernel, ks, masks, len(before)), o...  2 us
    pallas_call x1, Pallas kernels, mix(): pl.pallas_call(functools.partial(mix_kernel, masks), out_shape=jax.ShapeD...  1.15 us
  transfers between devices with their start and end apart: 10, of which 4 were waited for; matrix products, arithmetic and copies ran while one was open for 0% of the time, Pallas kernels for 9%

profile of v5, /device:TPU:0, one launch (start us, length us, event | category | flops | bytes accessed | tf_op | source)
XLA Modules:
  0.0 23.9 jit_solution(4762892217545678370)
XLA Ops:
  0.0 2.0 %gram_far.1 = (bf16[2,128,128]{2,1,0:T(8,128)(2,1)S(1)}, bf16[2,128,128]{2,1,0:T(8,128)(2,1)S(1)}, bf16[2,128,128]{2,1,0:T(8,128)(2,1)S(1)}, f32[2,128,128]{2,1,...) custom-call(bf16[2,3,256,128]{3,2,1,0:T(8,128)(2,1)} %bitcast.7, ...), custom_call_target="tpu_custom_call" | custom-call | flops 402653184 | bytes 524288 | tf_op jit(solution)/shard_map/gram_far/pallas_call | solution.py:205
  2.0 0.0 copy-start
  2.1 4.1 %collective-permute-start.2 = (bf16[2,128,128]{2,1,0:T(8,128)(2,1)S(1)}, bf16[2,128,128]{2,1,0:T(8,128)(2,1)S(1)}, u32[]{:S(2)}, u32[]{:S(2)}) collective-permute-start(bf16[2,128,128]{2,1,0:T(8,128)(2,1)S(1)} %get-tuple-element.22), channel_id=1, source_target_pairs={{0,2},{1,0},{3,1},{2,3},{4,6},{5,4},{7,5},{6,7},{8,10},{9,8},{11,9... | collective-permute-start | bytes 196616 | tf_op jit(solution)/shard_map/ppermute | solution.py:362
  6.2 0.0 collective-permute-start
  6.2 3.0 %collective-permute-start.1 = (bf16[2,128,128]{2,1,0:T(8,128)(2,1)S(1)}, bf16[2,128,128]{2,1,0:T(8,128)(2,1)S(1)}, u32[]{:S(2)}, u32[]{:S(2)}) collective-permute-start(bf16[2,128,128]{2,1,0:T(8,128)(2,1)S(1)} %get-tuple-element.21), channel_id=1, source_target_pairs={{0,3},{1,2},{3,0},{2,1},{4,7},{5,6},{7,4},{6,5},{8,11},{9,10},{11,... | collective-permute-start | bytes 196616 | tf_op jit(solution)/shard_map/ppermute | solution.py:362
  9.2 0.0 collective-permute-done.2
  9.2 4.0 %collective-permute-done = bf16[2,128,128]{2,1,0:T(8,128)(2,1)S(1)} collective-permute-done((bf16[2,128,128]{2,1,0:T(8,128)(2,1)S(1)}, bf16[2,128,128]{2,1,0:T(8,128)(2,1)S(1)}, u32[]{:S(2)}, u32[]{:S(2)}) %collective-permute-start) | collective-permute-done | bytes 65568 | tf_op jit(solution)/shard_map/ppermute | solution.py:362
  13.3 0.0 collective-permute-done.1
  13.3 2.5 %collective-permute-start.8 = (bf16[2,128,128]{2,1,0:T(8,128)(2,1)S(1)}, bf16[2,128,128]{2,1,0:T(8,128)(2,1)S(1)}, u32[]{:S(2)}, u32[]{:S(2)}) collective-permute-start(bf16[2,128,128]{2,1,0:T(8,128)(2,1)S(1)} %add_convert_fusion.sink.rest_0_), channel_id=1, source_target_pairs={{0,24},{4,28},{8,16},{12,20},{16,8},{20,12},{24,0},{28,4},{1,25},{... | collective-permute-start | bytes 196616 | tf_op jit(solution)/shard_map/ppermute | solution.py:372
  15.8 0.5 %collective-permute-start.5 = (bf16[2,128,128]{2,1,0:T(8,128)(2,1)S(1)}, bf16[2,128,128]{2,1,0:T(8,128)(2,1)S(1)}, u32[]{:S(2)}, u32[]{:S(2)}) collective-permute-start(bf16[2,128,128]{2,1,0:T(8,128)(2,1)S(1)} %add_convert_fusion.sink.rest_0_), channel_id=1, source_target_pairs={{0,8},{4,12},{8,0},{12,4},{16,24},{20,28},{24,16},{28,20},{1,9},{5... | collective-permute-start | bytes 196616 | tf_op jit(solution)/shard_map/ppermute | solution.py:372
  16.4 0.5 %collective-permute-start.3 = (bf16[2,128,128]{2,1,0:T(8,128)(2,1)S(1)}, bf16[2,128,128]{2,1,0:T(8,128)(2,1)S(1)}, u32[]{:S(2)}, u32[]{:S(2)}) collective-permute-start(bf16[2,128,128]{2,1,0:T(8,128)(2,1)S(1)} %add_convert_fusion.sink.rest_0_), channel_id=1, source_target_pairs={{0,16},{4,20},{8,24},{12,28},{16,0},{20,4},{24,8},{28,12},{1,17},{... | collective-permute-start | bytes 196616 | tf_op jit(solution)/shard_map/ppermute | solution.py:372
  16.9 0.0 collective-permute-start.7
  16.9 1.7 %collective-permute-done.8.rest_2_ = bf16[2,128,128]{2,1,0:T(8,128)(2,1)S(1)} collective-permute-done((bf16[2,128,128]{2,1,0:T(8,128)(2,1)S(1)}, bf16[2,128,128]{2,1,0:T(8,128)(2,1)S(1)}, u32[]{:S(2)}, u32[]{:S(2)}) %collective-permute-start.8) | collective-permute-done | bytes 65568 | tf_op jit(solution)/shard_map/ppermute | solution.py:372
  18.5 0.0 collective-permute-start.9
  18.6 1.6 %collective-permute-done.5.rest_5_ = bf16[2,128,128]{2,1,0:T(8,128)(2,1)S(1)} collective-permute-done((bf16[2,128,128]{2,1,0:T(8,128)(2,1)S(1)}, bf16[2,128,128]{2,1,0:T(8,128)(2,1)S(1)}, u32[]{:S(2)}, u32[]{:S(2)}) %collective-permute-start.5) | collective-permute-done | bytes 65568 | tf_op jit(solution)/shard_map/ppermute | solution.py:372
  20.1 0.0 collective-permute-start.6
  20.1 0.5 %collective-permute-done.3.rest_4_ = bf16[2,128,128]{2,1,0:T(8,128)(2,1)S(1)} collective-permute-done((bf16[2,128,128]{2,1,0:T(8,128)(2,1)S(1)}, bf16[2,128,128]{2,1,0:T(8,128)(2,1)S(1)}, u32[]{:S(2)}, u32[]{:S(2)}) %collective-permute-start.3) | collective-permute-done | bytes 65568 | tf_op jit(solution)/shard_map/ppermute | solution.py:372
  20.6 0.0 collective-permute-start.4
  20.6 0.0 copy-done
  20.6 1.2 %mix.1.mixed = bf16[8,128,256]{2,1,0:T(8,128)(2,1)S(1)} custom-call(bf16[2,128,128]{2,1,0:T(8,128)(2,1)S(1)} %add_convert_fusion.sink.rest_0_, bf16[8,2,128,128]{3,2,1,0:T(8,128)(2,1)S(1)} %bitcast.4, s32[2,4]{1,0:T(2,128)} %bitcast.6, s32[8]{0:T(128)} %labels.1), custom_call_target="tpu_custom_call" | custom-call | flops 134217728 | bytes 1048576 | tf_op jit(solution)/shard_map/mix/pallas_call | solution.py:281
  21.8 0.0 collective-permute-done.7.rest_1_
  21.8 0.0 collective-permute-done.9.rest_3_
  21.8 1.1 %close.2.rest_2_ = bf16[8,2,128,128]{3,2,1,0:T(8,128)(2,1)} custom-call(bf16[8,128,256]{2,1,0:T(8,128)(2,1)S(1)} %mix.1.mixed, bf16[2,128,128]{2,1,0:T(8,128)(2,1)S(1)} %add_convert_fusion.sink.rest_0_, bf16[2,128,128]{2,1,0:T(8,128)(2,1)S(1)} %collective-permute-done.7.rest_1_, bf16[2,128,128]{2,1,0:T(8,128)(2,1)S(1)} %collective-permute-done.8.rest_2_, ...), custom_call_target="tpu_custom_call" | custom-call | flops 100663296 | bytes 1179648 | tf_op jit(solution)/shard_map/close/pallas_call | solution.py:326
  22.9 0.0 collective-permute-done.6.rest_1_
  22.9 0.0 collective-permute-done.4.rest_0_
  23.0 0.9 %close.3 = bf16[8,2,128,128]{3,2,1,0:T(8,128)(2,1)} custom-call(bf16[8,128,256]{2,1,0:T(8,128)(2,1)S(1)} %mix.1.mixed, bf16[2,128,128]{2,1,0:T(8,128)(2,1)S(1)} %collective-permute-done.4.rest_0_, bf16[2,128,128]{2,1,0:T(8,128)(2,1)S(1)} %collective-permute-done.6.rest_1_, bf16[8,2,128,128]{3,2,1,0:T(8,128)(2,1)} %close.2.rest_2_), custom_call_target="tpu_custom_call", output_to_operand_aliasing={{}: (3, {})} | custom-call | flops 33554432 | bytes 393216 | tf_op jit(solution)/shard_map/close/pallas_call | solution.py:326
  (2 shorter events, 0.1 us)
Async XLA Ops:
  2.0 18.6 %copy-start = (bf16[1,1,8,2,128,128]{5,4,3,2,1,0:T(8,128)(2,1)S(1)}, bf16[1,1,8,2,128,128]{5,4,3,2,1,0:T(8,128)(2,1)}, u32[]{:S(2)}) copy-start(bf16[1,1,8,2,128,128]{5,4,3,2,1,0:T(8,128)(2,1)} %param.7) | copy-start | bytes 1572868
  2.1 7.1 %collective-permute-start.2 = (bf16[2,128,128]{2,1,0:T(8,128)(2,1)S(1)}, bf16[2,128,128]{2,1,0:T(8,128)(2,1)S(1)}, u32[]{:S(2)}, u32[]{:S(2)}) collective-permute-start(bf16[2,128,128]{2,1,0:T(8,128)(2,1)S(1)} %get-tuple-element.22), channel_id=1, source_target_pairs={{0,2},{1,0},{3,1},{2,3},{4,6},{5,4},{7,5},{6,7},{8,10},{9,8},{11,9... | collective-permute-start | bytes 196616 | tf_op jit(solution)/shard_map/ppermute | solution.py:362
  6.2 7.1 %collective-permute-start = (bf16[2,128,128]{2,1,0:T(8,128)(2,1)S(1)}, bf16[2,128,128]{2,1,0:T(8,128)(2,1)S(1)}, u32[]{:S(2)}, u32[]{:S(2)}) collective-permute-start(bf16[2,128,128]{2,1,0:T(8,128)(2,1)S(1)} %get-tuple-element.20), channel_id=1, source_target_pairs={{0,1},{1,3},{3,2},{2,0},{4,5},{5,7},{7,6},{6,4},{8,9},{9,11},{11,1... | collective-permute-start | bytes 196616 | tf_op jit(solution)/shard_map/ppermute | solution.py:362
  6.2 7.1 %collective-permute-start.1 = (bf16[2,128,128]{2,1,0:T(8,128)(2,1)S(1)}, bf16[2,128,128]{2,1,0:T(8,128)(2,1)S(1)}, u32[]{:S(2)}, u32[]{:S(2)}) collective-permute-start(bf16[2,128,128]{2,1,0:T(8,128)(2,1)S(1)} %get-tuple-element.21), channel_id=1, source_target_pairs={{0,3},{1,2},{3,0},{2,1},{4,7},{5,6},{7,4},{6,5},{8,11},{9,10},{11,... | collective-permute-start | bytes 196616 | tf_op jit(solution)/shard_map/ppermute | solution.py:362
  13.3 5.2 %collective-permute-start.8 = (bf16[2,128,128]{2,1,0:T(8,128)(2,1)S(1)}, bf16[2,128,128]{2,1,0:T(8,128)(2,1)S(1)}, u32[]{:S(2)}, u32[]{:S(2)}) collective-permute-start(bf16[2,128,128]{2,1,0:T(8,128)(2,1)S(1)} %add_convert_fusion.sink.rest_0_), channel_id=1, source_target_pairs={{0,24},{4,28},{8,16},{12,20},{16,8},{20,12},{24,0},{28,4},{1,25},{... | collective-permute-start | bytes 196616 | tf_op jit(solution)/shard_map/ppermute | solution.py:372
  15.8 4.3 %collective-permute-start.5 = (bf16[2,128,128]{2,1,0:T(8,128)(2,1)S(1)}, bf16[2,128,128]{2,1,0:T(8,128)(2,1)S(1)}, u32[]{:S(2)}, u32[]{:S(2)}) collective-permute-start(bf16[2,128,128]{2,1,0:T(8,128)(2,1)S(1)} %add_convert_fusion.sink.rest_0_), channel_id=1, source_target_pairs={{0,8},{4,12},{8,0},{12,4},{16,24},{20,28},{24,16},{28,20},{1,9},{5... | collective-permute-start | bytes 196616 | tf_op jit(solution)/shard_map/ppermute | solution.py:372
  16.4 4.3 %collective-permute-start.3 = (bf16[2,128,128]{2,1,0:T(8,128)(2,1)S(1)}, bf16[2,128,128]{2,1,0:T(8,128)(2,1)S(1)}, u32[]{:S(2)}, u32[]{:S(2)}) collective-permute-start(bf16[2,128,128]{2,1,0:T(8,128)(2,1)S(1)} %add_convert_fusion.sink.rest_0_), channel_id=1, source_target_pairs={{0,16},{4,20},{8,24},{12,28},{16,0},{20,4},{24,8},{28,12},{1,17},{... | collective-permute-start | bytes 196616 | tf_op jit(solution)/shard_map/ppermute | solution.py:372
  16.9 4.9 %collective-permute-start.7 = (bf16[2,128,128]{2,1,0:T(8,128)(2,1)S(1)}, bf16[2,128,128]{2,1,0:T(8,128)(2,1)S(1)}, u32[]{:S(2)}, u32[]{:S(2)}) collective-permute-start(bf16[2,128,128]{2,1,0:T(8,128)(2,1)S(1)} %add_convert_fusion.sink.rest_0_), channel_id=1, source_target_pairs={{0,4},{4,0},{8,12},{12,8},{16,20},{20,16},{24,28},{28,24},{1,5},{5... | collective-permute-start | bytes 196616 | tf_op jit(solution)/shard_map/ppermute | solution.py:376
  18.5 3.3 %collective-permute-start.9 = (bf16[2,128,128]{2,1,0:T(8,128)(2,1)S(1)}, bf16[2,128,128]{2,1,0:T(8,128)(2,1)S(1)}, u32[]{:S(2)}, u32[]{:S(2)}) collective-permute-start(bf16[2,128,128]{2,1,0:T(8,128)(2,1)S(1)} %collective-permute-done.8.rest_2_), channel_id=1, source_target_pairs={{0,4},{4,0},{8,12},{12,8},{16,20},{20,16},{24,28},{28,24},{1,5},{5... | collective-permute-start | bytes 196616 | tf_op jit(solution)/shard_map/ppermute | solution.py:376
  20.1 2.8 %collective-permute-start.6 = (bf16[2,128,128]{2,1,0:T(8,128)(2,1)S(1)}, bf16[2,128,128]{2,1,0:T(8,128)(2,1)S(1)}, u32[]{:S(2)}, u32[]{:S(2)}) collective-permute-start(bf16[2,128,128]{2,1,0:T(8,128)(2,1)S(1)} %collective-permute-done.5.rest_5_), channel_id=1, source_target_pairs={{0,4},{4,0},{8,12},{12,8},{16,20},{20,16},{24,28},{28,24},{1,5},{5... | collective-permute-start | bytes 196616 | tf_op jit(solution)/shard_map/ppermute | solution.py:376
  20.6 2.3 %collective-permute-start.4 = (bf16[2,128,128]{2,1,0:T(8,128)(2,1)S(1)}, bf16[2,128,128]{2,1,0:T(8,128)(2,1)S(1)}, u32[]{:S(2)}, u32[]{:S(2)}) collective-permute-start(bf16[2,128,128]{2,1,0:T(8,128)(2,1)S(1)} %collective-permute-done.3.rest_4_), channel_id=1, source_target_pairs={{0,4},{4,0},{8,12},{12,8},{16,20},{20,16},{24,28},{28,24},{1,5},{5... | collective-permute-start | bytes 196616 | tf_op jit(solution)/shard_map/ppermute | solution.py:376

commit v6 on v5

--- a/solution.py
+++ b/solution.py
@@ -235,12 +235,7 @@
     return dict(zip(far + near, first[: len(far)] + list(second)))
 
 
-def slot_of(masks):
-    me = lax.axis_index("tm")
-    return me ^ jnp.where(me & 1 == 1, masks[1], masks[0])
-
-
-def mix_kernel(masks, sink, peramb, table, labels, out, units, times, sems):
+def mix_kernel(sink, peramb, table, labels, out, units, times, sems):
     load_units = pltpu.make_async_copy(table, units, sems.at[0])
     load_times = pltpu.make_async_copy(labels, times, sems.at[1])
     load_units.start()
@@ -260,7 +255,7 @@
     me = lax.axis_index("tm")
     own = times[me]
     for k in range(peramb.shape[0]):
-        n = slot_of(masks[k])
+        n = lax.axis_index("tm") ^ k
         sign = jnp.where(times[n] > own, -1.0, 1.0).astype(jnp.float32)
         right = jnp.concatenate([peramb[n, 0], peramb[n, 1]], axis=0)
         mixed = jnp.dot(left, right, preferred_element_type=jnp.float32)
@@ -276,10 +271,10 @@
         ).astype(out.dtype)
 
 
-def mix(sink, peramb, table, labels, masks):
+def mix(sink, peramb, table, labels):
     slots, _, columns, _ = peramb.shape
     return pl.pallas_call(
-        functools.partial(mix_kernel, masks),
+        mix_kernel,
         out_shape=jax.ShapeDtypeStruct((slots, columns, 2 * columns), jnp.bfloat16),
         in_specs=[VMEM, VMEM, HBM, HBM],
         out_specs=VMEM,
@@ -296,7 +291,7 @@
     )(sink, peramb, in_hbm(table), in_hbm(labels))
 
 
-def close_kernel(ks, masks, before, mixed, *rest):
+def close_kernel(ks, before, mixed, *rest):
     sources = rest[: len(ks)]
     out, blocks, sems = rest[len(ks) + before :]
     columns = sources[0].shape[-1]
@@ -312,19 +307,19 @@
         )
         blocks[i, 0] = block[:, :columns].astype(out.dtype)
         blocks[i, 1] = block[:, columns:].astype(out.dtype)
-        store = pltpu.make_async_copy(blocks.at[i], out.at[slot_of(masks[k])], sems.at[i])
+        store = pltpu.make_async_copy(blocks.at[i], out.at[lax.axis_index("tm") ^ k], sems.at[i])
         store.start()
         stores.append(store)
     for store in stores:
         store.wait()
 
 
-def close(mixed, sources, ks, masks, out=None):
+def close(mixed, sources, ks, out=None):
     slots, columns, _ = mixed.shape
     before = [] if out is None else [out]
     shape = (slots, 2, columns, columns)
     return pl.pallas_call(
-        functools.partial(close_kernel, ks, masks, len(before)),
+        functools.partial(close_kernel, ks, len(before)),
         out_shape=jax.ShapeDtypeStruct(shape, jnp.bfloat16),
         in_specs=[VMEM] * (1 + len(ks)) + [HBM] * len(before),
         out_specs=HBM,
@@ -349,7 +344,11 @@
 
 
 def hop_order(times):
-    return [(k, k) for k in range(times - 2, 0, -2)]
+    return list(range(times - 2, 0, -2)) + [3]
+
+
+def swap_order(times):
+    return [times - 2, 0] + list(range(times - 4, 2, -2))
 
 
 def body(space, times, evecs, peramb, momenta, unit_table, time_labels):
@@ -362,22 +361,16 @@
         total = total + lax.ppermute(partials[shift], "space", pairs).astype(jnp.float32)
     sink = total.astype(jnp.bfloat16)
     hops = hop_order(times)
-    masks = [(0, 0), (1, 1)]
-    for even, odd in hops:
-        masks += [(even, odd), (odd ^ 1, even ^ 1)]
     sources = {0: sink}
-    for i in range(1, len(hops) + 1):
-        even, odd = masks[2 * i]
-        pairs = [(a, a ^ (odd if a & 1 else even)) for a in range(times)]
-        sources[2 * i] = lax.ppermute(sink, "tm", pairs)
-    mixed = mix(sink, peramb[0, 0], table, time_labels, masks)
-    for i in range(len(hops) + 1):
-        pairs = [(a, a ^ 1) for a in range(times)]
-        sources[2 * i + 1] = lax.ppermute(sources[2 * i], "tm", pairs)
-    late = [times - 3, times - 1]
-    early = [k for k in range(times) if k not in late]
-    out = close(mixed, sources, early, masks)
-    return close(mixed, sources, late, masks, out)[None, None]
+    for k in hops:
+        sources[k] = lax.ppermute(sink, "tm", [(a, a ^ k) for a in range(times)])
+    mixed = mix(sink, peramb[0, 0], table, time_labels)
+    swaps = swap_order(times)
+    for k in swaps:
+        sources[k ^ 1] = lax.ppermute(sources[k], "tm", [(a, a ^ 1) for a in range(times)])
+    late = [k for k in range(times) if k & 1 or k == 2]
+    out = close(mixed, sources, [k for k in range(times) if k not in late])
+    return close(mixed, sources, late, out)[None, None]
 
 
 def solution(mesh):

time: 24 us -> 23.5 us (0.979)
  waiting for transfers between devices: 7.82 us -> 5.96 us
  starting transfers between devices: 10.7 us -> 12 us
    ppermute x7, waiting for transfers between devices: 3.77 us -> 1.9 us  [the longest x4 1.89 us: body(): sources[k] = lax.ppermute(sink, 'tm', [(a, a ^ k) for a in range(times)])]
    ppermute x7, starting transfers between devices: 3.56 us -> 4.89 us  [the longest x4 3.56 us: body(): sources[k] = lax.ppermute(sink, 'tm', [(a, a ^ k) for a in range(times)])]
  transfers between devices with their start and end apart: 10 -> 10, of which waited for: 4 -> 3; matrix products, arithmetic and copies ran while one was open for 0% -> 0% of each run, Pallas kernels for 9% -> 9%
where the time goes in v6:
time: 23.5 us; the launch traced here: 23.3 us
  starting transfers between devices  12 us (51%)
  waiting for transfers between devices  5.96 us (25%)
  Pallas kernels  5.21 us (22%)
    ppermute x3, starting transfers between devices, body(): lax.ppermute(partials[shift], 'space', pairs).astype(jnp.float32)  7.14 us
    ppermute x3, waiting for transfers between devices, body(): lax.ppermute(partials[shift], 'space', pairs).astype(jnp.float32)  4.05 us
    ppermute x4, starting transfers between devices, body(): sources[k] = lax.ppermute(sink, 'tm', [(a, a ^ k) for a in range(times)])  3.56 us
    pallas_call x1, Pallas kernels, partial_elementals(): pl.pallas_call(functools.partial(gram_first, far, near), out_shape=[jax.S...  2.03 us
    pallas_call x2, Pallas kernels, close(): pl.pallas_call(functools.partial(close_kernel, ks, len(before)), out_shap...  1.99 us
    ppermute x4, waiting for transfers between devices, body(): sources[k] = lax.ppermute(sink, 'tm', [(a, a ^ k) for a in range(times)])  1.89 us
    ppermute x3, starting transfers between devices, body(): lax.ppermute(sources[k], 'tm', [(a, a ^ 1) for a in range(times)])  1.34 us
    pallas_call x1, Pallas kernels, mix(): pl.pallas_call(mix_kernel, out_shape=jax.ShapeDtypeStruct((slots, columns...  1.15 us
  transfers between devices with their start and end apart: 10, of which 3 were waited for; matrix products, arithmetic and copies ran while one was open for 0% of the time, Pallas kernels for 9%

profile of v6, /device:TPU:0, one launch (start us, length us, event | category | flops | bytes accessed | tf_op | source)
XLA Modules:
  0.0 23.3 jit_solution(3784670188758584616)
XLA Ops:
  0.0 2.0 %gram_far.1 = (bf16[2,128,128]{2,1,0:T(8,128)(2,1)S(1)}, bf16[2,128,128]{2,1,0:T(8,128)(2,1)S(1)}, bf16[2,128,128]{2,1,0:T(8,128)(2,1)S(1)}, f32[2,128,128]{2,1,...) custom-call(bf16[2,3,256,128]{3,2,1,0:T(8,128)(2,1)} %bitcast.7, ...), custom_call_target="tpu_custom_call" | custom-call | flops 402653184 | bytes 524288 | tf_op jit(solution)/shard_map/gram_far/pallas_call | solution.py:205
  2.0 0.0 copy-start
  2.1 4.1 %collective-permute-start.2 = (bf16[2,128,128]{2,1,0:T(8,128)(2,1)S(1)}, bf16[2,128,128]{2,1,0:T(8,128)(2,1)S(1)}, u32[]{:S(2)}, u32[]{:S(2)}) collective-permute-start(bf16[2,128,128]{2,1,0:T(8,128)(2,1)S(1)} %get-tuple-element.22), channel_id=1, source_target_pairs={{0,2},{1,0},{3,1},{2,3},{4,6},{5,4},{7,5},{6,7},{8,10},{9,8},{11,9... | collective-permute-start | bytes 196616 | tf_op jit(solution)/shard_map/ppermute | solution.py:361
  6.2 0.0 collective-permute-start
  6.2 3.0 %collective-permute-start.1 = (bf16[2,128,128]{2,1,0:T(8,128)(2,1)S(1)}, bf16[2,128,128]{2,1,0:T(8,128)(2,1)S(1)}, u32[]{:S(2)}, u32[]{:S(2)}) collective-permute-start(bf16[2,128,128]{2,1,0:T(8,128)(2,1)S(1)} %get-tuple-element.21), channel_id=1, source_target_pairs={{0,3},{1,2},{3,0},{2,1},{4,7},{5,6},{7,4},{6,5},{8,11},{9,10},{11,... | collective-permute-start | bytes 196616 | tf_op jit(solution)/shard_map/ppermute | solution.py:361
  9.2 0.0 collective-permute-done.2
  9.2 4.0 %collective-permute-done = bf16[2,128,128]{2,1,0:T(8,128)(2,1)S(1)} collective-permute-done((bf16[2,128,128]{2,1,0:T(8,128)(2,1)S(1)}, bf16[2,128,128]{2,1,0:T(8,128)(2,1)S(1)}, u32[]{:S(2)}, u32[]{:S(2)}) %collective-permute-start) | collective-permute-done | bytes 65568 | tf_op jit(solution)/shard_map/ppermute | solution.py:361
  13.3 0.0 collective-permute-done.1
  13.3 2.5 %collective-permute-start.8 = (bf16[2,128,128]{2,1,0:T(8,128)(2,1)S(1)}, bf16[2,128,128]{2,1,0:T(8,128)(2,1)S(1)}, u32[]{:S(2)}, u32[]{:S(2)}) collective-permute-start(bf16[2,128,128]{2,1,0:T(8,128)(2,1)S(1)} %add_convert_fusion.sink.rest_0_), channel_id=1, source_target_pairs={{0,24},{4,28},{8,16},{12,20},{16,8},{20,12},{24,0},{28,4},{1,25},{... | collective-permute-start | bytes 196616 | tf_op jit(solution)/shard_map/ppermute | solution.py:366
  15.8 0.5 %collective-permute-start.6 = (bf16[2,128,128]{2,1,0:T(8,128)(2,1)S(1)}, bf16[2,128,128]{2,1,0:T(8,128)(2,1)S(1)}, u32[]{:S(2)}, u32[]{:S(2)}) collective-permute-start(bf16[2,128,128]{2,1,0:T(8,128)(2,1)S(1)} %add_convert_fusion.sink.rest_0_), channel_id=1, source_target_pairs={{0,16},{4,20},{8,24},{12,28},{16,0},{20,4},{24,8},{28,12},{1,17},{... | collective-permute-start | bytes 196616 | tf_op jit(solution)/shard_map/ppermute | solution.py:366
  16.3 0.0 collective-permute-start.5
  16.4 0.5 %collective-permute-start.4 = (bf16[2,128,128]{2,1,0:T(8,128)(2,1)S(1)}, bf16[2,128,128]{2,1,0:T(8,128)(2,1)S(1)}, u32[]{:S(2)}, u32[]{:S(2)}) collective-permute-start(bf16[2,128,128]{2,1,0:T(8,128)(2,1)S(1)} %add_convert_fusion.sink.rest_0_), channel_id=1, source_target_pairs={{0,8},{4,12},{8,0},{12,4},{16,24},{20,28},{24,16},{28,20},{1,9},{5... | collective-permute-start | bytes 196616 | tf_op jit(solution)/shard_map/ppermute | solution.py:366
  16.9 1.3 %collective-permute-start.3 = (bf16[2,128,128]{2,1,0:T(8,128)(2,1)S(1)}, bf16[2,128,128]{2,1,0:T(8,128)(2,1)S(1)}, u32[]{:S(2)}, u32[]{:S(2)}) collective-permute-start(bf16[2,128,128]{2,1,0:T(8,128)(2,1)S(1)} %add_convert_fusion.sink.rest_0_), channel_id=1, source_target_pairs={{0,4},{4,0},{8,12},{12,8},{16,20},{20,16},{24,28},{28,24},{1,5},{5... | collective-permute-start | bytes 196616 | tf_op jit(solution)/shard_map/ppermute | solution.py:370
  18.2 0.3 %collective-permute-done.8.rest_2_ = bf16[2,128,128]{2,1,0:T(8,128)(2,1)S(1)} collective-permute-done((bf16[2,128,128]{2,1,0:T(8,128)(2,1)S(1)}, bf16[2,128,128]{2,1,0:T(8,128)(2,1)S(1)}, u32[]{:S(2)}, u32[]{:S(2)}) %collective-permute-start.8) | collective-permute-done | bytes 65568 | tf_op jit(solution)/shard_map/ppermute | solution.py:366
  18.5 0.0 collective-permute-start.9
  18.6 1.6 %collective-permute-done.6.rest_1_ = bf16[2,128,128]{2,1,0:T(8,128)(2,1)S(1)} collective-permute-done((bf16[2,128,128]{2,1,0:T(8,128)(2,1)S(1)}, bf16[2,128,128]{2,1,0:T(8,128)(2,1)S(1)}, u32[]{:S(2)}, u32[]{:S(2)}) %collective-permute-start.6) | collective-permute-done | bytes 65568 | tf_op jit(solution)/shard_map/ppermute | solution.py:366
  20.1 0.0 collective-permute-start.7
  20.1 0.0 copy-done
  20.1 1.2 %mix.1.mixed = bf16[8,128,256]{2,1,0:T(8,128)(2,1)S(1)} custom-call(bf16[2,128,128]{2,1,0:T(8,128)(2,1)S(1)} %add_convert_fusion.sink.rest_0_, bf16[8,2,128,128]{3,2,1,0:T(8,128)(2,1)S(1)} %bitcast.4, s32[2,4]{1,0:T(2,128)} %bitcast.6, s32[8]{0:T(128)} %labels.1), custom_call_target="tpu_custom_call" | custom-call | flops 134217728 | bytes 1048576 | tf_op jit(solution)/shard_map/mix/pallas_call | solution.py:276
  21.3 0.9 %close.2.rest_5_ = bf16[8,2,128,128]{3,2,1,0:T(8,128)(2,1)} custom-call(bf16[8,128,256]{2,1,0:T(8,128)(2,1)S(1)} %mix.1.mixed, bf16[2,128,128]{2,1,0:T(8,128)(2,1)S(1)} %add_convert_fusion.sink.rest_0_, bf16[2,128,128]{2,1,0:T(8,128)(2,1)S(1)} %collective-permute-done.6.rest_1_, bf16[2,128,128]{2,1,0:T(8,128)(2,1)S(1)} %collective-permute-done.8.rest_2_), custom_call_target="tpu_custom_call" | custom-call | flops 50331648 | bytes 589824 | tf_op jit(solution)/shard_map/close/pallas_call | solution.py:321
  22.2 0.0 collective-permute-done.5.rest_2_
  22.2 0.0 collective-permute-done.4.rest_1_
  22.2 0.0 collective-permute-done.3.rest_0_
  22.2 0.0 collective-permute-done.9.rest_4_
  22.3 0.0 collective-permute-done.7.rest_3_
  22.3 1.1 %close.3 = bf16[8,2,128,128]{3,2,1,0:T(8,128)(2,1)} custom-call(bf16[8,128,256]{2,1,0:T(8,128)(2,1)S(1)} %mix.1.mixed, bf16[2,128,128]{2,1,0:T(8,128)(2,1)S(1)} %collective-permute-done.3.rest_0_, bf16[2,128,128]{2,1,0:T(8,128)(2,1)S(1)} %collective-permute-done.4.rest_1_, ...), custom_call_target="tpu_custom_call", output_to_operand_aliasing={{}: (6, {})} | custom-call | flops 83886080 | bytes 983040 | tf_op jit(solution)/shard_map/close/pallas_call | solution.py:321
  (2 shorter events, 0.1 us)
Async XLA Ops:
  2.0 18.1 %copy-start = (bf16[1,1,8,2,128,128]{5,4,3,2,1,0:T(8,128)(2,1)S(1)}, bf16[1,1,8,2,128,128]{5,4,3,2,1,0:T(8,128)(2,1)}, u32[]{:S(2)}) copy-start(bf16[1,1,8,2,128,128]{5,4,3,2,1,0:T(8,128)(2,1)} %param.7) | copy-start | bytes 1572868
  2.1 7.1 %collective-permute-start.2 = (bf16[2,128,128]{2,1,0:T(8,128)(2,1)S(1)}, bf16[2,128,128]{2,1,0:T(8,128)(2,1)S(1)}, u32[]{:S(2)}, u32[]{:S(2)}) collective-permute-start(bf16[2,128,128]{2,1,0:T(8,128)(2,1)S(1)} %get-tuple-element.22), channel_id=1, source_target_pairs={{0,2},{1,0},{3,1},{2,3},{4,6},{5,4},{7,5},{6,7},{8,10},{9,8},{11,9... | collective-permute-start | bytes 196616 | tf_op jit(solution)/shard_map/ppermute | solution.py:361
  6.2 7.1 %collective-permute-start = (bf16[2,128,128]{2,1,0:T(8,128)(2,1)S(1)}, bf16[2,128,128]{2,1,0:T(8,128)(2,1)S(1)}, u32[]{:S(2)}, u32[]{:S(2)}) collective-permute-start(bf16[2,128,128]{2,1,0:T(8,128)(2,1)S(1)} %get-tuple-element.20), channel_id=1, source_target_pairs={{0,1},{1,3},{3,2},{2,0},{4,5},{5,7},{7,6},{6,4},{8,9},{9,11},{11,1... | collective-permute-start | bytes 196616 | tf_op jit(solution)/shard_map/ppermute | solution.py:361
  6.2 7.1 %collective-permute-start.1 = (bf16[2,128,128]{2,1,0:T(8,128)(2,1)S(1)}, bf16[2,128,128]{2,1,0:T(8,128)(2,1)S(1)}, u32[]{:S(2)}, u32[]{:S(2)}) collective-permute-start(bf16[2,128,128]{2,1,0:T(8,128)(2,1)S(1)} %get-tuple-element.21), channel_id=1, source_target_pairs={{0,3},{1,2},{3,0},{2,1},{4,7},{5,6},{7,4},{6,5},{8,11},{9,10},{11,... | collective-permute-start | bytes 196616 | tf_op jit(solution)/shard_map/ppermute | solution.py:361
  13.3 5.2 %collective-permute-start.8 = (bf16[2,128,128]{2,1,0:T(8,128)(2,1)S(1)}, bf16[2,128,128]{2,1,0:T(8,128)(2,1)S(1)}, u32[]{:S(2)}, u32[]{:S(2)}) collective-permute-start(bf16[2,128,128]{2,1,0:T(8,128)(2,1)S(1)} %add_convert_fusion.sink.rest_0_), channel_id=1, source_target_pairs={{0,24},{4,28},{8,16},{12,20},{16,8},{20,12},{24,0},{28,4},{1,25},{... | collective-permute-start | bytes 196616 | tf_op jit(solution)/shard_map/ppermute | solution.py:366
  15.8 4.3 %collective-permute-start.6 = (bf16[2,128,128]{2,1,0:T(8,128)(2,1)S(1)}, bf16[2,128,128]{2,1,0:T(8,128)(2,1)S(1)}, u32[]{:S(2)}, u32[]{:S(2)}) collective-permute-start(bf16[2,128,128]{2,1,0:T(8,128)(2,1)S(1)} %add_convert_fusion.sink.rest_0_), channel_id=1, source_target_pairs={{0,16},{4,20},{8,24},{12,28},{16,0},{20,4},{24,8},{28,12},{1,17},{... | collective-permute-start | bytes 196616 | tf_op jit(solution)/shard_map/ppermute | solution.py:366
  16.3 5.9 %collective-permute-start.5 = (bf16[2,128,128]{2,1,0:T(8,128)(2,1)S(1)}, bf16[2,128,128]{2,1,0:T(8,128)(2,1)S(1)}, u32[]{:S(2)}, u32[]{:S(2)}) collective-permute-start(bf16[2,128,128]{2,1,0:T(8,128)(2,1)S(1)} %add_convert_fusion.sink.rest_0_), channel_id=1, source_target_pairs={{0,12},{4,8},{8,4},{12,0},{16,28},{20,24},{24,20},{28,16},{1,13},{... | collective-permute-start | bytes 196616 | tf_op jit(solution)/shard_map/ppermute | solution.py:366
  16.4 5.9 %collective-permute-start.4 = (bf16[2,128,128]{2,1,0:T(8,128)(2,1)S(1)}, bf16[2,128,128]{2,1,0:T(8,128)(2,1)S(1)}, u32[]{:S(2)}, u32[]{:S(2)}) collective-permute-start(bf16[2,128,128]{2,1,0:T(8,128)(2,1)S(1)} %add_convert_fusion.sink.rest_0_), channel_id=1, source_target_pairs={{0,8},{4,12},{8,0},{12,4},{16,24},{20,28},{24,16},{28,20},{1,9},{5... | collective-permute-start | bytes 196616 | tf_op jit(solution)/shard_map/ppermute | solution.py:366
  16.9 5.4 %collective-permute-start.3 = (bf16[2,128,128]{2,1,0:T(8,128)(2,1)S(1)}, bf16[2,128,128]{2,1,0:T(8,128)(2,1)S(1)}, u32[]{:S(2)}, u32[]{:S(2)}) collective-permute-start(bf16[2,128,128]{2,1,0:T(8,128)(2,1)S(1)} %add_convert_fusion.sink.rest_0_), channel_id=1, source_target_pairs={{0,4},{4,0},{8,12},{12,8},{16,20},{20,16},{24,28},{28,24},{1,5},{5... | collective-permute-start | bytes 196616 | tf_op jit(solution)/shard_map/ppermute | solution.py:370
  18.5 3.7 %collective-permute-start.9 = (bf16[2,128,128]{2,1,0:T(8,128)(2,1)S(1)}, bf16[2,128,128]{2,1,0:T(8,128)(2,1)S(1)}, u32[]{:S(2)}, u32[]{:S(2)}) collective-permute-start(bf16[2,128,128]{2,1,0:T(8,128)(2,1)S(1)} %collective-permute-done.8.rest_2_), channel_id=1, source_target_pairs={{0,4},{4,0},{8,12},{12,8},{16,20},{20,16},{24,28},{28,24},{1,5},{5... | collective-permute-start | bytes 196616 | tf_op jit(solution)/shard_map/ppermute | solution.py:370
  20.1 2.2 %collective-permute-start.7 = (bf16[2,128,128]{2,1,0:T(8,128)(2,1)S(1)}, bf16[2,128,128]{2,1,0:T(8,128)(2,1)S(1)}, u32[]{:S(2)}, u32[]{:S(2)}) collective-permute-start(bf16[2,128,128]{2,1,0:T(8,128)(2,1)S(1)} %collective-permute-done.6.rest_1_), channel_id=1, source_target_pairs={{0,4},{4,0},{8,12},{12,8},{16,20},{20,16},{24,28},{28,24},{1,5},{5... | collective-permute-start | bytes 196616 | tf_op jit(solution)/shard_map/ppermute | solution.py:370

commit v7 on v6

--- a/solution.py
+++ b/solution.py
@@ -235,48 +235,33 @@
     return dict(zip(far + near, first[: len(far)] + list(second)))
 
 
-def mix_kernel(sink, peramb, table, labels, out, units, times, sems):
-    load_units = pltpu.make_async_copy(table, units, sems.at[0])
-    load_times = pltpu.make_async_copy(labels, times, sems.at[1])
-    load_units.start()
-    load_times.start()
-    real = sink[0]
-    imag = sink[1]
-    columns = real.shape[0]
-    left = jnp.concatenate(
-        [jnp.concatenate([real, -imag], axis=1), jnp.concatenate([imag, real], axis=1)], axis=0
-    )
-    load_units.wait()
-    load_times.wait()
-    turns = units[1, lax.axis_index("space")]
-    odd = lax.rem(turns, 2)
-    phase_real = ((1 - odd) * (1 - turns)).astype(jnp.float32)
-    phase_imag = (odd * (2 - turns)).astype(jnp.float32)
+def turn_kernel(table, labels_in, turns, units, labels, sems):
+    loads = [
+        pltpu.make_async_copy(source, target, sems.at[i])
+        for i, (source, target) in enumerate(((table, units), (labels_in, labels)))
+    ]
+    for load in loads:
+        load.start()
+    for load in loads:
+        load.wait()
+    power = units[1, lax.axis_index("space")]
+    odd = lax.rem(power, 2)
+    phase_real = ((1 - odd) * (1 - power)).astype(jnp.float32)
+    phase_imag = (odd * (2 - power)).astype(jnp.float32)
     me = lax.axis_index("tm")
-    own = times[me]
-    for k in range(peramb.shape[0]):
-        n = lax.axis_index("tm") ^ k
-        sign = jnp.where(times[n] > own, -1.0, 1.0).astype(jnp.float32)
-        right = jnp.concatenate([peramb[n, 0], peramb[n, 1]], axis=0)
-        mixed = jnp.dot(left, right, preferred_element_type=jnp.float32)
-        mixed_real = mixed[:columns]
-        mixed_imag = mixed[columns:]
-        turn_real = sign * phase_real
-        turn_imag = sign * phase_imag
-        out[k, :, pl.ds(0, columns)] = (turn_real * mixed_real - turn_imag * mixed_imag).astype(
-            out.dtype
-        )
-        out[k, :, pl.ds(columns, columns)] = (
-            turn_real * mixed_imag + turn_imag * mixed_real
-        ).astype(out.dtype)
-
-
-def mix(sink, peramb, table, labels):
-    slots, _, columns, _ = peramb.shape
+    own = labels[me]
+    for k in range(turns.shape[0]):
+        sign = jnp.where(labels[me ^ k] > own, -1.0, 1.0).astype(jnp.float32)
+        turns[k, 0] = jnp.full(turns.shape[2:], sign * phase_real, jnp.float32)
+        turns[k, 1] = jnp.full(turns.shape[2:], sign * phase_imag, jnp.float32)
+
+
+def turn_factors(table, labels, columns):
+    slots = labels.shape[0]
     return pl.pallas_call(
-        mix_kernel,
-        out_shape=jax.ShapeDtypeStruct((slots, columns, 2 * columns), jnp.bfloat16),
-        in_specs=[VMEM, VMEM, HBM, HBM],
+        turn_kernel,
+        out_shape=jax.ShapeDtypeStruct((slots, 2, 8, columns), jnp.float32),
+        in_specs=[HBM] * 2,
         out_specs=VMEM,
         scratch_shapes=[
             pltpu.SMEM(table.shape, jnp.int32),
@@ -285,10 +270,49 @@
         ],
         compiler_params=pltpu.CompilerParams(vmem_limit_bytes=LIMIT),
         cost_estimate=pl.CostEstimate(
+            flops=slots, bytes_accessed=slots * 64 * columns, transcendentals=0
+        ),
+        name="turn",
+    )(in_hbm(table), in_hbm(labels))
+
+
+def mix_kernel(sink, peramb, turns, out):
+    real = sink[0]
+    imag = sink[1]
+    columns = real.shape[0]
+    left = jnp.concatenate(
+        [jnp.concatenate([real, -imag], axis=1), jnp.concatenate([imag, real], axis=1)], axis=0
+    )
+    me = lax.axis_index("tm")
+    for k in range(peramb.shape[0]):
+        n = me ^ k
+        right = jnp.concatenate([peramb[n, 0], peramb[n, 1]], axis=0)
+        mixed = jnp.dot(left, right, preferred_element_type=jnp.float32)
+        mixed_real = mixed[:columns]
+        mixed_imag = mixed[columns:]
+        turn_real = turns[k, 0, 0:1, :]
+        turn_imag = turns[k, 1, 0:1, :]
+        out[k, :, pl.ds(0, columns)] = (turn_real * mixed_real - turn_imag * mixed_imag).astype(
+            out.dtype
+        )
+        out[k, :, pl.ds(columns, columns)] = (
+            turn_real * mixed_imag + turn_imag * mixed_real
+        ).astype(out.dtype)
+
+
+def mix(sink, peramb, turns):
+    slots, _, columns, _ = peramb.shape
+    return pl.pallas_call(
+        mix_kernel,
+        out_shape=jax.ShapeDtypeStruct((slots, columns, 2 * columns), jnp.bfloat16),
+        in_specs=[VMEM] * 3,
+        out_specs=VMEM,
+        compiler_params=pltpu.CompilerParams(vmem_limit_bytes=LIMIT),
+        cost_estimate=pl.CostEstimate(
             flops=slots * 8 * columns**3, bytes_accessed=slots * 8 * columns**2, transcendentals=0
         ),
         name="mix",
-    )(sink, peramb, in_hbm(table), in_hbm(labels))
+    )(sink, peramb, turns)
 
 
 def close_kernel(ks, before, mixed, *rest):
@@ -355,6 +379,7 @@
     table = unit_table.T
     shifts, far = sum_order(space)
     partials = partial_elementals(evecs[0], momenta, table, shifts[:far], shifts[far:] + [0])
+    turns = turn_factors(table, time_labels, peramb.shape[-1])
     total = partials[0]
     for shift in shifts:
         pairs = along(space, shift)
@@ -364,11 +389,11 @@
     sources = {0: sink}
     for k in hops:
         sources[k] = lax.ppermute(sink, "tm", [(a, a ^ k) for a in range(times)])
-    mixed = mix(sink, peramb[0, 0], table, time_labels)
+    mixed = mix(sink, peramb[0, 0], turns)
     swaps = swap_order(times)
     for k in swaps:
         sources[k ^ 1] = lax.ppermute(sources[k], "tm", [(a, a ^ 1) for a in range(times)])
-    late = [k for k in range(times) if k & 1 or k == 2]
+    late = [2, 3] + list(range(5, times - 2, 2))
     out = close(mixed, sources, [k for k in range(times) if k not in late])
     return close(mixed, sources, late, out)[None, None]
 

time: 23.5 us -> 25.2 us (1.072)
  waiting for transfers between devices: 5.96 us -> 7.34 us
  starting transfers between devices: 12 us -> 12.3 us
    ppermute x4, waiting for transfers between devices: 1.89 us -> 3.28 us  [body(): sources[k] = lax.ppermute(sink, 'tm', [(a, a ^ k) for a in range(times)])]
    ppermute x4, starting transfers between devices: 3.56 us -> 4.89 us  [body(): sources[k] = lax.ppermute(sink, 'tm', [(a, a ^ k) for a in range(times)])]
    ppermute x3, starting transfers between devices: 1.34 us -> 0.29 us  [body(): lax.ppermute(sources[k], 'tm', [(a, a ^ 1) for a in range(times)])]
    pallas_call x0 -> x1, Pallas kernels: none -> 0.74 us  [turn_factors(): pl.pallas_call(turn_kernel, out_shape=jax.ShapeDtypeStruct((slots, 2, 8,...]
    pallas_call x1, Pallas kernels: 1.15 us -> 0.44 us  [mix(): pl.pallas_call(mix_kernel, out_shape=jax.ShapeDtypeStruct((slots, columns...]
  transfers between devices with their start and end apart: 10 -> 10, of which waited for: 3 -> 4; matrix products, arithmetic and copies ran while one was open for 0% -> 0% of each run, Pallas kernels for 9% -> 9%
where the time goes in v7:
time: 25.2 us; the launch traced here: 25 us
  starting transfers between devices  12.3 us (49%)
  waiting for transfers between devices  7.34 us (29%)
  Pallas kernels  5.24 us (21%)
    ppermute x3, starting transfers between devices, body(): lax.ppermute(partials[shift], 'space', pairs).astype(jnp.float32)  7.14 us
    ppermute x4, starting transfers between devices, body(): sources[k] = lax.ppermute(sink, 'tm', [(a, a ^ k) for a in range(times)])  4.89 us
    ppermute x3, waiting for transfers between devices, body(): lax.ppermute(partials[shift], 'space', pairs).astype(jnp.float32)  4.05 us
    ppermute x4, waiting for transfers between devices, body(): sources[k] = lax.ppermute(sink, 'tm', [(a, a ^ k) for a in range(times)])  3.28 us
    pallas_call x1, Pallas kernels, partial_elementals(): pl.pallas_call(functools.partial(gram_first, far, near), out_shape=[jax.S...  2.03 us
    pallas_call x2, Pallas kernels, close(): pl.pallas_call(functools.partial(close_kernel, ks, len(before)), out_shap...  2 us
    pallas_call x1, Pallas kernels, turn_factors(): pl.pallas_call(turn_kernel, out_shape=jax.ShapeDtypeStruct((slots, 2, 8,...  0.74 us
  transfers between devices with their start and end apart: 10, of which 4 were waited for; matrix products, arithmetic and copies ran while one was open for 0% of the time, Pallas kernels for 9%

profile of v7, /device:TPU:0, one launch (start us, length us, event | category | flops | bytes accessed | tf_op | source)
XLA Modules:
  0.0 25.0 jit_solution(10965043281236251660)
XLA Ops:
  0.0 2.0 %gram_far.1 = (bf16[2,128,128]{2,1,0:T(8,128)(2,1)S(1)}, bf16[2,128,128]{2,1,0:T(8,128)(2,1)S(1)}, bf16[2,128,128]{2,1,0:T(8,128)(2,1)S(1)}, f32[2,128,128]{2,1,...) custom-call(bf16[2,3,256,128]{3,2,1,0:T(8,128)(2,1)} %bitcast.7, ...), custom_call_target="tpu_custom_call" | custom-call | flops 402653184 | bytes 524288 | tf_op jit(solution)/shard_map/gram_far/pallas_call | solution.py:205
  2.0 0.0 copy-start
  2.1 4.1 %collective-permute-start.2 = (bf16[2,128,128]{2,1,0:T(8,128)(2,1)S(1)}, bf16[2,128,128]{2,1,0:T(8,128)(2,1)S(1)}, u32[]{:S(2)}, u32[]{:S(2)}) collective-permute-start(bf16[2,128,128]{2,1,0:T(8,128)(2,1)S(1)} %get-tuple-element.22), channel_id=1, source_target_pairs={{0,2},{1,0},{3,1},{2,3},{4,6},{5,4},{7,5},{6,7},{8,10},{9,8},{11,9... | collective-permute-start | bytes 196616 | tf_op jit(solution)/shard_map/ppermute | solution.py:386
  6.2 0.0 collective-permute-start
  6.2 3.0 %collective-permute-start.1 = (bf16[2,128,128]{2,1,0:T(8,128)(2,1)S(1)}, bf16[2,128,128]{2,1,0:T(8,128)(2,1)S(1)}, u32[]{:S(2)}, u32[]{:S(2)}) collective-permute-start(bf16[2,128,128]{2,1,0:T(8,128)(2,1)S(1)} %get-tuple-element.21), channel_id=1, source_target_pairs={{0,3},{1,2},{3,0},{2,1},{4,7},{5,6},{7,4},{6,5},{8,11},{9,10},{11,... | collective-permute-start | bytes 196616 | tf_op jit(solution)/shard_map/ppermute | solution.py:386
  9.2 0.0 collective-permute-done.2
  9.2 4.0 %collective-permute-done = bf16[2,128,128]{2,1,0:T(8,128)(2,1)S(1)} collective-permute-done((bf16[2,128,128]{2,1,0:T(8,128)(2,1)S(1)}, bf16[2,128,128]{2,1,0:T(8,128)(2,1)S(1)}, u32[]{:S(2)}, u32[]{:S(2)}) %collective-permute-start) | collective-permute-done | bytes 65568 | tf_op jit(solution)/shard_map/ppermute | solution.py:386
  13.3 0.0 collective-permute-done.1
  13.3 2.5 %collective-permute-start.8 = (bf16[2,128,128]{2,1,0:T(8,128)(2,1)S(1)}, bf16[2,128,128]{2,1,0:T(8,128)(2,1)S(1)}, u32[]{:S(2)}, u32[]{:S(2)}) collective-permute-start(bf16[2,128,128]{2,1,0:T(8,128)(2,1)S(1)} %add_convert_fusion.sink.rest_0_), channel_id=1, source_target_pairs={{0,24},{4,28},{8,16},{12,20},{16,8},{20,12},{24,0},{28,4},{1,25},{... | collective-permute-start | bytes 196616 | tf_op jit(solution)/shard_map/ppermute | solution.py:391
  15.8 0.5 %collective-permute-start.5 = (bf16[2,128,128]{2,1,0:T(8,128)(2,1)S(1)}, bf16[2,128,128]{2,1,0:T(8,128)(2,1)S(1)}, u32[]{:S(2)}, u32[]{:S(2)}) collective-permute-start(bf16[2,128,128]{2,1,0:T(8,128)(2,1)S(1)} %add_convert_fusion.sink.rest_0_), channel_id=1, source_target_pairs={{0,16},{4,20},{8,24},{12,28},{16,0},{20,4},{24,8},{28,12},{1,17},{... | collective-permute-start | bytes 196616 | tf_op jit(solution)/shard_map/ppermute | solution.py:391
  16.3 0.0 collective-permute-start.7
  16.4 2.2 %collective-permute-done.8.rest_3_ = bf16[2,128,128]{2,1,0:T(8,128)(2,1)S(1)} collective-permute-done((bf16[2,128,128]{2,1,0:T(8,128)(2,1)S(1)}, bf16[2,128,128]{2,1,0:T(8,128)(2,1)S(1)}, u32[]{:S(2)}, u32[]{:S(2)}) %collective-permute-start.8) | collective-permute-done | bytes 65568 | tf_op jit(solution)/shard_map/ppermute | solution.py:391
  18.5 0.0 collective-permute-start.9
  18.6 1.5 %collective-permute-start.3 = (bf16[2,128,128]{2,1,0:T(8,128)(2,1)S(1)}, bf16[2,128,128]{2,1,0:T(8,128)(2,1)S(1)}, u32[]{:S(2)}, u32[]{:S(2)}) collective-permute-start(bf16[2,128,128]{2,1,0:T(8,128)(2,1)S(1)} %add_convert_fusion.sink.rest_0_), channel_id=1, source_target_pairs={{0,8},{4,12},{8,0},{12,4},{16,24},{20,28},{24,16},{28,20},{1,9},{5... | collective-permute-start | bytes 196616 | tf_op jit(solution)/shard_map/ppermute | solution.py:391
  20.1 0.4 %collective-permute-start.4 = (bf16[2,128,128]{2,1,0:T(8,128)(2,1)S(1)}, bf16[2,128,128]{2,1,0:T(8,128)(2,1)S(1)}, u32[]{:S(2)}, u32[]{:S(2)}) collective-permute-start(bf16[2,128,128]{2,1,0:T(8,128)(2,1)S(1)} %add_convert_fusion.sink.rest_0_), channel_id=1, source_target_pairs={{0,12},{4,8},{8,4},{12,0},{16,28},{20,24},{24,20},{28,16},{1,13},{... | collective-permute-start | bytes 196616 | tf_op jit(solution)/shard_map/ppermute | solution.py:391
  20.4 0.0 collective-permute-done.5.rest_2_
  20.4 0.3 %collective-permute-start.6 = (bf16[2,128,128]{2,1,0:T(8,128)(2,1)S(1)}, bf16[2,128,128]{2,1,0:T(8,128)(2,1)S(1)}, u32[]{:S(2)}, u32[]{:S(2)}) collective-permute-start(bf16[2,128,128]{2,1,0:T(8,128)(2,1)S(1)} %collective-permute-done.5.rest_2_), channel_id=1, source_target_pairs={{0,4},{4,0},{8,12},{12,8},{16,20},{20,16},{24,28},{28,24},{1,5},{5... | collective-permute-start | bytes 196616 | tf_op jit(solution)/shard_map/ppermute | solution.py:395
  20.7 0.7 %turn.1.turns = f32[8,2,8,128]{3,2,1,0:T(8,128)S(1)} custom-call(s32[2,4]{1,0:T(2,128)} %bitcast.6, s32[8]{0:T(128)} %labels_in.1), custom_call_target="tpu_custom_call" | custom-call | flops 8 | bytes 65536 | tf_op jit(solution)/shard_map/turn/pallas_call | solution.py:261
  21.4 0.0 copy-done
  21.5 0.4 %mix.1.mixed = bf16[8,128,256]{2,1,0:T(8,128)(2,1)S(1)} custom-call(bf16[2,128,128]{2,1,0:T(8,128)(2,1)S(1)} %add_convert_fusion.sink.rest_0_, bf16[8,2,128,128]{3,2,1,0:T(8,128)(2,1)S(1)} %bitcast.4, f32[8,2,8,128]{3,2,1,0:T(8,128)S(1)} %turn.1.turns), custom_call_target="tpu_custom_call" | custom-call | flops 134217728 | bytes 1048576 | tf_op jit(solution)/shard_map/mix/pallas_call | solution.py:305
  21.9 0.0 collective-permute-done.7.rest_1_
  21.9 0.0 collective-permute-done.9.rest_4_
  21.9 1.0 %close.2.rest_3_ = bf16[8,2,128,128]{3,2,1,0:T(8,128)(2,1)} custom-call(bf16[8,128,256]{2,1,0:T(8,128)(2,1)S(1)} %mix.1.mixed, bf16[2,128,128]{2,1,0:T(8,128)(2,1)S(1)} %add_convert_fusion.sink.rest_0_, bf16[2,128,128]{2,1,0:T(8,128)(2,1)S(1)} %collective-permute-done.7.rest_1_, bf16[2,128,128]{2,1,0:T(8,128)(2,1)S(1)} %collective-permute-done.5.rest_2_, ...), custom_call_target="tpu_custom_call" | custom-call | flops 83886080 | bytes 983040 | tf_op jit(solution)/shard_map/close/pallas_call | solution.py:345
  23.0 0.1 collective-permute-done.3.rest_0_
  23.1 1.0 %collective-permute-done.4.rest_1_ = bf16[2,128,128]{2,1,0:T(8,128)(2,1)S(1)} collective-permute-done((bf16[2,128,128]{2,1,0:T(8,128)(2,1)S(1)}, bf16[2,128,128]{2,1,0:T(8,128)(2,1)S(1)}, u32[]{:S(2)}, u32[]{:S(2)}) %collective-permute-start.4) | collective-permute-done | bytes 65568 | tf_op jit(solution)/shard_map/ppermute | solution.py:391
  24.1 0.0 collective-permute-done.6.rest_2_
  24.1 0.9 %close.3 = bf16[8,2,128,128]{3,2,1,0:T(8,128)(2,1)} custom-call(bf16[8,128,256]{2,1,0:T(8,128)(2,1)S(1)} %mix.1.mixed, bf16[2,128,128]{2,1,0:T(8,128)(2,1)S(1)} %collective-permute-done.3.rest_0_, bf16[2,128,128]{2,1,0:T(8,128)(2,1)S(1)} %collective-permute-done.4.rest_1_, ...), custom_call_target="tpu_custom_call", output_to_operand_aliasing={{}: (4, {})} | custom-call | flops 50331648 | bytes 589824 | tf_op jit(solution)/shard_map/close/pallas_call | solution.py:345
  (2 shorter events, 0.1 us)
Async XLA Ops:
  2.0 19.4 %copy-start = (bf16[1,1,8,2,128,128]{5,4,3,2,1,0:T(8,128)(2,1)S(1)}, bf16[1,1,8,2,128,128]{5,4,3,2,1,0:T(8,128)(2,1)}, u32[]{:S(2)}) copy-start(bf16[1,1,8,2,128,128]{5,4,3,2,1,0:T(8,128)(2,1)} %param.7) | copy-start | bytes 1572868
  2.1 7.1 %collective-permute-start.2 = (bf16[2,128,128]{2,1,0:T(8,128)(2,1)S(1)}, bf16[2,128,128]{2,1,0:T(8,128)(2,1)S(1)}, u32[]{:S(2)}, u32[]{:S(2)}) collective-permute-start(bf16[2,128,128]{2,1,0:T(8,128)(2,1)S(1)} %get-tuple-element.22), channel_id=1, source_target_pairs={{0,2},{1,0},{3,1},{2,3},{4,6},{5,4},{7,5},{6,7},{8,10},{9,8},{11,9... | collective-permute-start | bytes 196616 | tf_op jit(solution)/shard_map/ppermute | solution.py:386
  6.2 7.1 %collective-permute-start = (bf16[2,128,128]{2,1,0:T(8,128)(2,1)S(1)}, bf16[2,128,128]{2,1,0:T(8,128)(2,1)S(1)}, u32[]{:S(2)}, u32[]{:S(2)}) collective-permute-start(bf16[2,128,128]{2,1,0:T(8,128)(2,1)S(1)} %get-tuple-element.20), channel_id=1, source_target_pairs={{0,1},{1,3},{3,2},{2,0},{4,5},{5,7},{7,6},{6,4},{8,9},{9,11},{11,1... | collective-permute-start | bytes 196616 | tf_op jit(solution)/shard_map/ppermute | solution.py:386
  6.2 7.1 %collective-permute-start.1 = (bf16[2,128,128]{2,1,0:T(8,128)(2,1)S(1)}, bf16[2,128,128]{2,1,0:T(8,128)(2,1)S(1)}, u32[]{:S(2)}, u32[]{:S(2)}) collective-permute-start(bf16[2,128,128]{2,1,0:T(8,128)(2,1)S(1)} %get-tuple-element.21), channel_id=1, source_target_pairs={{0,3},{1,2},{3,0},{2,1},{4,7},{5,6},{7,4},{6,5},{8,11},{9,10},{11,... | collective-permute-start | bytes 196616 | tf_op jit(solution)/shard_map/ppermute | solution.py:386
  13.3 5.2 %collective-permute-start.8 = (bf16[2,128,128]{2,1,0:T(8,128)(2,1)S(1)}, bf16[2,128,128]{2,1,0:T(8,128)(2,1)S(1)}, u32[]{:S(2)}, u32[]{:S(2)}) collective-permute-start(bf16[2,128,128]{2,1,0:T(8,128)(2,1)S(1)} %add_convert_fusion.sink.rest_0_), channel_id=1, source_target_pairs={{0,24},{4,28},{8,16},{12,20},{16,8},{20,12},{24,0},{28,4},{1,25},{... | collective-permute-start | bytes 196616 | tf_op jit(solution)/shard_map/ppermute | solution.py:391
  15.8 4.6 %collective-permute-start.5 = (bf16[2,128,128]{2,1,0:T(8,128)(2,1)S(1)}, bf16[2,128,128]{2,1,0:T(8,128)(2,1)S(1)}, u32[]{:S(2)}, u32[]{:S(2)}) collective-permute-start(bf16[2,128,128]{2,1,0:T(8,128)(2,1)S(1)} %add_convert_fusion.sink.rest_0_), channel_id=1, source_target_pairs={{0,16},{4,20},{8,24},{12,28},{16,0},{20,4},{24,8},{28,12},{1,17},{... | collective-permute-start | bytes 196616 | tf_op jit(solution)/shard_map/ppermute | solution.py:391
  16.3 5.6 %collective-permute-start.7 = (bf16[2,128,128]{2,1,0:T(8,128)(2,1)S(1)}, bf16[2,128,128]{2,1,0:T(8,128)(2,1)S(1)}, u32[]{:S(2)}, u32[]{:S(2)}) collective-permute-start(bf16[2,128,128]{2,1,0:T(8,128)(2,1)S(1)} %add_convert_fusion.sink.rest_0_), channel_id=1, source_target_pairs={{0,4},{4,0},{8,12},{12,8},{16,20},{20,16},{24,28},{28,24},{1,5},{5... | collective-permute-start | bytes 196616 | tf_op jit(solution)/shard_map/ppermute | solution.py:395
  18.5 3.4 %collective-permute-start.9 = (bf16[2,128,128]{2,1,0:T(8,128)(2,1)S(1)}, bf16[2,128,128]{2,1,0:T(8,128)(2,1)S(1)}, u32[]{:S(2)}, u32[]{:S(2)}) collective-permute-start(bf16[2,128,128]{2,1,0:T(8,128)(2,1)S(1)} %collective-permute-done.8.rest_3_), channel_id=1, source_target_pairs={{0,4},{4,0},{8,12},{12,8},{16,20},{20,16},{24,28},{28,24},{1,5},{5... | collective-permute-start | bytes 196616 | tf_op jit(solution)/shard_map/ppermute | solution.py:395
  18.6 4.5 %collective-permute-start.3 = (bf16[2,128,128]{2,1,0:T(8,128)(2,1)S(1)}, bf16[2,128,128]{2,1,0:T(8,128)(2,1)S(1)}, u32[]{:S(2)}, u32[]{:S(2)}) collective-permute-start(bf16[2,128,128]{2,1,0:T(8,128)(2,1)S(1)} %add_convert_fusion.sink.rest_0_), channel_id=1, source_target_pairs={{0,8},{4,12},{8,0},{12,4},{16,24},{20,28},{24,16},{28,20},{1,9},{5... | collective-permute-start | bytes 196616 | tf_op jit(solution)/shard_map/ppermute | solution.py:391
  20.1 4.0 %collective-permute-start.4 = (bf16[2,128,128]{2,1,0:T(8,128)(2,1)S(1)}, bf16[2,128,128]{2,1,0:T(8,128)(2,1)S(1)}, u32[]{:S(2)}, u32[]{:S(2)}) collective-permute-start(bf16[2,128,128]{2,1,0:T(8,128)(2,1)S(1)} %add_convert_fusion.sink.rest_0_), channel_id=1, source_target_pairs={{0,12},{4,8},{8,4},{12,0},{16,28},{20,24},{24,20},{28,16},{1,13},{... | collective-permute-start | bytes 196616 | tf_op jit(solution)/shard_map/ppermute | solution.py:391
  20.4 3.6 %collective-permute-start.6 = (bf16[2,128,128]{2,1,0:T(8,128)(2,1)S(1)}, bf16[2,128,128]{2,1,0:T(8,128)(2,1)S(1)}, u32[]{:S(2)}, u32[]{:S(2)}) collective-permute-start(bf16[2,128,128]{2,1,0:T(8,128)(2,1)S(1)} %collective-permute-done.5.rest_2_), channel_id=1, source_target_pairs={{0,4},{4,0},{8,12},{12,8},{16,20},{20,16},{24,28},{28,24},{1,5},{5... | collective-permute-start | bytes 196616 | tf_op jit(solution)/shard_map/ppermute | solution.py:395
